TPU v7x, 128 devices: a whole 4x4x4 slice. The times are simulated.
128 devices in a mesh: grp: 4 (over z_lo, core), mem: 32 (over z_hi, x, y).
Axes of the slice: x: 4, y: 4, z: 4 (z_hi: 2, z_lo: 2; z = z_hi * 2 + z_lo), core: 2. Of those that a mesh axis runs over, the one named last changes fastest.
Arguments:
- source_pts: float32 [64, 32768], P(None, ('grp', 'mem')), may hold values from -30 to 30
- target_pts: float32 [64, 32768], P(None, ('grp', 'mem')), may hold values from -30 to 30
- source_pot: float32 [32768], P(('grp', 'mem')), may hold values from -8 to 520
- target_pot: float32 [32768], P(('grp', 'mem')), may hold values from -8 to 520
- source_logw: float32 [32768], P(('grp', 'mem')), may hold values from -1 to 4
- target_logw: float32 [32768], P(('grp', 'mem')), may hold values from -1 to 4
Outputs:
- source_new: float32 [32768], P(('grp', 'mem'))
- target_new: float32 [32768], P(('grp', 'mem'))
All inputs are finite; a program needn't handle non-finite values.
Results may differ from a plain program's by a relative error of at most 0.0001.
Values sent between devices are 32-bit elements; how exact they have to be, the bound alone decides.
No kernel may reach another device: no remote copies, remote signals or barrier semaphores. Data moves between devices by JAX's collectives and lax.ppermute only.
A program may use at most 64 MiB of HBM per device.

v0:
```python
import math

import jax
import jax.numpy as jnp
from jax import lax
from jax.sharding import Mesh
from jax.sharding import PartitionSpec as P

GRP_MEM = ("grp_0", "grp_1", "mem_0", "mem_1", "mem_2")
MEM = ("mem_0", "mem_1", "mem_2")
GRP = ("grp_0", "grp_1")


epsilon = 4.0
floor_value = -1e30


def by_axis(x, axes):
    for axis in axes:
        x = lax.pmax(x, axis)
    return x


def by_axis_2(x, axes):
    for axis in axes:
        x = lax.psum(x, axis)
    return x


def in_order(pieces, dim):
    dims = list(pieces.shape[1:])
    dims[dim] *= pieces.shape[0]
    return jnp.moveaxis(pieces, 0, dim).reshape(dims)


def sent_to_all(x, axis):
    copies = jnp.broadcast_to(x, (lax.axis_size(axis), *x.shape))
    return lax.all_to_all(copies, axis, split_axis=0, concat_axis=0, tiled=True)


def collect(x, axis, dim):
    return in_order(sent_to_all(x, axis), dim)


def over_copies(x, axis):
    return sent_to_all(x, axis).max(axis=0)


def cut_along(x, dim, devices):
    dims = x.shape
    pieces = x.reshape(*dims[:dim], devices, dims[dim] // devices, *dims[dim + 1 :])
    return jnp.moveaxis(pieces, dim, 0)


def sum_at_owner(x, axis, dim):
    devices = lax.axis_size(axis)
    pieces = lax.all_to_all(cut_along(x, dim, devices), axis, 0, 0, tiled=True)
    return jnp.sum(pieces, axis=0)


def sweep(carry, points, squares, row_term, moving, offset):
    count = moving.shape[1]
    limit = 128
    width = math.gcd(count, limit)

    def block(index, state):
        row_max, row_sum, col_max, col_sum = state
        begin = index * width
        cols = lax.dynamic_slice_in_dim(moving, begin, width, 1)
        ycols = cols[:-1]
        cvals = cols[-1]
        ysq = 0.5 * jnp.sum(ycols * ycols, 0)
        cross = lax.dot_general(
            points,
            ycols,
            (((0,), (0,)), ((), ())),
            precision=lax.Precision.HIGHEST,
            preferred_element_type=jnp.float32,
        )
        half = (squares[:, None] + ysq[None, :] - cross) / epsilon
        scores = cvals[None, :] - half
        new_row = jnp.maximum(row_max, jnp.max(scores, 1))
        row_sum = row_sum * jnp.exp(row_max - new_row) + jnp.sum(
            jnp.exp(scores - new_row[:, None]), 1
        )
        others = row_term[:, None] - half
        place = offset + begin
        old_max = lax.dynamic_slice_in_dim(col_max, place, width, 0)
        old_sum = lax.dynamic_slice_in_dim(col_sum, place, width, 0)
        new_col = jnp.maximum(old_max, jnp.max(others, 0))
        new_sum = old_sum * jnp.exp(old_max - new_col) + jnp.sum(
            jnp.exp(others - new_col[None, :]), 0
        )
        col_max = lax.dynamic_update_slice_in_dim(col_max, new_col, place, 0)
        col_sum = lax.dynamic_update_slice_in_dim(col_sum, new_sum, place, 0)
        return (new_row, row_sum, col_max, col_sum)

    return lax.fori_loop(0, count // width, block, carry)


def totals(source_logw, target_logw):
    peaks = (by_axis(jnp.max(source_logw), GRP_MEM), by_axis(jnp.max(target_logw), GRP_MEM))
    masses = (
        by_axis_2(jnp.sum(jnp.exp(source_logw - peaks[0])), GRP_MEM),
        by_axis_2(jnp.sum(jnp.exp(target_logw - peaks[1])), GRP_MEM),
    )
    return (peaks[0] + jnp.log(masses[0]), peaks[1] + jnp.log(masses[1]))


def local(source_pts, target_pts, source_pot, target_pot, source_logw, target_logw):
    members = lax.axis_size(MEM)
    rows = source_pts.shape[1]
    outer = rows * members
    row_term = source_logw + source_pot / epsilon
    col_term = target_logw + target_pot / epsilon
    moving = jnp.concatenate([target_pts, col_term[None, :]], 0)
    standing = jnp.concatenate([source_pts, row_term[None, :]], 0)
    row_block = collect(standing, MEM, 1)
    col_block = collect(moving, GRP, 1)
    block_pts = row_block[:-1]
    block_terms = row_block[-1]
    block_sq = 0.5 * jnp.sum(block_pts * block_pts, 0)
    span = col_block.shape[1]
    carry = (
        jnp.full((outer,), floor_value, jnp.float32),
        jnp.zeros((outer,), jnp.float32),
        jnp.full((span,), floor_value, jnp.float32),
        jnp.zeros((span,), jnp.float32),
    )
    row_max, row_sum, col_max, col_sum = sweep(
        carry, block_pts, block_sq, block_terms, col_block, 0
    )
    rpeak = over_copies(row_max, MEM)
    own_rsum = sum_at_owner(row_sum * jnp.exp(row_max - rpeak), MEM, 0)
    own_rmax = lax.dynamic_slice_in_dim(rpeak, lax.axis_index(MEM) * rows, rows, 0)
    row_total = own_rmax + jnp.log(own_rsum)
    cpeak = over_copies(col_max, GRP)
    own_sum = sum_at_owner(col_sum * jnp.exp(col_max - cpeak), GRP, 0)
    own_max = lax.dynamic_slice_in_dim(cpeak, lax.axis_index(GRP) * rows, rows, 0)
    col_total = own_max + jnp.log(own_sum)
    src_norm, tgt_norm = totals(source_logw, target_logw)
    row_hat = -epsilon * (row_total - tgt_norm)
    col_hat = -epsilon * (col_total - src_norm)
    return (0.5 * (source_pot + row_hat), 0.5 * (target_pot + col_hat))


def solution(mesh):
    finer = Mesh(mesh.devices.reshape(2, 2, 2, 4, 4), ("grp_0", "grp_1", "mem_0", "mem_1", "mem_2"))
    return jax.shard_map(
        local,
        mesh=finer,
        in_specs=(
            P(None, GRP_MEM),
            P(None, GRP_MEM),
            P(GRP_MEM),
            P(GRP_MEM),
            P(GRP_MEM),
            P(GRP_MEM),
        ),
        out_specs=(P(GRP_MEM), P(GRP_MEM)),
        check_vma=False,
    )
```

profile of v0, /device:TPU:2, one launch (start us, length us, event | category | flops | bytes accessed | tf_op | source)
XLA Modules:
  0.0 234.5 jit_solution(10569163708637977095)
XLA Ops:
  3.2 5.6 %all-reduce.9 = (f32[]{:T(128)}, f32[]{:T(128)}) all-reduce(f32[]{:T(128)} %reduce_max.63, f32[]{:T(128)} %reduce_max.65), channel_id=1, replica_groups=mesh['grp_0'=2,'grp_1'=2,'mem_0'=2,'mem_1'=4,'mem_2'=4] {'grp_0'}, use_global_device_ids=true, to_apply=%region_11.0 | all-reduce | flops 2 | bytes 16 | tf_op jit(solution)/shard_map/pmax | solution.py:20
  11.8 7.4 %all-reduce.7 = (f32[]{:T(128)}, f32[]{:T(128)}) all-reduce(f32[]{:T(128)} %get-tuple-element.231, f32[]{:T(128)} %get-tuple-element.232), channel_id=1, replica_groups=mesh['grp_0'=2,'grp_1'=2,'mem_0'=2,'mem_1'=4,'mem_2'=4] {'mem_0'}, use_global_device_ids=true, to_apply=%region_13.0 | all-reduce | flops 2 | bytes 16 | tf_op jit(solution)/shard_map/pmax | solution.py:20
  19.2 9.2 %all-reduce.3 = (f32[]{:T(128)}, f32[]{:T(128)}) all-reduce(f32[]{:T(128)} %get-tuple-element.229, f32[]{:T(128)} %get-tuple-element.230), channel_id=1, replica_groups=mesh['grp_0'=2,'grp_1'=2,'mem_0'=2,'mem_1'=4,'mem_2'=4] {'mem_1'}, use_global_device_ids=true, to_apply=%region_14.0 | all-reduce | flops 2 | bytes 16 | tf_op jit(solution)/shard_map/pmax | solution.py:20
  28.5 11.4 %all-reduce.2 = (f32[]{:T(128)}, f32[]{:T(128)}) all-reduce(f32[]{:T(128)} %get-tuple-element.221, f32[]{:T(128)} %get-tuple-element.222), channel_id=1, replica_groups=mesh['grp_0'=2,'grp_1'=2,'mem_0'=2,'mem_1'=4,'mem_2'=4] {'mem_2'}, use_global_device_ids=true, to_apply=%region_15.0 | all-reduce | flops 2 | bytes 16 | tf_op jit(solution)/shard_map/pmax | solution.py:20
  48.3 5.5 %all-to-all-done = f32[4,65,256]{2,1,0:T(8,128)S(1)} async-done(((f32[4,65,256]{2,1,0:T(8,128)}), f32[4,65,256]{2,1,0:T(8,128)S(1)}, u32[]{:S(2)}, u32[]{:S(2)}) %all-to-all-start) | async-done | bytes 266272 | tf_op jit(solution)/shard_map/all_to_all | solution.py:38
  55.4 8.0 %all-to-all-start.1 = ((f32[32,65,256]{2,1,0:T(8,128)}), f32[32,65,256]{2,1,0:T(8,128)S(1)}, u32[]{:S(2)}, u32[]{:S(2)}) async-start(f32[32,65,256]{2,1,0:T(8,128)} %broadcast_in_dim.49), calls=%async_computation.1 | async-start | bytes 4718592 | tf_op jit(solution)/shard_map/all_to_all | solution.py:38
  63.6 30.3 %all-to-all-done.1 = f32[32,65,256]{2,1,0:T(8,128)S(1)} async-done(((f32[32,65,256]{2,1,0:T(8,128)}), f32[32,65,256]{2,1,0:T(8,128)S(1)}, u32[]{:S(2)}, u32[]{:S(2)}) %all-to-all-start.1) | async-done | bytes 2129952 | tf_op jit(solution)/shard_map/all_to_all | solution.py:38
  94.6 53.8 %while.20 = (s32[]{:T(128)}, f32[8192]{0:T(1024)S(1)}, f32[8192]{0:T(1024)S(1)}, f32[1024]{0:T(1024)S(1)}, f32[1024]{0:T(1024)S(1)}, /*index=5*/f32[65,1024]{1,0...) while((s32[]{:T(128)}, f32[8192]{0:T(1024)S(1)}, ...), condition=%wide.region_7.0_spmd.clone, body=%wide.region_1.0_spmd.clone.sunk | while | flops 818995456 | bytes 11102442 | solution.py:98
  101.4 4.5 %subtract_reduce_fusion.3 = (f32[128]{0:T(128)S(1)}, f32[8192]{0:T(1024)S(1)}, f32[8192,128]{0,1:T(8,128)S(1)}) fusion(f32[8192]{0:T(1024)S(1)} %bitcast.36, f32[128]{0:T(128)S(1)} %dynamic-slice_bitcast_fusion.2, f32[64,8192]{1,0:T(8,128)S(1)} %get-tuple-element.350, f32[65,1024]{1,0:T(8,128)S(1)} %get-tuple-element.348, s32[]{:T(128)S(6)} %select_n.21, ...), kind=kOutput, calls=%fused_computation.5.clone.1 | convolution fusion | flops 812638080 | bytes 6424068 | tf_op jit(solution)/shard_map/while/body/eval_jaxpr/dot_general | solution.py:73
  108.1 4.5 %subtract_reduce_fusion.3 = (f32[128]{0:T(128)S(1)}, f32[8192]{0:T(1024)S(1)}, f32[8192,128]{0,1:T(8,128)S(1)}) fusion(f32[8192]{0:T(1024)S(1)} %bitcast.36, f32[128]{0:T(128)S(1)} %dynamic-slice_bitcast_fusion.2, f32[64,8192]{1,0:T(8,128)S(1)} %get-tuple-element.350, f32[65,1024]{1,0:T(8,128)S(1)} %get-tuple-element.348, s32[]{:T(128)S(6)} %select_n.21, ...), kind=kOutput, calls=%fused_computation.5.clone.1 | convolution fusion | flops 812638080 | bytes 6424068 | tf_op jit(solution)/shard_map/while/body/eval_jaxpr/dot_general | solution.py:73
  114.8 4.5 %subtract_reduce_fusion.3 = (f32[128]{0:T(128)S(1)}, f32[8192]{0:T(1024)S(1)}, f32[8192,128]{0,1:T(8,128)S(1)}) fusion(f32[8192]{0:T(1024)S(1)} %bitcast.36, f32[128]{0:T(128)S(1)} %dynamic-slice_bitcast_fusion.2, f32[64,8192]{1,0:T(8,128)S(1)} %get-tuple-element.350, f32[65,1024]{1,0:T(8,128)S(1)} %get-tuple-element.348, s32[]{:T(128)S(6)} %select_n.21, ...), kind=kOutput, calls=%fused_computation.5.clone.1 | convolution fusion | flops 812638080 | bytes 6424068 | tf_op jit(solution)/shard_map/while/body/eval_jaxpr/dot_general | solution.py:73
  121.5 4.5 %subtract_reduce_fusion.3 = (f32[128]{0:T(128)S(1)}, f32[8192]{0:T(1024)S(1)}, f32[8192,128]{0,1:T(8,128)S(1)}) fusion(f32[8192]{0:T(1024)S(1)} %bitcast.36, f32[128]{0:T(128)S(1)} %dynamic-slice_bitcast_fusion.2, f32[64,8192]{1,0:T(8,128)S(1)} %get-tuple-element.350, f32[65,1024]{1,0:T(8,128)S(1)} %get-tuple-element.348, s32[]{:T(128)S(6)} %select_n.21, ...), kind=kOutput, calls=%fused_computation.5.clone.1 | convolution fusion | flops 812638080 | bytes 6424068 | tf_op jit(solution)/shard_map/while/body/eval_jaxpr/dot_general | solution.py:73
  128.2 4.5 %subtract_reduce_fusion.3 = (f32[128]{0:T(128)S(1)}, f32[8192]{0:T(1024)S(1)}, f32[8192,128]{0,1:T(8,128)S(1)}) fusion(f32[8192]{0:T(1024)S(1)} %bitcast.36, f32[128]{0:T(128)S(1)} %dynamic-slice_bitcast_fusion.2, f32[64,8192]{1,0:T(8,128)S(1)} %get-tuple-element.350, f32[65,1024]{1,0:T(8,128)S(1)} %get-tuple-element.348, s32[]{:T(128)S(6)} %select_n.21, ...), kind=kOutput, calls=%fused_computation.5.clone.1 | convolution fusion | flops 812638080 | bytes 6424068 | tf_op jit(solution)/shard_map/while/body/eval_jaxpr/dot_general | solution.py:73
  135.0 4.5 %subtract_reduce_fusion.3 = (f32[128]{0:T(128)S(1)}, f32[8192]{0:T(1024)S(1)}, f32[8192,128]{0,1:T(8,128)S(1)}) fusion(f32[8192]{0:T(1024)S(1)} %bitcast.36, f32[128]{0:T(128)S(1)} %dynamic-slice_bitcast_fusion.2, f32[64,8192]{1,0:T(8,128)S(1)} %get-tuple-element.350, f32[65,1024]{1,0:T(8,128)S(1)} %get-tuple-element.348, s32[]{:T(128)S(6)} %select_n.21, ...), kind=kOutput, calls=%fused_computation.5.clone.1 | convolution fusion | flops 812638080 | bytes 6424068 | tf_op jit(solution)/shard_map/while/body/eval_jaxpr/dot_general | solution.py:73
  141.7 4.5 %subtract_reduce_fusion.3 = (f32[128]{0:T(128)S(1)}, f32[8192]{0:T(1024)S(1)}, f32[8192,128]{0,1:T(8,128)S(1)}) fusion(f32[8192]{0:T(1024)S(1)} %bitcast.36, f32[128]{0:T(128)S(1)} %dynamic-slice_bitcast_fusion.2, f32[64,8192]{1,0:T(8,128)S(1)} %get-tuple-element.350, f32[65,1024]{1,0:T(8,128)S(1)} %get-tuple-element.348, s32[]{:T(128)S(6)} %select_n.21, ...), kind=kOutput, calls=%fused_computation.5.clone.1 | convolution fusion | flops 812638080 | bytes 6424068 | tf_op jit(solution)/shard_map/while/body/eval_jaxpr/dot_general | solution.py:73
  148.4 6.2 %all_to_all.40 = f32[4,1,1024]{2,1,0:T(1,128)S(1)} all-to-all(f32[4,1,1024]{2,1,0:T(1,128)S(1)} %broadcast_in_dim.51), channel_id=1, replica_groups=mesh['grp_0'=2,'grp_1'=2,'mem_0'=2,'mem_1'=4,'mem_2'=4] {'grp_0','grp_1'}, dimensions={0} | all-to-all | bytes 32768 | tf_op jit(solution)/shard_map/all_to_all | solution.py:38
  154.6 6.1 %all_to_all.41 = f32[4,1,256]{2,1,0:T(1,128)S(1)} all-to-all(f32[4,1,256]{2,1,0:T(1,128)S(1)} %bitcast.42), channel_id=1, replica_groups=mesh['grp_0'=2,'grp_1'=2,'mem_0'=2,'mem_1'=4,'mem_2'=4] {'grp_0','grp_1'}, dimensions={0} | all-to-all | bytes 8192 | tf_op jit(solution)/shard_map/all_to_all | solution.py:57
  162.7 8.2 %all-to-all-start.2 = ((f32[32,1,8192]{2,1,0:T(1,128)}), f32[32,1,8192]{2,1,0:T(1,128)S(1)}, u32[]{:S(2)}, u32[]{:S(2)}) async-start(f32[32,1,8192]{2,1,0:T(1,128)} %broadcast_in_dim.50), calls=%async_computation.2 | async-start | bytes 2097152 | tf_op jit(solution)/shard_map/all_to_all | solution.py:38
  170.9 7.9 %all-reduce.6 = (f32[]{:T(128)}, f32[]{:T(128)}) all-reduce(f32[]{:T(128)} %get-tuple-element.245, f32[]{:T(128)} %get-tuple-element.240), channel_id=1, replica_groups=mesh['grp_0'=2,'grp_1'=2,'mem_0'=2,'mem_1'=4,'mem_2'=4] {'grp_0'}, use_global_device_ids=true, to_apply=%region_17.0 | all-reduce | flops 2 | bytes 16 | tf_op jit(solution)/shard_map/psum | solution.py:26
  181.9 7.1 %all-reduce.4 = (f32[]{:T(128)}, f32[]{:T(128)}) all-reduce(f32[]{:T(128)} %get-tuple-element.225, f32[]{:T(128)} %get-tuple-element.226), channel_id=1, replica_groups=mesh['grp_0'=2,'grp_1'=2,'mem_0'=2,'mem_1'=4,'mem_2'=4] {'mem_0'}, use_global_device_ids=true, to_apply=%region_19.0 | all-reduce | flops 2 | bytes 16 | tf_op jit(solution)/shard_map/psum | solution.py:26
  189.0 13.7 %all-reduce.1 = (f32[]{:T(128)}, f32[]{:T(128)}) all-reduce(f32[]{:T(128)} %get-tuple-element.223, f32[]{:T(128)} %get-tuple-element.224), channel_id=1, replica_groups=mesh['grp_0'=2,'grp_1'=2,'mem_0'=2,'mem_1'=4,'mem_2'=4] {'mem_1'}, use_global_device_ids=true, to_apply=%region_20.0 | all-reduce | flops 2 | bytes 16 | tf_op jit(solution)/shard_map/psum | solution.py:26
  202.7 9.7 %all-reduce = (f32[]{:T(128)}, f32[]{:T(128)}) all-reduce(f32[]{:T(128)} %get-tuple-element.217, f32[]{:T(128)} %get-tuple-element.218), channel_id=1, replica_groups=mesh['grp_0'=2,'grp_1'=2,'mem_0'=2,'mem_1'=4,'mem_2'=4] {'mem_2'}, use_global_device_ids=true, to_apply=%region_21.0 | all-reduce | flops 2 | bytes 16 | tf_op jit(solution)/shard_map/psum | solution.py:26
  216.3 8.8 %all-to-all-start.3 = ((f32[32,1,256]{2,1,0:T(1,128)}), f32[32,1,256]{2,1,0:T(1,128)S(1)}, u32[]{:S(2)}, u32[]{:S(2)}) async-start(f32[32,1,256]{2,1,0:T(1,128)} %bitcast.5), calls=%async_computation.3 | async-start | bytes 65536 | tf_op jit(solution)/shard_map/all_to_all | solution.py:57
  225.8 8.0 %all-to-all-done.3 = f32[32,1,256]{2,1,0:T(1,128)S(1)} async-done(((f32[32,1,256]{2,1,0:T(1,128)}), f32[32,1,256]{2,1,0:T(1,128)S(1)}, u32[]{:S(2)}, u32[]{:S(2)}) %all-to-all-start.3) | async-done | bytes 32800 | tf_op jit(solution)/shard_map/all_to_all | solution.py:57
  (126 shorter events, 46.0 us)
Async XLA Ops:
  44.0 9.8 %all-to-all-start = ((f32[4,65,256]{2,1,0:T(8,128)}), f32[4,65,256]{2,1,0:T(8,128)S(1)}, u32[]{:S(2)}, u32[]{:S(2)}) async-start(f32[4,65,256]{2,1,0:T(8,128)} %broadcast_in_dim.47), calls=%async_computation | async-start | bytes 589824 | tf_op jit(solution)/shard_map/all_to_all | solution.py:38
  55.4 38.5 %all-to-all-start.1 = ((f32[32,65,256]{2,1,0:T(8,128)}), f32[32,65,256]{2,1,0:T(8,128)S(1)}, u32[]{:S(2)}, u32[]{:S(2)}) async-start(f32[32,65,256]{2,1,0:T(8,128)} %broadcast_in_dim.49), calls=%async_computation.1 | async-start | bytes 4718592 | tf_op jit(solution)/shard_map/all_to_all | solution.py:38
  148.3 76.8 %copy-start = (f32[256]{0:T(256)S(1)}, f32[256]{0:T(256)}, u32[]{:S(2)}) copy-start(f32[256]{0:T(256)} %param.11) | copy-start | bytes 3076
  148.4 85.5 %copy-start.1 = (f32[256]{0:T(256)S(1)}, f32[256]{0:T(256)}, u32[]{:S(2)}) copy-start(f32[256]{0:T(256)} %param.10) | copy-start | bytes 3076
  162.7 52.3 %all-to-all-start.2 = ((f32[32,1,8192]{2,1,0:T(1,128)}), f32[32,1,8192]{2,1,0:T(1,128)S(1)}, u32[]{:S(2)}, u32[]{:S(2)}) async-start(f32[32,1,8192]{2,1,0:T(1,128)} %broadcast_in_dim.50), calls=%async_computation.2 | async-start | bytes 2097152 | tf_op jit(solution)/shard_map/all_to_all | solution.py:38
  216.3 17.4 %all-to-all-start.3 = ((f32[32,1,256]{2,1,0:T(1,128)}), f32[32,1,256]{2,1,0:T(1,128)S(1)}, u32[]{:S(2)}, u32[]{:S(2)}) async-start(f32[32,1,256]{2,1,0:T(1,128)} %bitcast.5), calls=%async_computation.3 | async-start | bytes 65536 | tf_op jit(solution)/shard_map/all_to_all | solution.py:57
where the time goes:
time: 236 us; the launch traced here: 234 us
  blocking collectives  90.4 us (38%)
  waiting for transfers between devices  43.7 us (19%)
  matrix products  36.3 us (15%)
  starting transfers between devices  28.4 us (12%)
  other arithmetic  27.1 us (11%)
  local copies, waits for them, and re-layouts  4.76 us (2%)
  between operations  3.45 us (1%)
    psum x5, blocking collectives, by_axis_2(): x = lax.psum(x, axis)  41.5 us
    pmax x5, blocking collectives, by_axis(): x = lax.pmax(x, axis)  36.6 us
    dot_general x8, matrix products, block(): lax.dot_general(points, ycols, (((0,), (0,)), ((), ())), precision=lax.Pr...  36.3 us
    all_to_all x3, waiting for transfers between devices, sent_to_all(): return lax.all_to_all(copies, axis, split_axis=0, concat_axis=0, tiled=True)  35.8 us
    all_to_all x3, starting transfers between devices, sent_to_all(): return lax.all_to_all(copies, axis, split_axis=0, concat_axis=0, tiled=True)  19.6 us
    reduce_sum x8, other arithmetic, block(): jnp.sum(jnp.exp(others - new_col[None, :]), 0)  13.5 us
    all_to_all x1, starting transfers between devices, sum_at_owner(): pieces = lax.all_to_all(cut_along(x, dim, devices), axis, 0, 0, tiled=True)  8.79 us
    all_to_all x1, waiting for transfers between devices, sum_at_owner(): pieces = lax.all_to_all(cut_along(x, dim, devices), axis, 0, 0, tiled=True)  7.97 us
  transfers between devices with their start and end apart: 4, of which 3 were waited for; matrix products, arithmetic and copies ran while one was open for 1% of the time, Pallas kernels for 0%

commit v1 on v0

v1 whole, which is shorter than its diff:
```python
import functools

import jax
import jax.numpy as jnp
from jax import lax
from jax.experimental import pallas as pl
from jax.experimental.pallas import tpu as pltpu
from jax.sharding import Mesh
from jax.sharding import PartitionSpec as P

epsilon = 4.0
LOG2E = 1.4426950408889634
LN2 = 0.6931471805599453
FEAT = 64
BLK = 256
LOW = 2.0 ** -90
HIGH = 2.0 ** 120
NORMS = 2.0 ** 15


def split(v):
    head = v.astype(jnp.bfloat16).astype(jnp.float32)
    return head, v - head


def bias_rows(bias, first):
    b1, rest = split(bias)
    b2, b3 = split(rest)
    row = lax.broadcasted_iota(jnp.int32, (16, BLK), 0)
    out = jnp.zeros((16, BLK), jnp.float32)
    for k, piece in enumerate((b1, b2, b3)):
        out = jnp.where(row == k + first, piece, out)
    return jnp.where((row >= 3 - first) & (row < 6 - first), 1.0, out)


def tile_kernel(nrow, ncol, M, *refs):
    row_refs = refs[:-9]
    col_ref, rowp, colp, xt, yk, rowacc, colacc, rmax, rsum = refs[-9:]
    views = []
    for r in row_refs:
        if len(r.shape) == 2:
            views.append(r)
        else:
            views.extend(r.at[k] for k in range(r.shape[0]))

    def terms(ref):
        pts = ref[:FEAT, :]
        sq = 0.5 * jnp.sum(pts * pts, 0, keepdims=True)
        return pts, sq, ref[FEAT:FEAT + 1, :]

    row_sq = jnp.zeros((1, BLK), jnp.float32)
    row_mass = jnp.zeros((1, BLK), jnp.float32)
    for k, ref in enumerate(views):
        pts, sq, term = terms(ref)
        row_sq = jnp.maximum(row_sq, sq)
        row_mass += jnp.exp(ref[FEAT + 1:FEAT + 2, :])
        x1, x2 = split(pts * (LOG2E / epsilon))
        bias = bias_rows((term - sq / epsilon) * LOG2E, 0)
        left = jnp.concatenate([x1, x2], 0)
        right = jnp.concatenate([x1, bias, jnp.zeros((48, BLK), jnp.float32)], 0)
        xt[k * BLK:(k + 1) * BLK, :128] = left.T.astype(jnp.bfloat16)
        xt[k * BLK:(k + 1) * BLK, 128:] = right.T.astype(jnp.bfloat16)

    def prep(j, state):
        col_sq, col_mass = state
        ref = col_ref.at[j]
        pts, sq, term = terms(ref)
        y1, y2 = split(pts)
        bias = bias_rows((term - sq / epsilon) * LOG2E, 3)
        at = pl.ds(pl.multiple_of(j * BLK, BLK), BLK)
        y1 = y1.astype(jnp.bfloat16)
        yk[0:64, at] = y1
        yk[64:128, at] = y1
        yk[128:192, at] = y2.astype(jnp.bfloat16)
        yk[192:208, at] = bias.astype(jnp.bfloat16)
        yk[208:256, at] = jnp.zeros((48, BLK), jnp.bfloat16)
        return jnp.maximum(col_sq, sq), col_mass + jnp.exp(ref[FEAT + 1:FEAT + 2, :])

    zero = jnp.zeros((1, BLK), jnp.float32)
    col_sq, col_mass = lax.fori_loop(0, ncol, prep, (zero, zero), unroll=4)
    rowacc[...] = jnp.zeros_like(rowacc)
    R = nrow * BLK

    def sweep(j, _):
        at = pl.ds(pl.multiple_of(j * BLK, BLK), BLK)
        right = yk[:, at]
        total = jnp.zeros((8, BLK), jnp.float32)
        for i in range(R // M):
            rows = slice(i * M, (i + 1) * M)
            e = jnp.exp2(jnp.dot(xt[rows, :], right, preferred_element_type=jnp.float32))
            rowacc[rows, :] += e[:, :128] + e[:, 128:]
            total += jnp.sum(e.reshape(M // 8, 8, BLK), 0)
        colacc[:, at] = total
        return 0

    lax.fori_loop(0, ncol, sweep, 0)
    rows = lax.dot_general(jnp.ones((8, 128), jnp.float32), rowacc[...], (((1,), (1,)), ((), ())),
                           precision=lax.Precision.HIGHEST, preferred_element_type=jnp.float32)[:1]
    cols = jnp.sum(colacc[...], 0, keepdims=True)
    low = jnp.minimum(jnp.min(rows), jnp.min(cols))
    high = jnp.maximum(jnp.max(rows), jnp.max(cols))
    fast = (low > LOW) & (high < HIGH) & (4.0 * jnp.max(row_sq) * jnp.max(col_sq) < NORMS)
    row_log, col_log = jnp.log(rows), jnp.log(cols)
    col_total = jnp.broadcast_to(jnp.sum(col_mass), (1, BLK))
    row_total = jnp.broadcast_to(jnp.sum(row_mass), (1, BLK))
    for k in range(nrow):
        rowp[k, 0:1, :] = row_log[:, k * BLK:(k + 1) * BLK]
        rowp[k, 1:2, :] = col_total
    for j in range(ncol):
        colp[j, 0:1, :] = col_log[:, j * BLK:(j + 1) * BLK]
        colp[j, 1:2, :] = row_total

    @pl.when(jnp.logical_not(fast))
    def _():
        rowacc[...] = jnp.zeros_like(rowacc)
        rmax[...] = jnp.full(rmax.shape, -1e30, jnp.float32)
        colacc[0:1, :] = jnp.full((1, ncol * BLK), -1e30, jnp.float32)
        colacc[1:2, :] = jnp.zeros((1, ncol * BLK), jnp.float32)
        rsum[...] = jnp.zeros_like(rsum)
        for k, ref in enumerate(views):
            flip = ref[...].T
            pts_t = flip[:, :FEAT]
            sq_t = 0.5 * jnp.sum(pts_t * pts_t, 1, keepdims=True)
            term_t = flip[:, FEAT:FEAT + 1]
            rmax[...] = jnp.full(rmax.shape, -1e30, jnp.float32)
            rsum[...] = jnp.zeros_like(rsum)

            def block(j, _):
                at = pl.ds(pl.multiple_of(j * BLK, BLK), BLK)
                pts, sq, term = terms(col_ref.at[j])
                cross = jnp.dot(pts_t, pts, precision=lax.Precision.HIGHEST,
                                preferred_element_type=jnp.float32)
                half = (sq_t + sq - cross) / epsilon
                scores = term - half
                old = rmax[...]
                new = jnp.maximum(old, jnp.broadcast_to(jnp.max(scores, 1, keepdims=True), old.shape))
                part = jnp.sum(jnp.exp(scores - new[:, :1]), 1, keepdims=True)
                rsum[...] = rsum[...] * jnp.exp(old - new) + part
                rmax[...] = new
                others = term_t - half
                cold = colacc[0:1, at]
                cnew = jnp.maximum(cold, jnp.max(others, 0, keepdims=True))
                colacc[1:2, at] = colacc[1:2, at] * jnp.exp(cold - cnew) + jnp.sum(
                    jnp.exp(others - cnew), 0, keepdims=True)
                colacc[0:1, at] = cnew
                return 0

            lax.fori_loop(0, ncol, block, 0)
            total = (rmax[...] + jnp.log(rsum[...])).T
            rowp[k, 0:1, :] = total[:1] + ref[FEAT:FEAT + 1, :]

        def finish(j, _):
            at = pl.ds(pl.multiple_of(j * BLK, BLK), BLK)
            colp[j, 0:1, :] = colacc[0:1, at] + jnp.log(colacc[1:2, at]) + col_ref[j, FEAT:FEAT + 1, :]
            return 0

        lax.fori_loop(0, ncol, finish, 0)


def tile(row_parts, cols, M=512):
    nrow = sum(1 if p.ndim == 2 else p.shape[0] for p in row_parts)
    ncol = cols.shape[0]
    vm = pl.BlockSpec(memory_space=pltpu.VMEM)
    return pl.pallas_call(
        functools.partial(tile_kernel, nrow, ncol, M),
        out_shape=(jax.ShapeDtypeStruct((nrow, 2, BLK), jnp.float32),
                   jax.ShapeDtypeStruct((ncol, 2, BLK), jnp.float32)),
        in_specs=[vm] * (len(row_parts) + 1),
        out_specs=(vm, vm),
        scratch_shapes=[
            pltpu.VMEM((nrow * BLK, 256), jnp.bfloat16),
            pltpu.VMEM((256, ncol * BLK), jnp.bfloat16),
            pltpu.VMEM((nrow * BLK, 128), jnp.float32),
            pltpu.VMEM((8, ncol * BLK), jnp.float32),
            pltpu.VMEM((BLK, 128), jnp.float32),
            pltpu.VMEM((BLK, 128), jnp.float32),
        ],
        compiler_params=pltpu.CompilerParams(vmem_limit_bytes=48 * 2 ** 20),
        cost_estimate=pl.CostEstimate(flops=2 * 256 * nrow * ncol * BLK * BLK, bytes_accessed=2 * 2 ** 20, transcendentals=nrow * ncol * BLK * BLK),
    )(*row_parts, cols)


GRP_MEM = ("grp_0", "grp_1", "mem_0", "mem_1", "mem_2")
PLANE = ("mem_1", "mem_2")
LINE = ("grp_0", "mem_0")
CORE = "grp_1"


def packed(pts, pot, logw):
    rest = jnp.zeros((6, pts.shape[1]), jnp.float32)
    return jnp.concatenate([pts, (logw + pot / epsilon)[None], logw[None], rest], 0)


def along(step):
    index = [(z % 2) * 2 + z // 2 for z in range(4)]
    return [(index[z], index[(z + step) % 4]) for z in range(4)]


def log_sum(pieces):
    logs, masses = pieces[:, 0], pieces[:, 1]
    peak = jnp.max(logs, 0)
    total = peak + jnp.log(jnp.sum(jnp.exp(logs - peak), 0))
    return total - jnp.log(jnp.sum(masses, 0))


def local(source_pts, target_pts, source_pot, target_pot, source_logw, target_logw):
    line = lax.axis_size(LINE)
    plane = lax.axis_size(PLANE)
    flip = [(0, 1), (1, 0)]
    rows = packed(source_pts, source_pot, source_logw)
    cols = packed(target_pts, target_pot, target_logw)
    mine = [rows]
    for k in range(1, line):
        mine.append(lax.ppermute(rows, LINE, along(-k)))
    others = lax.ppermute(jnp.stack(mine), CORE, flip)
    cols = lax.all_to_all(jnp.broadcast_to(cols, (plane, *cols.shape)), PLANE, 0, 0, tiled=True)
    rowp, colp = tile((*mine, others), cols)
    sibling = lax.ppermute(rowp[line:], CORE, flip)
    colp = lax.all_to_all(colp, PLANE, 0, 0, tiled=True)
    pairs = jnp.stack([rowp[:line], sibling], 1)
    got = [pairs[0]]
    for k in range(1, line):
        got.append(lax.ppermute(pairs[k], LINE, along(k)))
    row_total = log_sum(jnp.concatenate(got, 0)) - (source_logw + source_pot / epsilon)
    col_total = log_sum(colp) - (target_logw + target_pot / epsilon)
    return (0.5 * (source_pot - epsilon * row_total), 0.5 * (target_pot - epsilon * col_total))


def solution(mesh):
    finer = Mesh(mesh.devices.reshape(2, 2, 2, 4, 4), GRP_MEM)
    return jax.shard_map(
        local,
        mesh=finer,
        in_specs=(P(None, GRP_MEM), P(None, GRP_MEM), P(GRP_MEM), P(GRP_MEM), P(GRP_MEM), P(GRP_MEM)),
        out_specs=(P(GRP_MEM), P(GRP_MEM)),
        check_vma=False,
    )
```

time: 236 us -> 142 us (0.60)
  Pallas kernels: 0 us -> 91.8 us
  blocking collectives: 90.4 us -> 0 us
  matrix products: 36.3 us -> 0 us
  waiting for transfers between devices: 43.7 us -> 16.6 us
  other arithmetic: 27.1 us -> 3.71 us
  local copies, waits for them, and re-layouts: 4.76 us -> 1.2 us
  between operations: 3.45 us -> 0.75 us
    pallas_call x0 -> x1, Pallas kernels: none -> 91.8 us  [tile(): pl.pallas_call(functools.partial(tile_kernel, nrow, ncol, M), out_shape=(...]
    psum x5 -> x0, blocking collectives: 41.5 us -> none  [by_axis_2(): x = lax.psum(x, axis)]
    pmax x5 -> x0, blocking collectives: 36.6 us -> none  [by_axis(): x = lax.pmax(x, axis)]
    dot_general x8 -> x0, matrix products: 36.3 us -> none  [block(): lax.dot_general(points, ycols, (((0,), (0,)), ((), ())), precision=lax.Pr...]
    all_to_all x4 -> x2, waiting for transfers between devices: 43.7 us -> 10.5 us  [the longest x1 5.6 us: local(): colp = lax.all_to_all(colp, PLANE, 0, 0, tiled=True)]
    reduce_sum x19 -> x2, other arithmetic: 16.5 us -> 0.05 us  [log_sum(): total = peak + jnp.log(jnp.sum(jnp.exp(logs - peak), 0))]
    all_to_all x4 -> x2, starting transfers between devices: 28.4 us -> 13.7 us  [the longest x1 7.48 us: local(): lax.all_to_all(jnp.broadcast_to(cols, (plane, *cols.shape)), PLANE, 0, 0,...]
    ppermute x0 -> x8, starting transfers between devices: none -> 12.6 us  [the longest x3 6.51 us: local(): mine.append(lax.ppermute(rows, LINE, along(-k)))]
  transfers between devices with their start and end apart: 4 -> 10, of which waited for: 3 -> 7; matrix products, arithmetic and copies ran while one was open for 1% -> 0% of each run, Pallas kernels for 0% -> 0%
where the time goes in v1:
time: 142 us; the launch traced here: 140 us
  Pallas kernels  91.8 us (65%)
  starting transfers between devices  26.3 us (19%)
  waiting for transfers between devices  16.6 us (12%)
  other arithmetic  3.71 us (3%)
    pallas_call x1, Pallas kernels, tile(): pl.pallas_call(functools.partial(tile_kernel, nrow, ncol, M), out_shape=(...  91.8 us
    all_to_all x1, starting transfers between devices, local(): lax.all_to_all(jnp.broadcast_to(cols, (plane, *cols.shape)), PLANE, 0, 0,...  7.48 us
    ppermute x3, starting transfers between devices, local(): mine.append(lax.ppermute(rows, LINE, along(-k)))  6.51 us
    all_to_all x1, starting transfers between devices, local(): colp = lax.all_to_all(colp, PLANE, 0, 0, tiled=True)  6.21 us
    ppermute x3, starting transfers between devices, local(): got.append(lax.ppermute(pairs[k], LINE, along(k)))  5.98 us
    all_to_all x1, waiting for transfers between devices, local(): colp = lax.all_to_all(colp, PLANE, 0, 0, tiled=True)  5.6 us
    all_to_all x1, waiting for transfers between devices, local(): lax.all_to_all(jnp.broadcast_to(cols, (plane, *cols.shape)), PLANE, 0, 0,...  4.89 us
    ppermute x3, waiting for transfers between devices, local(): mine.append(lax.ppermute(rows, LINE, along(-k)))  3.34 us
  transfers between devices with their start and end apart: 10, of which 7 were waited for; matrix products, arithmetic and copies ran while one was open for 0% of the time, Pallas kernels for 0%

profile of v1, /device:TPU:2, one launch (start us, length us, event | category | flops | bytes accessed | tf_op | source)
XLA Modules:
  0.0 140.3 jit_solution(715752878254518281)
XLA Ops:
  0.6 0.1 pad.17.clone
  0.7 0.7 multiply_add_fusion.1
  1.4 0.7 multiply_add_fusion
  2.1 1.0 fusion.11
  3.1 1.1 broadcast_in_dim.21
  4.2 7.5 %all-to-all-start = ((f32[16,72,256]{2,1,0:T(8,128)}), f32[16,72,256]{2,1,0:T(8,128)S(1)}, u32[]{:S(2)}, u32[]{:S(2)}) async-start(f32[16,72,256]{2,1,0:T(8,128)} %broadcast_in_dim.21), calls=%async_computation | async-start | bytes 2359296 | tf_op jit(solution)/shard_map/all_to_all | solution.py:216
  11.7 1.9 %collective-permute-start.2 = (f32[72,256]{1,0:T(8,128)S(1)}, f32[72,256]{1,0:T(8,128)S(1)}, u32[]{:S(2)}, u32[]{:S(2)}) collective-permute-start(f32[72,256]{1,0:T(8,128)S(1)} %get-tuple-element.11.refs_0_), channel_id=1, source_target_pairs={{0,64},{64,16},{16,80},{80,0},{1,65},{65,17},{17,81},{81,1},{2,66}... | collective-permute-start | bytes 221192 | tf_op jit(solution)/shard_map/ppermute | solution.py:214
  13.6 3.6 %collective-permute-start.1 = (f32[72,256]{1,0:T(8,128)S(1)}, f32[72,256]{1,0:T(8,128)S(1)}, u32[]{:S(2)}, u32[]{:S(2)}) collective-permute-start(f32[72,256]{1,0:T(8,128)S(1)} %get-tuple-element.11.refs_0_), channel_id=1, source_target_pairs={{0,16},{64,80},{16,0},{80,64},{1,17},{65,81},{17,1},{81,65},{2,18}... | collective-permute-start | bytes 221192 | tf_op jit(solution)/shard_map/ppermute | solution.py:214
  17.2 1.0 collective-permute-start
  18.2 0.6 collective-permute-done.2.refs_3_
  18.8 1.5 %collective-permute-done.1.refs_2_ = f32[72,256]{1,0:T(8,128)S(1)} collective-permute-done((f32[72,256]{1,0:T(8,128)S(1)}, f32[72,256]{1,0:T(8,128)S(1)}, u32[]{:S(2)}, u32[]{:S(2)}) %collective-permute-start.1) | collective-permute-done | bytes 73760 | tf_op jit(solution)/shard_map/ppermute | solution.py:214
  20.3 1.2 collective-permute-done.refs_1_
  21.6 0.1 collective-permute-start.3
  21.7 1.6 %collective-permute-done.3.refs_4_ = f32[4,72,256]{2,1,0:T(8,128)S(1)} collective-permute-done((f32[4,72,256]{2,1,0:T(8,128)S(1)}, f32[4,72,256]{2,1,0:T(8,128)S(1)}, u32[]{:S(2)}, u32[]{:S(2)}) %collective-permute-start.3) | collective-permute-done | bytes 294944 | tf_op jit(solution)/shard_map/ppermute | solution.py:215
  23.3 4.9 %all-to-all-done.refs_5_ = f32[16,72,256]{2,1,0:T(8,128)S(1)} async-done(((f32[16,72,256]{2,1,0:T(8,128)}), f32[16,72,256]{2,1,0:T(8,128)S(1)}, u32[]{:S(2)}, u32[]{:S(2)}) %all-to-all-start) | async-done | bytes 1179680 | tf_op jit(solution)/shard_map/all_to_all | solution.py:216
  28.2 91.8 %shard_map.77 = (f32[8,2,256]{2,1,0:T(2,128)S(1)}, f32[16,2,256]{2,1,0:T(2,128)}) custom-call(f32[72,256]{1,0:T(8,128)S(1)} %get-tuple-element.11.refs_0_, f32[72,256]{1,0:T(8,128)S(1)} %collective-permute-done.refs_1_, f32[72,256]{1,0:T(8,128)S(1)} %collective-permute-done.1.refs_2_, f32[72,256]{1,0:T(8,128)S(1)} %collective-permute-done.2.refs_3_, ...), custom_call_target="tpu_custom_call" | custom-call | flops 4294967296 | bytes 2097152 | tf_op jit(solution)/shard_map/pallas_call | solution.py:164
  119.9 1.2 collective-permute-done.4
  121.1 1.9 %collective-permute-start.5 = (f32[2,2,256]{2,1,0:T(2,128)S(1)}, f32[2,2,256]{2,1,0:T(2,128)S(1)}, u32[]{:S(2)}, u32[]{:S(2)}) collective-permute-start(f32[2,2,256]{2,1,0:T(2,128)S(1)} %get-tuple-element.15), channel_id=1, source_target_pairs={{0,64},{64,16},{16,80},{80,0},{1,65},{65,17},{17,81},{81,1},{2,66}... | collective-permute-start | bytes 12296 | tf_op jit(solution)/shard_map/ppermute | solution.py:223
  123.1 2.2 %collective-permute-start.7 = (f32[2,2,256]{2,1,0:T(2,128)S(1)}, f32[2,2,256]{2,1,0:T(2,128)S(1)}, u32[]{:S(2)}, u32[]{:S(2)}) collective-permute-start(f32[2,2,256]{2,1,0:T(2,128)S(1)} %get-tuple-element.16), channel_id=1, source_target_pairs={{0,80},{64,0},{16,64},{80,16},{1,81},{65,1},{17,65},{81,17},{2,82}... | collective-permute-start | bytes 12296 | tf_op jit(solution)/shard_map/ppermute | solution.py:223
  125.3 1.8 %collective-permute-start.6 = (f32[2,2,256]{2,1,0:T(2,128)S(1)}, f32[2,2,256]{2,1,0:T(2,128)S(1)}, u32[]{:S(2)}, u32[]{:S(2)}) collective-permute-start(f32[2,2,256]{2,1,0:T(2,128)S(1)} %get-tuple-element.17), channel_id=1, source_target_pairs={{0,16},{64,80},{16,0},{80,64},{1,17},{65,81},{17,1},{81,65},{2,18}... | collective-permute-start | bytes 12296 | tf_op jit(solution)/shard_map/ppermute | solution.py:223
  127.1 6.2 %all-to-all-start.1 = ((f32[16,2,256]{2,1,0:T(2,128)}), f32[16,2,256]{2,1,0:T(2,128)S(1)}, u32[]{:S(2)}, u32[]{:S(2)}) async-start(f32[16,2,256]{2,1,0:T(2,128)} %get-tuple-element.5), calls=%async_computation.1 | async-start | bytes 65536 | tf_op jit(solution)/shard_map/all_to_all | solution.py:219
  133.4 0.6 subtract_multiply_fusion.1
  134.0 5.6 %all-to-all-done.1 = f32[16,2,256]{2,1,0:T(2,128)S(1)} async-done(((f32[16,2,256]{2,1,0:T(2,128)}), f32[16,2,256]{2,1,0:T(2,128)S(1)}, u32[]{:S(2)}, u32[]{:S(2)}) %all-to-all-start.1) | async-done | bytes 32800 | tf_op jit(solution)/shard_map/all_to_all | solution.py:219
  139.7 0.6 subtract_multiply_fusion
  (21 shorter events, 0.2 us)
Async XLA Ops:
  4.2 24.0 %all-to-all-start = ((f32[16,72,256]{2,1,0:T(8,128)}), f32[16,72,256]{2,1,0:T(8,128)S(1)}, u32[]{:S(2)}, u32[]{:S(2)}) async-start(f32[16,72,256]{2,1,0:T(8,128)} %broadcast_in_dim.21), calls=%async_computation | async-start | bytes 2359296 | tf_op jit(solution)/shard_map/all_to_all | solution.py:216
  11.7 7.2 %collective-permute-start.2 = (f32[72,256]{1,0:T(8,128)S(1)}, f32[72,256]{1,0:T(8,128)S(1)}, u32[]{:S(2)}, u32[]{:S(2)}) collective-permute-start(f32[72,256]{1,0:T(8,128)S(1)} %get-tuple-element.11.refs_0_), channel_id=1, source_target_pairs={{0,64},{64,16},{16,80},{80,0},{1,65},{65,17},{17,81},{81,1},{2,66}... | collective-permute-start | bytes 221192 | tf_op jit(solution)/shard_map/ppermute | solution.py:214
  13.6 6.7 %collective-permute-start.1 = (f32[72,256]{1,0:T(8,128)S(1)}, f32[72,256]{1,0:T(8,128)S(1)}, u32[]{:S(2)}, u32[]{:S(2)}) collective-permute-start(f32[72,256]{1,0:T(8,128)S(1)} %get-tuple-element.11.refs_0_), channel_id=1, source_target_pairs={{0,16},{64,80},{16,0},{80,64},{1,17},{65,81},{17,1},{81,65},{2,18}... | collective-permute-start | bytes 221192 | tf_op jit(solution)/shard_map/ppermute | solution.py:214
  17.2 4.4 %collective-permute-start = (f32[72,256]{1,0:T(8,128)S(1)}, f32[72,256]{1,0:T(8,128)S(1)}, u32[]{:S(2)}, u32[]{:S(2)}) collective-permute-start(f32[72,256]{1,0:T(8,128)S(1)} %get-tuple-element.11.refs_0_), channel_id=1, source_target_pairs={{0,80},{64,0},{16,64},{80,16},{1,81},{65,1},{17,65},{81,17},{2,82}... | collective-permute-start | bytes 221192 | tf_op jit(solution)/shard_map/ppermute | solution.py:214
  21.6 111.9 %copy-start = (f32[256]{0:T(256)S(1)}, f32[256]{0:T(256)}, u32[]{:S(2)}) copy-start(f32[256]{0:T(256)} %param.10) | copy-start | bytes 3076
  21.6 111.9 %copy-start.2 = (f32[256]{0:T(256)S(1)}, f32[256]{0:T(256)}, u32[]{:S(2)}) copy-start(f32[256]{0:T(256)} %param.8) | copy-start | bytes 3076
  21.6 118.1 %copy-start.1 = (f32[256]{0:T(256)S(1)}, f32[256]{0:T(256)}, u32[]{:S(2)}) copy-start(f32[256]{0:T(256)} %param.11) | copy-start | bytes 3076
  21.6 118.1 %copy-start.3 = (f32[256]{0:T(256)S(1)}, f32[256]{0:T(256)}, u32[]{:S(2)}) copy-start(f32[256]{0:T(256)} %param.9) | copy-start | bytes 3076
  21.6 1.7 %collective-permute-start.3 = (f32[4,72,256]{2,1,0:T(8,128)S(1)}, f32[4,72,256]{2,1,0:T(8,128)S(1)}, u32[]{:S(2)}, u32[]{:S(2)}) collective-permute-start(f32[4,72,256]{2,1,0:T(8,128)S(1)} %pad_maximum_fusion), channel_id=1, source_target_pairs={{0,32},{32,0},{1,33},{33,1},{2,34},{34,2},{3,35},{35,3},{4,36},{36... | collective-permute-start | bytes 884744 | tf_op jit(solution)/shard_map/ppermute | solution.py:215
  119.9 1.2 collective-permute-start.4
  121.1 12.2 %collective-permute-start.5 = (f32[2,2,256]{2,1,0:T(2,128)S(1)}, f32[2,2,256]{2,1,0:T(2,128)S(1)}, u32[]{:S(2)}, u32[]{:S(2)}) collective-permute-start(f32[2,2,256]{2,1,0:T(2,128)S(1)} %get-tuple-element.15), channel_id=1, source_target_pairs={{0,64},{64,16},{16,80},{80,0},{1,65},{65,17},{17,81},{81,1},{2,66}... | collective-permute-start | bytes 12296 | tf_op jit(solution)/shard_map/ppermute | solution.py:223
  123.1 10.3 %collective-permute-start.7 = (f32[2,2,256]{2,1,0:T(2,128)S(1)}, f32[2,2,256]{2,1,0:T(2,128)S(1)}, u32[]{:S(2)}, u32[]{:S(2)}) collective-permute-start(f32[2,2,256]{2,1,0:T(2,128)S(1)} %get-tuple-element.16), channel_id=1, source_target_pairs={{0,80},{64,0},{16,64},{80,16},{1,81},{65,1},{17,65},{81,17},{2,82}... | collective-permute-start | bytes 12296 | tf_op jit(solution)/shard_map/ppermute | solution.py:223
  125.3 8.0 %collective-permute-start.6 = (f32[2,2,256]{2,1,0:T(2,128)S(1)}, f32[2,2,256]{2,1,0:T(2,128)S(1)}, u32[]{:S(2)}, u32[]{:S(2)}) collective-permute-start(f32[2,2,256]{2,1,0:T(2,128)S(1)} %get-tuple-element.17), channel_id=1, source_target_pairs={{0,16},{64,80},{16,0},{80,64},{1,17},{65,81},{17,1},{81,65},{2,18}... | collective-permute-start | bytes 12296 | tf_op jit(solution)/shard_map/ppermute | solution.py:223
  127.1 12.5 %all-to-all-start.1 = ((f32[16,2,256]{2,1,0:T(2,128)}), f32[16,2,256]{2,1,0:T(2,128)S(1)}, u32[]{:S(2)}, u32[]{:S(2)}) async-start(f32[16,2,256]{2,1,0:T(2,128)} %get-tuple-element.5), calls=%async_computation.1 | async-start | bytes 65536 | tf_op jit(solution)/shard_map/all_to_all | solution.py:219

commit v2 on v1

v2 whole, which is shorter than its diff:
```python
import functools

import jax
import jax.numpy as jnp
from jax import lax
from jax.experimental import pallas as pl
from jax.experimental.pallas import tpu as pltpu
from jax.sharding import Mesh
from jax.sharding import PartitionSpec as P

GRP_MEM = ("grp_0", "grp_1", "mem_0", "mem_1", "mem_2")
GROUP = ("grp_0", "grp_1", "mem_0")
PLANE = ("mem_1", "mem_2")
LINE = ("grp_0", "mem_0")
CORE = "grp_1"
SIDE = 4

epsilon = 4.0
LOG2E = 1.4426950408889634
FEAT = 64
BLK = 256
TALL = 136
floor_value = -1e30
LOW = 2.0**-90
HIGH = 2.0**120
NORMS = 2.0**15

VMEM = pl.BlockSpec(memory_space=pltpu.VMEM)


ANY = pl.BlockSpec(memory_space=pl.ANY)


def call(kernel, out, ins, scratch=(), cost=None, specs=None):
    return pl.pallas_call(
        kernel,
        out_shape=out,
        in_specs=[ANY if specs else VMEM] * ins,
        out_specs=specs or jax.tree.map(lambda _: VMEM, out),
        scratch_shapes=scratch,
        compiler_params=pltpu.CompilerParams(vmem_limit_bytes=40 * 2**20),
        cost_estimate=cost,
    )


def f32(*shape):
    return jax.ShapeDtypeStruct(shape, jnp.float32)


def pack_kernel(spts, tpts, spot, tpot, slogw, tlogw, rows, copies, cols, lines, sems, out_sems):
    loads = []
    for pts, block in ((spts, rows), (tpts, cols)):
        for half in range(2):
            loads.append((pts.at[:, 128 * half : 128 * (half + 1)], block.at[64 * half : 64 * (half + 1), :]))
    for k, ref in enumerate((slogw, spot, tlogw, tpot)):
        loads.append((ref, lines.at[k]))
    loads = [pltpu.make_async_copy(a, b, sems.at[k]) for k, (a, b) in enumerate(loads)]
    for load in loads:
        load.start()
    for k in range(4, 8):
        loads[k].wait()
    for block, logw, pot in ((rows, lines[0], lines[1]), (cols, lines[2], lines[3])):
        tail = (logw + pot / epsilon, logw, pot, jnp.zeros((2, 128), jnp.float32))
        block[128:136, :] = jnp.concatenate(tail, 0)
    loads[2].wait()
    loads[3].wait()
    stores = [pltpu.make_async_copy(cols, copies.at[k], out_sems.at[k]) for k in range(copies.shape[0])]
    for store in stores:
        store.start()
    loads[0].wait()
    loads[1].wait()
    for store in stores:
        store.wait()


def wide(block, line):
    return jnp.concatenate([block[line : line + 1, :], block[line + 1 : line + 2, :]], 1)


def unpacked(block):
    pts = jnp.concatenate([block[0:64, :], block[64:128, :]], 1)
    return pts, 0.5 * jnp.sum(pts * pts, 0, keepdims=True), wide(block, 128)


def split(v):
    head = v.astype(jnp.bfloat16).astype(jnp.float32)
    return head, v - head


def bias_lines(bias, first):
    b1, rest = split(bias)
    b2, b3 = split(rest)
    line = lax.broadcasted_iota(jnp.int32, (16, BLK), 0)
    out = jnp.zeros((16, BLK), jnp.float32)
    for k, piece in enumerate((b1, b2, b3)):
        out = jnp.where(line == k + first, piece, out)
    return jnp.where((line >= 3 - first) & (line < 6 - first), 1.0, out)


def blocks_of(refs):
    out = []
    for ref in refs:
        out.extend([ref] if len(ref.shape) == 2 else [ref.at[k] for k in range(ref.shape[0])])
    return out


def rows_kernel(*refs):
    blocks = blocks_of(refs[:-2])
    xt, stats = refs[-2:]
    most = jnp.zeros((1, BLK), jnp.float32)
    mass = jnp.zeros((1, BLK), jnp.float32)
    for k, block in enumerate(blocks):
        pts, sq, term = unpacked(block)
        most = jnp.maximum(most, sq)
        mass += jnp.exp(wide(block, 130))
        x1, x2 = split(pts * (LOG2E / epsilon))
        bias = bias_lines((term - sq / epsilon) * LOG2E, 0)
        left = jnp.concatenate([x1, x2], 0)
        right = jnp.concatenate([x1, bias, jnp.zeros((48, BLK), jnp.float32)], 0)
        xt[k * BLK : (k + 1) * BLK, :128] = left.T.astype(jnp.bfloat16)
        xt[k * BLK : (k + 1) * BLK, 128:] = right.T.astype(jnp.bfloat16)
    stats[0:1, :] = most
    stats[1:2, :] = mass


def tile_kernel(nrow, ncol, *refs):
    blocks = blocks_of(refs[:5])
    cols, xt, stats, out, own, yk, rowacc, colacc, rmax, rsum, rlog = refs[5:]
    high, core, mem_0 = (lax.axis_index(n) for n in GROUP)
    at_plane = lax.axis_index("mem_1") * SIDE + lax.axis_index("mem_2")
    at_group = (high * 2 + core) * 2 + mem_0
    z = mem_0 * 2 + high

    def owner(k):
        far = lax.rem(z + k % SIDE, SIDE)
        side = core if k < SIDE else 1 - core
        return ((lax.rem(far, 2) * 2 + side) * 2 + far // 2) * (SIDE * SIDE) + at_plane

    def prepare(j, state):
        most, mass = state
        block = cols.at[j]
        pts, sq, term = unpacked(block)
        y1, y2 = split(pts)
        bias = bias_lines((term - sq / epsilon) * LOG2E, 3)
        at = pl.ds(pl.multiple_of(j * BLK, BLK), BLK)
        y1 = y1.astype(jnp.bfloat16)
        yk[0:64, at] = y1
        yk[64:128, at] = y1
        yk[128:192, at] = y2.astype(jnp.bfloat16)
        yk[192:208, at] = bias.astype(jnp.bfloat16)
        yk[208:256, at] = jnp.zeros((48, BLK), jnp.bfloat16)
        return jnp.maximum(most, sq), mass + jnp.exp(wide(block, 130))

    zero = jnp.zeros((1, BLK), jnp.float32)
    most, mass = lax.fori_loop(0, ncol, prepare, (zero, zero), unroll=4)
    rowacc[...] = jnp.zeros_like(rowacc)
    step = 512

    def sweep(j, _):
        at = pl.ds(pl.multiple_of(j * BLK, BLK), BLK)
        right = yk[:, at]
        total = jnp.zeros((8, BLK), jnp.float32)
        for i in range(nrow * BLK // step):
            rows = slice(i * step, (i + 1) * step)
            e = jnp.exp2(jnp.dot(xt[rows, :], right, preferred_element_type=jnp.float32))
            rowacc[rows, :] += e[:, :128] + e[:, 128:]
            total += jnp.sum(e.reshape(step // 8, 8, BLK), 0)
        colacc[:, at] = total
        return 0

    lax.fori_loop(0, ncol, sweep, 0, unroll=8)
    s1, s2 = split(rowacc[...])
    parts = jnp.concatenate([s1, s2], 1).astype(jnp.bfloat16)
    rows = lax.dot_general(
        jnp.ones((16, 256), jnp.bfloat16), parts, (((1,), (1,)), ((), ())), preferred_element_type=jnp.float32
    )[:1]
    sums = jnp.sum(colacc[...], 0, keepdims=True)
    low = jnp.minimum(jnp.min(rows), jnp.min(sums))
    high = jnp.maximum(jnp.max(rows), jnp.max(sums))
    fast = (low > LOW) & (high < HIGH) & (4.0 * jnp.max(stats[0:1, :]) * jnp.max(most) < NORMS)
    rlog[...] = jnp.log(rows)
    colacc[0:1, :] = jnp.log(sums)

    @pl.when(jnp.logical_not(fast))
    def _():
        colacc[0:1, :] = jnp.full((1, ncol * BLK), floor_value, jnp.float32)
        colacc[1:2, :] = jnp.zeros((1, ncol * BLK), jnp.float32)
        for k, block in enumerate(blocks):
            flat, _, term = unpacked(block)
            pts_t = flat.T
            sq_t = 0.5 * jnp.sum(pts_t * pts_t, 1, keepdims=True)
            term_t = jnp.broadcast_to(term, (128, BLK)).T[:, :1]
            rmax[...] = jnp.full(rmax.shape, floor_value, jnp.float32)
            rsum[...] = jnp.zeros_like(rsum)

            def exact(j, _):
                at = pl.ds(pl.multiple_of(j * BLK, BLK), BLK)
                pts, sq, col_term = unpacked(cols.at[j])
                cross = jnp.dot(
                    pts_t, pts, precision=lax.Precision.HIGHEST, preferred_element_type=jnp.float32
                )
                half = (sq_t + sq - cross) / epsilon
                scores = col_term - half
                old = rmax[...]
                new = jnp.maximum(old, jnp.max(scores, 1, keepdims=True))
                part = jnp.sum(jnp.exp(scores - new[:, :1]), 1, keepdims=True)
                rsum[...] = rsum[...] * jnp.exp(old - new) + part
                rmax[...] = new
                others = term_t - half
                old = colacc[0:1, at]
                new = jnp.maximum(old, jnp.max(others, 0, keepdims=True))
                part = jnp.sum(jnp.exp(others - new), 0, keepdims=True)
                colacc[1:2, at] = colacc[1:2, at] * jnp.exp(old - new) + part
                colacc[0:1, at] = new
                return 0

            lax.fori_loop(0, ncol, exact, 0)
            total = (rmax[...] + jnp.log(rsum[...])).T[:1]
            rlog[:, k * BLK : (k + 1) * BLK] = total + term

        def finish(j, _):
            at = pl.ds(pl.multiple_of(j * BLK, BLK), BLK)
            colacc[0:1, at] = colacc[0:1, at] + jnp.log(colacc[1:2, at]) + wide(cols.at[j], 128)
            return 0

        lax.fori_loop(0, ncol, finish, 0)

    row_mass = jnp.broadcast_to(jnp.sum(stats[1:2, :], 1, keepdims=True), (1, BLK))
    col_mass = jnp.broadcast_to(jnp.sum(mass, 1, keepdims=True), (1, BLK))
    for j in range(ncol):
        to = at_group * ncol + j
        out[to, 0:1, :] = colacc[0:1, j * BLK : (j + 1) * BLK]
        out[to, 1:2, :] = row_mass
    mine = pl.ds(pl.multiple_of(at_plane * BLK, BLK), BLK)
    own[0:1, :] = colacc[0:1, mine]
    own[1:2, :] = row_mass
    for k in range(nrow):
        to = owner(k)
        out[to, 0:1, :] = rlog[:, k * BLK : (k + 1) * BLK]
        out[to, 1:2, :] = col_mass
    own[2:3, :] = wide(blocks[0], 128)
    own[3:4, :] = wide(blocks[0], 132)
    own[4:5, :] = wide(cols.at[at_plane], 128)
    own[5:6, :] = wide(cols.at[at_plane], 132)


def finish_kernel(nrow, ncol, got, own, source, target):
    at_plane = lax.axis_index("mem_1") * SIDE + lax.axis_index("mem_2")
    high, core, mem_0 = (lax.axis_index(n) for n in GROUP)
    at_group = (high * 2 + core) * 2 + mem_0

    def total(pieces):
        logs = jnp.concatenate([p[0:1, :] for p in pieces], 0)
        mass = sum(p[1:2, :] for p in pieces)
        peak = jnp.max(logs, 0, keepdims=True)
        return peak + jnp.log(jnp.sum(jnp.exp(logs - peak), 0, keepdims=True)) - jnp.log(mass)

    row_total = total([got[k * ncol + at_plane] for k in range(nrow)]) - own[2:3, :]
    local = own[0:2, :]
    from_cols = []
    for j in range(ncol):
        from_cols.append(jnp.where(at_plane == j, local, got[at_group * ncol + j]))
    col_total = total(from_cols) - own[4:5, :]
    source[...] = (0.5 * (own[3:4, :] - epsilon * row_total)).reshape(BLK)
    target[...] = (0.5 * (own[5:6, :] - epsilon * col_total)).reshape(BLK)


def along(step):
    index = [(z % 2) * 2 + z // 2 for z in range(SIDE)]
    return [(index[z], index[(z + step) % SIDE]) for z in range(SIDE)]


def local(source_pts, target_pts, source_pot, target_pot, source_logw, target_logw):
    nrow, ncol = lax.axis_size(GROUP), lax.axis_size(PLANE)
    lines = [v.reshape(2, 128) for v in (source_pot, target_pot, source_logw, target_logw)]
    rows, copies = call(
        pack_kernel,
        (f32(TALL, 128), f32(ncol, TALL, 128)),
        6,
        scratch=[
            pltpu.VMEM((TALL, 128), jnp.float32),
            pltpu.VMEM((4, 2, 128), jnp.float32),
            pltpu.SemaphoreType.DMA((8,)),
            pltpu.SemaphoreType.DMA((ncol,)),
        ],
        specs=(VMEM, ANY),
    )(source_pts, target_pts, *lines)
    mine = [rows]
    for k in range(1, SIDE):
        mine.append(lax.ppermute(rows, LINE, along(-k)))
    others = lax.ppermute(jnp.stack(mine), CORE, [(0, 1), (1, 0)])
    cols = lax.all_to_all(copies, PLANE, 0, 0, tiled=True)
    size = nrow * ncol * BLK * BLK
    xt, stats = call(
        rows_kernel,
        (jax.ShapeDtypeStruct((nrow * BLK, 256), jnp.bfloat16), f32(2, BLK)),
        5,
        cost=pl.CostEstimate(flops=10**6, bytes_accessed=10**6, transcendentals=0),
    )(*mine, others)
    out, own = call(
        functools.partial(tile_kernel, nrow, ncol),
        (f32(nrow * ncol, 2, BLK), f32(8, BLK)),
        8,
        scratch=[
            pltpu.VMEM((256, ncol * BLK), jnp.bfloat16),
            pltpu.VMEM((nrow * BLK, 128), jnp.float32),
            pltpu.VMEM((8, ncol * BLK), jnp.float32),
            pltpu.VMEM((BLK, 128), jnp.float32),
            pltpu.VMEM((BLK, 128), jnp.float32),
            pltpu.VMEM((1, nrow * BLK), jnp.float32),
        ],
        cost=pl.CostEstimate(flops=512 * size, bytes_accessed=4 * 2**20, transcendentals=size),
    )(*mine, others, cols, xt, stats)
    got = lax.all_to_all(out, GRP_MEM, 0, 0, tiled=True)
    return call(functools.partial(finish_kernel, nrow, ncol), (f32(BLK), f32(BLK)), 2)(got, own)


def solution(mesh):
    finer = Mesh(mesh.devices.reshape(2, 2, 2, 4, 4), GRP_MEM)
    return jax.shard_map(
        local,
        mesh=finer,
        in_specs=(P(None, GRP_MEM), P(None, GRP_MEM), P(GRP_MEM), P(GRP_MEM), P(GRP_MEM), P(GRP_MEM)),
        out_specs=(P(GRP_MEM), P(GRP_MEM)),
        check_vma=False,
    )
```

time: 142 us -> 136 us (0.958)
  blocking collectives: 0 us -> 19.1 us
  starting transfers between devices: 26.3 us -> 14.1 us
  waiting for transfers between devices: 16.6 us -> 8.75 us
  Pallas kernels: 91.8 us -> 87 us
  other arithmetic: 3.71 us -> 0.02 us
  local copies, waits for them, and re-layouts: 1.2 us -> 4.39 us
    all_to_all x0 -> x1, blocking collectives: none -> 19.1 us  [local(): got = lax.all_to_all(out, GRP_MEM, 0, 0, tiled=True)]
    all_to_all x2 -> x1, waiting for transfers between devices: 10.5 us -> 3.9 us  [local(): cols = lax.all_to_all(copies, PLANE, 0, 0, tiled=True)]
    all_to_all x2 -> x1, starting transfers between devices: 13.7 us -> 7.49 us  [local(): cols = lax.all_to_all(copies, PLANE, 0, 0, tiled=True)]
    ppermute x5 -> x1, starting transfers between devices: 6.07 us -> 0.09 us  [local(): others = lax.ppermute(jnp.stack(mine), CORE, [(0, 1), (1, 0)])]
    pallas_call x1 -> x4, Pallas kernels: 91.8 us -> 87 us  [the longest x1 84.7 us: local(): call(functools.partial(tile_kernel, nrow, ncol), (f32(nrow * ncol, 2, BLK...]
    unnamed x8 -> x12, local copies, waits for them, and re-layouts: 0.02 us -> 4.39 us
  transfers between devices with their start and end apart: 10 -> 5, of which waited for: 7 -> 5; matrix products, arithmetic and copies ran while one was open for 0% -> 0% of each run, Pallas kernels for 0% -> 0%
where the time goes in v2:
time: 136 us; the launch traced here: 134 us
  Pallas kernels  87 us (64%)
  blocking collectives  19.1 us (14%)
  starting transfers between devices  14.1 us (10%)
  waiting for transfers between devices  8.75 us (6%)
  local copies, waits for them, and re-layouts  4.39 us (3%)
    pallas_call x1, Pallas kernels, local(): call(functools.partial(tile_kernel, nrow, ncol), (f32(nrow * ncol, 2, BLK...  84.7 us
    all_to_all x1, blocking collectives, local(): got = lax.all_to_all(out, GRP_MEM, 0, 0, tiled=True)  19.1 us
    all_to_all x1, starting transfers between devices, local(): cols = lax.all_to_all(copies, PLANE, 0, 0, tiled=True)  7.49 us
    ppermute x3, starting transfers between devices, local(): mine.append(lax.ppermute(rows, LINE, along(-k)))  6.51 us
    unnamed x12, local copies, waits for them, and re-layouts  4.39 us
    all_to_all x1, waiting for transfers between devices, local(): cols = lax.all_to_all(copies, PLANE, 0, 0, tiled=True)  3.9 us
    ppermute x3, waiting for transfers between devices, local(): mine.append(lax.ppermute(rows, LINE, along(-k)))  3.3 us
  transfers between devices with their start and end apart: 5, of which 5 were waited for; matrix products, arithmetic and copies ran while one was open for 0% of the time, Pallas kernels for 0%

profile of v2, /device:TPU:2, one launch (start us, length us, event | category | flops | bytes accessed | tf_op | source)
XLA Modules:
  0.0 134.0 jit_solution(8378132547149300001)
XLA Ops:
  0.6 0.0 copy-start
  0.6 0.8 copy-done
  1.5 0.0 copy-start.1
  1.5 0.8 copy-done.1
  2.3 0.0 copy-start.2
  2.3 0.7 copy-done.2
  3.0 0.7 copy-done.3
  3.7 0.7 copy-done.4
  4.4 0.7 copy-done.5
  5.0 1.2 shard_map.77
  6.3 7.5 %all-to-all-start = ((f32[16,136,128]{2,1,0:T(8,128)}), f32[16,136,128]{2,1,0:T(8,128)S(1)}, u32[]{:S(2)}, u32[]{:S(2)}) async-start(f32[16,136,128]{2,1,0:T(8,128)} %get-tuple-element.9), calls=%async_computation | async-start | bytes 2228224 | tf_op jit(solution)/shard_map/all_to_all | solution.py:292
  13.8 1.9 %collective-permute-start.2 = (f32[136,128]{1,0:T(8,128)S(1)}, f32[136,128]{1,0:T(8,128)S(1)}, u32[]{:S(2)}, u32[]{:S(2)}) collective-permute-start(f32[136,128]{1,0:T(8,128)S(1)} %get-tuple-element.8.refs_0_), channel_id=1, source_target_pairs={{0,64},{64,16},{16,80},{80,0},{1,65},{65,17},{17,81},{81,1},{2,66}... | collective-permute-start | bytes 208904 | tf_op jit(solution)/shard_map/ppermute | solution.py:290
  15.7 3.6 %collective-permute-start.1 = (f32[136,128]{1,0:T(8,128)S(1)}, f32[136,128]{1,0:T(8,128)S(1)}, u32[]{:S(2)}, u32[]{:S(2)}) collective-permute-start(f32[136,128]{1,0:T(8,128)S(1)} %get-tuple-element.8.refs_0_), channel_id=1, source_target_pairs={{0,16},{64,80},{16,0},{80,64},{1,17},{65,81},{17,1},{81,65},{2,18}... | collective-permute-start | bytes 208904 | tf_op jit(solution)/shard_map/ppermute | solution.py:290
  19.3 1.0 collective-permute-start
  20.3 0.6 collective-permute-done.2.refs_3_
  20.8 1.5 %collective-permute-done.1.refs_2_ = f32[136,128]{1,0:T(8,128)S(1)} collective-permute-done((f32[136,128]{1,0:T(8,128)S(1)}, f32[136,128]{1,0:T(8,128)S(1)}, u32[]{:S(2)}, u32[]{:S(2)}) %collective-permute-start.1) | collective-permute-done | bytes 69664 | tf_op jit(solution)/shard_map/ppermute | solution.py:290
  22.3 1.3 collective-permute-done.refs_1_
  23.6 0.1 collective-permute-start.3
  23.7 1.5 %collective-permute-done.3.refs_4_ = f32[4,136,128]{2,1,0:T(8,128)S(1)} collective-permute-done((f32[4,136,128]{2,1,0:T(8,128)S(1)}, f32[4,136,128]{2,1,0:T(8,128)S(1)}, u32[]{:S(2)}, u32[]{:S(2)}) %collective-permute-start.3) | collective-permute-done | bytes 278560 | tf_op jit(solution)/shard_map/ppermute | solution.py:291
  25.2 0.4 shard_map.78
  25.7 3.9 %all-to-all-done.refs_5_ = f32[16,136,128]{2,1,0:T(8,128)S(1)} async-done(((f32[16,136,128]{2,1,0:T(8,128)}), f32[16,136,128]{2,1,0:T(8,128)S(1)}, u32[]{:S(2)}, u32[]{:S(2)}) %all-to-all-start) | async-done | bytes 1114144 | tf_op jit(solution)/shard_map/all_to_all | solution.py:292
  29.6 84.7 %shard_map.79 = (f32[128,2,256]{2,1,0:T(2,128)S(1)}, f32[8,256]{1,0:T(8,128)S(1)}) custom-call(f32[136,128]{1,0:T(8,128)S(1)} %get-tuple-element.8.refs_0_, f32[136,128]{1,0:T(8,128)S(1)} %collective-permute-done.refs_1_, f32[136,128]{1,0:T(8,128)S(1)} %collective-permute-done.1.refs_2_, f32[136,128]{1,0:T(8,128)S(1)} %collective-permute-done.2.refs_3_, ...), custom_call_target="tpu_custom_call" | custom-call | flops 4294967296 | bytes 4194304 | tf_op jit(solution)/shard_map/pallas_call | solution.py:300
  114.3 19.1 %all_to_all.10.got = f32[128,2,256]{2,1,0:T(2,128)S(1)} all-to-all(f32[128,2,256]{2,1,0:T(2,128)S(1)} %get-tuple-element.12), channel_id=1, replica_groups=mesh['grp_0'=2,'grp_1'=2,'mem_0'=2,'mem_1'=4,'mem_2'=4] {'grp_0','grp_1'..., dimensions={0} | all-to-all | bytes 524288 | tf_op jit(solution)/shard_map/all_to_all | solution.py:314
  133.3 0.6 shard_map.80
  (4 shorter events, 0.0 us)
Async XLA Ops:
  0.6 0.8 copy-start
  1.5 0.8 copy-start.1
  2.3 0.7 copy-start.2
  3.0 0.7 copy-start.3
  3.7 0.7 copy-start.4
  4.4 0.7 copy-start.5
  6.3 23.3 %all-to-all-start = ((f32[16,136,128]{2,1,0:T(8,128)}), f32[16,136,128]{2,1,0:T(8,128)S(1)}, u32[]{:S(2)}, u32[]{:S(2)}) async-start(f32[16,136,128]{2,1,0:T(8,128)} %get-tuple-element.9), calls=%async_computation | async-start | bytes 2228224 | tf_op jit(solution)/shard_map/all_to_all | solution.py:292
  13.8 7.1 %collective-permute-start.2 = (f32[136,128]{1,0:T(8,128)S(1)}, f32[136,128]{1,0:T(8,128)S(1)}, u32[]{:S(2)}, u32[]{:S(2)}) collective-permute-start(f32[136,128]{1,0:T(8,128)S(1)} %get-tuple-element.8.refs_0_), channel_id=1, source_target_pairs={{0,64},{64,16},{16,80},{80,0},{1,65},{65,17},{17,81},{81,1},{2,66}... | collective-permute-start | bytes 208904 | tf_op jit(solution)/shard_map/ppermute | solution.py:290
  15.7 6.6 %collective-permute-start.1 = (f32[136,128]{1,0:T(8,128)S(1)}, f32[136,128]{1,0:T(8,128)S(1)}, u32[]{:S(2)}, u32[]{:S(2)}) collective-permute-start(f32[136,128]{1,0:T(8,128)S(1)} %get-tuple-element.8.refs_0_), channel_id=1, source_target_pairs={{0,16},{64,80},{16,0},{80,64},{1,17},{65,81},{17,1},{81,65},{2,18}... | collective-permute-start | bytes 208904 | tf_op jit(solution)/shard_map/ppermute | solution.py:290
  19.3 4.3 %collective-permute-start = (f32[136,128]{1,0:T(8,128)S(1)}, f32[136,128]{1,0:T(8,128)S(1)}, u32[]{:S(2)}, u32[]{:S(2)}) collective-permute-start(f32[136,128]{1,0:T(8,128)S(1)} %get-tuple-element.8.refs_0_), channel_id=1, source_target_pairs={{0,80},{64,0},{16,64},{80,16},{1,81},{65,1},{17,65},{81,17},{2,82}... | collective-permute-start | bytes 208904 | tf_op jit(solution)/shard_map/ppermute | solution.py:290
  23.6 1.6 %collective-permute-start.3 = (f32[4,136,128]{2,1,0:T(8,128)S(1)}, f32[4,136,128]{2,1,0:T(8,128)S(1)}, u32[]{:S(2)}, u32[]{:S(2)}) collective-permute-start(f32[4,136,128]{2,1,0:T(8,128)S(1)} %pad_maximum_fusion), channel_id=1, source_target_pairs={{0,32},{32,0},{1,33},{33,1},{2,34},{34,2},{3,35},{35,3},{4,36},{36... | collective-permute-start | bytes 835592 | tf_op jit(solution)/shard_map/ppermute | solution.py:291

commit v3 on v2

--- a/solution.py
+++ b/solution.py
@@ -28,14 +28,14 @@
 VMEM = pl.BlockSpec(memory_space=pltpu.VMEM)
 
 
-ANY = pl.BlockSpec(memory_space=pl.ANY)
+HBM = pl.BlockSpec(memory_space=pltpu.HBM)
 
 
 def call(kernel, out, ins, scratch=(), cost=None, specs=None):
     return pl.pallas_call(
         kernel,
         out_shape=out,
-        in_specs=[ANY if specs else VMEM] * ins,
+        in_specs=[HBM if specs else VMEM] * ins,
         out_specs=specs or jax.tree.map(lambda _: VMEM, out),
         scratch_shapes=scratch,
         compiler_params=pltpu.CompilerParams(vmem_limit_bytes=40 * 2**20),
@@ -59,8 +59,8 @@
         load.start()
     for k in range(4, 8):
         loads[k].wait()
-    for block, logw, pot in ((rows, lines[0], lines[1]), (cols, lines[2], lines[3])):
-        tail = (logw + pot / epsilon, logw, pot, jnp.zeros((2, 128), jnp.float32))
+    for block, logw, pot, other in ((rows, lines[0], lines[1], lines[2]), (cols, lines[2], lines[3], lines[0])):
+        tail = (logw + pot / epsilon, logw, pot, other)
         block[128:136, :] = jnp.concatenate(tail, 0)
     loads[2].wait()
     loads[3].wait()
@@ -108,19 +108,16 @@
     blocks = blocks_of(refs[:-2])
     xt, stats = refs[-2:]
     most = jnp.zeros((1, BLK), jnp.float32)
-    mass = jnp.zeros((1, BLK), jnp.float32)
     for k, block in enumerate(blocks):
         pts, sq, term = unpacked(block)
         most = jnp.maximum(most, sq)
-        mass += jnp.exp(wide(block, 130))
         x1, x2 = split(pts * (LOG2E / epsilon))
         bias = bias_lines((term - sq / epsilon) * LOG2E, 0)
         left = jnp.concatenate([x1, x2], 0)
         right = jnp.concatenate([x1, bias, jnp.zeros((48, BLK), jnp.float32)], 0)
         xt[k * BLK : (k + 1) * BLK, :128] = left.T.astype(jnp.bfloat16)
         xt[k * BLK : (k + 1) * BLK, 128:] = right.T.astype(jnp.bfloat16)
-    stats[0:1, :] = most
-    stats[1:2, :] = mass
+    stats[...] = most
 
 
 def tile_kernel(nrow, ncol, *refs):
@@ -137,7 +134,7 @@
         return ((lax.rem(far, 2) * 2 + side) * 2 + far // 2) * (SIDE * SIDE) + at_plane
 
     def prepare(j, state):
-        most, mass = state
+        most, masses = state
         block = cols.at[j]
         pts, sq, term = unpacked(block)
         y1, y2 = split(pts)
@@ -149,10 +146,11 @@
         yk[128:192, at] = y2.astype(jnp.bfloat16)
         yk[192:208, at] = bias.astype(jnp.bfloat16)
         yk[208:256, at] = jnp.zeros((48, BLK), jnp.bfloat16)
-        return jnp.maximum(most, sq), mass + jnp.exp(wide(block, 130))
-
-    zero = jnp.zeros((1, BLK), jnp.float32)
-    most, mass = lax.fori_loop(0, ncol, prepare, (zero, zero), unroll=4)
+        return jnp.maximum(most, sq), masses + jnp.exp(block[128:136, :])
+
+    most, masses = lax.fori_loop(
+        0, ncol, prepare, (jnp.zeros((1, BLK), jnp.float32), jnp.zeros((8, 128), jnp.float32)), unroll=4
+    )
     rowacc[...] = jnp.zeros_like(rowacc)
     step = 512
 
@@ -177,7 +175,7 @@
     sums = jnp.sum(colacc[...], 0, keepdims=True)
     low = jnp.minimum(jnp.min(rows), jnp.min(sums))
     high = jnp.maximum(jnp.max(rows), jnp.max(sums))
-    fast = (low > LOW) & (high < HIGH) & (4.0 * jnp.max(stats[0:1, :]) * jnp.max(most) < NORMS)
+    fast = (low > LOW) & (high < HIGH) & (4.0 * jnp.max(stats[...]) * jnp.max(most) < NORMS)
     rlog[...] = jnp.log(rows)
     colacc[0:1, :] = jnp.log(sums)
 
@@ -225,19 +223,20 @@
 
         lax.fori_loop(0, ncol, finish, 0)
 
-    row_mass = jnp.broadcast_to(jnp.sum(stats[1:2, :], 1, keepdims=True), (1, BLK))
-    col_mass = jnp.broadcast_to(jnp.sum(mass, 1, keepdims=True), (1, BLK))
+    target_mass = jnp.sum(masses[2:4, :], keepdims=True)
+    source_mass = jnp.sum(masses[6:8, :], keepdims=True)
+    mass = jnp.concatenate(
+        [jnp.broadcast_to(source_mass, (1, 128)), jnp.broadcast_to(target_mass, (1, 128))], 1
+    )
+    before = lax.rem(at_plane + ncol - 1, ncol)
+    for k in range(nrow):
+        out[k * ncol + before] = mass
     for j in range(ncol):
-        to = at_group * ncol + j
-        out[to, 0:1, :] = colacc[0:1, j * BLK : (j + 1) * BLK]
-        out[to, 1:2, :] = row_mass
-    mine = pl.ds(pl.multiple_of(at_plane * BLK, BLK), BLK)
-    own[0:1, :] = colacc[0:1, mine]
-    own[1:2, :] = row_mass
+        out[at_group * ncol + j] = colacc[0:1, j * BLK : (j + 1) * BLK]
     for k in range(nrow):
-        to = owner(k)
-        out[to, 0:1, :] = rlog[:, k * BLK : (k + 1) * BLK]
-        out[to, 1:2, :] = col_mass
+        out[owner(k)] = rlog[:, k * BLK : (k + 1) * BLK]
+    own[0:1, :] = colacc[0:1, pl.ds(pl.multiple_of(at_plane * BLK, BLK), BLK)]
+    own[1:2, :] = mass
     own[2:3, :] = wide(blocks[0], 128)
     own[3:4, :] = wide(blocks[0], 132)
     own[4:5, :] = wide(cols.at[at_plane], 128)
@@ -248,21 +247,27 @@
     at_plane = lax.axis_index("mem_1") * SIDE + lax.axis_index("mem_2")
     high, core, mem_0 = (lax.axis_index(n) for n in GROUP)
     at_group = (high * 2 + core) * 2 + mem_0
+    after = lax.rem(at_plane + 1, ncol)
 
     def total(pieces):
-        logs = jnp.concatenate([p[0:1, :] for p in pieces], 0)
-        mass = sum(p[1:2, :] for p in pieces)
+        logs = jnp.concatenate(pieces, 0)
         peak = jnp.max(logs, 0, keepdims=True)
-        return peak + jnp.log(jnp.sum(jnp.exp(logs - peak), 0, keepdims=True)) - jnp.log(mass)
-
-    row_total = total([got[k * ncol + at_plane] for k in range(nrow)]) - own[2:3, :]
-    local = own[0:2, :]
-    from_cols = []
-    for j in range(ncol):
-        from_cols.append(jnp.where(at_plane == j, local, got[at_group * ncol + j]))
-    col_total = total(from_cols) - own[4:5, :]
+        return peak + jnp.log(jnp.sum(jnp.exp(logs - peak), 0, keepdims=True))
+
+    mass = own[1:2, :]
+    for k in range(nrow):
+        mass = mass + jnp.where(at_group == k, 0.0, got[k * ncol + after])
+    mass = jnp.log(mass)
+    row_total = total([got[k * ncol + at_plane] for k in range(nrow)]) - own[2:3, :] - wide_of(mass, 1)
+    pieces = [jnp.where(at_plane == j, own[0:1, :], got[at_group * ncol + j]) for j in range(ncol)]
+    col_total = total(pieces) - own[4:5, :] - wide_of(mass, 0)
     source[...] = (0.5 * (own[3:4, :] - epsilon * row_total)).reshape(BLK)
     target[...] = (0.5 * (own[5:6, :] - epsilon * col_total)).reshape(BLK)
+
+
+def wide_of(mass, half):
+    line = mass[:, 128 * half : 128 * (half + 1)]
+    return jnp.concatenate([line, line], 1)
 
 
 def along(step):
@@ -283,8 +288,8 @@
             pltpu.SemaphoreType.DMA((8,)),
             pltpu.SemaphoreType.DMA((ncol,)),
         ],
-        specs=(VMEM, ANY),
-    )(source_pts, target_pts, *lines)
+        specs=(VMEM, HBM),
+    )(*(pltpu.with_memory_space_constraint(v, pltpu.HBM) for v in (source_pts, target_pts, *lines)))
     mine = [rows]
     for k in range(1, SIDE):
         mine.append(lax.ppermute(rows, LINE, along(-k)))
@@ -293,13 +298,13 @@
     size = nrow * ncol * BLK * BLK
     xt, stats = call(
         rows_kernel,
-        (jax.ShapeDtypeStruct((nrow * BLK, 256), jnp.bfloat16), f32(2, BLK)),
+        (jax.ShapeDtypeStruct((nrow * BLK, 256), jnp.bfloat16), f32(1, BLK)),
         5,
         cost=pl.CostEstimate(flops=10**6, bytes_accessed=10**6, transcendentals=0),
     )(*mine, others)
     out, own = call(
         functools.partial(tile_kernel, nrow, ncol),
-        (f32(nrow * ncol, 2, BLK), f32(8, BLK)),
+        (f32(nrow * ncol, 1, BLK), f32(8, BLK)),
         8,
         scratch=[
             pltpu.VMEM((256, ncol * BLK), jnp.bfloat16),

time: 136 us -> 132 us (0.971)
  local copies, waits for them, and re-layouts: 4.39 us -> 0 us
    unnamed x12 -> x0, local copies, waits for them, and re-layouts: 4.39 us -> none
where the time goes in v3:
time: 132 us; the launch traced here: 129 us
  Pallas kernels  87.8 us (67%)
  blocking collectives  18 us (14%)
  starting transfers between devices  14.1 us (11%)
  waiting for transfers between devices  8.75 us (7%)
    pallas_call x1, Pallas kernels, local(): call(functools.partial(tile_kernel, nrow, ncol), (f32(nrow * ncol, 1, BLK...  84.7 us
    all_to_all x1, blocking collectives, local(): got = lax.all_to_all(out, GRP_MEM, 0, 0, tiled=True)  18 us
    all_to_all x1, starting transfers between devices, local(): cols = lax.all_to_all(copies, PLANE, 0, 0, tiled=True)  7.49 us
    ppermute x3, starting transfers between devices, local(): mine.append(lax.ppermute(rows, LINE, along(-k)))  6.51 us
    all_to_all x1, waiting for transfers between devices, local(): cols = lax.all_to_all(copies, PLANE, 0, 0, tiled=True)  3.9 us
    ppermute x3, waiting for transfers between devices, local(): mine.append(lax.ppermute(rows, LINE, along(-k)))  3.3 us
  transfers between devices with their start and end apart: 5, of which 5 were waited for; matrix products, arithmetic and copies ran while one was open for 0% of the time, Pallas kernels for 0%

profile of v3, /device:TPU:2, one launch (start us, length us, event | category | flops | bytes accessed | tf_op | source)
XLA Modules:
  0.0 129.3 jit_solution(9872250770763638541)
XLA Ops:
  0.6 2.0 %shard_map.77 = (f32[136,128]{1,0:T(8,128)S(1)}, f32[16,136,128]{2,1,0:T(8,128)}) custom-call(f32[64,256]{1,0:T(8,128)} %spts.1, f32[64,256]{1,0:T(8,128)} %tpts.1, f32[2,128]{1,0:T(2,128)} %bitcast.12, f32[2,128]{1,0:T(2,128)} %bitcast.13, f32[2,128]{1,0:T(2,128)} %bitcast.14, f32[2,128]{1,0:T(2,128)} %bitcast.15), custom_call_target="tpu_custom_call" | custom-call | tf_op jit(solution)/shard_map/pallas_call | solution.py:281
  2.7 7.5 %all-to-all-start = ((f32[16,136,128]{2,1,0:T(8,128)}), f32[16,136,128]{2,1,0:T(8,128)S(1)}, u32[]{:S(2)}, u32[]{:S(2)}) async-start(f32[16,136,128]{2,1,0:T(8,128)} %get-tuple-element.9), calls=%async_computation | async-start | bytes 2228224 | tf_op jit(solution)/shard_map/all_to_all | solution.py:297
  10.1 1.9 %collective-permute-start.2 = (f32[136,128]{1,0:T(8,128)S(1)}, f32[136,128]{1,0:T(8,128)S(1)}, u32[]{:S(2)}, u32[]{:S(2)}) collective-permute-start(f32[136,128]{1,0:T(8,128)S(1)} %get-tuple-element.8.refs_0_), channel_id=1, source_target_pairs={{0,64},{64,16},{16,80},{80,0},{1,65},{65,17},{17,81},{81,1},{2,66}... | collective-permute-start | bytes 208904 | tf_op jit(solution)/shard_map/ppermute | solution.py:295
  12.1 3.6 %collective-permute-start.1 = (f32[136,128]{1,0:T(8,128)S(1)}, f32[136,128]{1,0:T(8,128)S(1)}, u32[]{:S(2)}, u32[]{:S(2)}) collective-permute-start(f32[136,128]{1,0:T(8,128)S(1)} %get-tuple-element.8.refs_0_), channel_id=1, source_target_pairs={{0,16},{64,80},{16,0},{80,64},{1,17},{65,81},{17,1},{81,65},{2,18}... | collective-permute-start | bytes 208904 | tf_op jit(solution)/shard_map/ppermute | solution.py:295
  15.6 1.0 collective-permute-start
  16.7 0.6 collective-permute-done.2.refs_3_
  17.2 1.5 %collective-permute-done.1.refs_2_ = f32[136,128]{1,0:T(8,128)S(1)} collective-permute-done((f32[136,128]{1,0:T(8,128)S(1)}, f32[136,128]{1,0:T(8,128)S(1)}, u32[]{:S(2)}, u32[]{:S(2)}) %collective-permute-start.1) | collective-permute-done | bytes 69664 | tf_op jit(solution)/shard_map/ppermute | solution.py:295
  18.7 1.3 collective-permute-done.refs_1_
  20.0 0.1 collective-permute-start.3
  20.1 1.5 %collective-permute-done.3.refs_4_ = f32[4,136,128]{2,1,0:T(8,128)S(1)} collective-permute-done((f32[4,136,128]{2,1,0:T(8,128)S(1)}, f32[4,136,128]{2,1,0:T(8,128)S(1)}, u32[]{:S(2)}, u32[]{:S(2)}) %collective-permute-start.3) | collective-permute-done | bytes 278560 | tf_op jit(solution)/shard_map/ppermute | solution.py:296
  21.6 0.4 shard_map.78
  22.0 3.9 %all-to-all-done.refs_5_ = f32[16,136,128]{2,1,0:T(8,128)S(1)} async-done(((f32[16,136,128]{2,1,0:T(8,128)}), f32[16,136,128]{2,1,0:T(8,128)S(1)}, u32[]{:S(2)}, u32[]{:S(2)}) %all-to-all-start) | async-done | bytes 1114144 | tf_op jit(solution)/shard_map/all_to_all | solution.py:297
  25.9 84.7 %shard_map.79 = (f32[128,1,256]{2,1,0:T(1,128)S(1)}, f32[8,256]{1,0:T(8,128)S(1)}) custom-call(f32[136,128]{1,0:T(8,128)S(1)} %get-tuple-element.8.refs_0_, f32[136,128]{1,0:T(8,128)S(1)} %collective-permute-done.refs_1_, f32[136,128]{1,0:T(8,128)S(1)} %collective-permute-done.1.refs_2_, f32[136,128]{1,0:T(8,128)S(1)} %collective-permute-done.2.refs_3_, ...), custom_call_target="tpu_custom_call" | custom-call | flops 4294967296 | bytes 4194304 | tf_op jit(solution)/shard_map/pallas_call | solution.py:305
  110.7 18.0 %all_to_all.10.got = f32[128,1,256]{2,1,0:T(1,128)S(1)} all-to-all(f32[128,1,256]{2,1,0:T(1,128)S(1)} %get-tuple-element.12), channel_id=1, replica_groups=mesh['grp_0'=2,'grp_1'=2,'mem_0'=2,'mem_1'=4,'mem_2'=4] {'grp_0','grp_1'..., dimensions={0} | all-to-all | bytes 262144 | tf_op jit(solution)/shard_map/all_to_all | solution.py:319
  128.7 0.6 shard_map.80
  (1 shorter events, 0.0 us)
Async XLA Ops:
  2.7 23.3 %all-to-all-start = ((f32[16,136,128]{2,1,0:T(8,128)}), f32[16,136,128]{2,1,0:T(8,128)S(1)}, u32[]{:S(2)}, u32[]{:S(2)}) async-start(f32[16,136,128]{2,1,0:T(8,128)} %get-tuple-element.9), calls=%async_computation | async-start | bytes 2228224 | tf_op jit(solution)/shard_map/all_to_all | solution.py:297
  10.1 7.1 %collective-permute-start.2 = (f32[136,128]{1,0:T(8,128)S(1)}, f32[136,128]{1,0:T(8,128)S(1)}, u32[]{:S(2)}, u32[]{:S(2)}) collective-permute-start(f32[136,128]{1,0:T(8,128)S(1)} %get-tuple-element.8.refs_0_), channel_id=1, source_target_pairs={{0,64},{64,16},{16,80},{80,0},{1,65},{65,17},{17,81},{81,1},{2,66}... | collective-permute-start | bytes 208904 | tf_op jit(solution)/shard_map/ppermute | solution.py:295
  12.1 6.6 %collective-permute-start.1 = (f32[136,128]{1,0:T(8,128)S(1)}, f32[136,128]{1,0:T(8,128)S(1)}, u32[]{:S(2)}, u32[]{:S(2)}) collective-permute-start(f32[136,128]{1,0:T(8,128)S(1)} %get-tuple-element.8.refs_0_), channel_id=1, source_target_pairs={{0,16},{64,80},{16,0},{80,64},{1,17},{65,81},{17,1},{81,65},{2,18}... | collective-permute-start | bytes 208904 | tf_op jit(solution)/shard_map/ppermute | solution.py:295
  15.6 4.3 %collective-permute-start = (f32[136,128]{1,0:T(8,128)S(1)}, f32[136,128]{1,0:T(8,128)S(1)}, u32[]{:S(2)}, u32[]{:S(2)}) collective-permute-start(f32[136,128]{1,0:T(8,128)S(1)} %get-tuple-element.8.refs_0_), channel_id=1, source_target_pairs={{0,80},{64,0},{16,64},{80,16},{1,81},{65,1},{17,65},{81,17},{2,82}... | collective-permute-start | bytes 208904 | tf_op jit(solution)/shard_map/ppermute | solution.py:295
  20.0 1.6 %collective-permute-start.3 = (f32[4,136,128]{2,1,0:T(8,128)S(1)}, f32[4,136,128]{2,1,0:T(8,128)S(1)}, u32[]{:S(2)}, u32[]{:S(2)}) collective-permute-start(f32[4,136,128]{2,1,0:T(8,128)S(1)} %pad_maximum_fusion), channel_id=1, source_target_pairs={{0,32},{32,0},{1,33},{33,1},{2,34},{34,2},{3,35},{35,3},{4,36},{36... | collective-permute-start | bytes 835592 | tf_op jit(solution)/shard_map/ppermute | solution.py:296

commit v4 on v3

--- a/solution.py
+++ b/solution.py
@@ -120,39 +120,36 @@
     stats[...] = most
 
 
-def tile_kernel(nrow, ncol, *refs):
-    blocks = blocks_of(refs[:5])
-    cols, xt, stats, out, own, yk, rowacc, colacc, rmax, rsum, rlog = refs[5:]
-    high, core, mem_0 = (lax.axis_index(n) for n in GROUP)
-    at_plane = lax.axis_index("mem_1") * SIDE + lax.axis_index("mem_2")
-    at_group = (high * 2 + core) * 2 + mem_0
-    z = mem_0 * 2 + high
-
-    def owner(k):
-        far = lax.rem(z + k % SIDE, SIDE)
-        side = core if k < SIDE else 1 - core
-        return ((lax.rem(far, 2) * 2 + side) * 2 + far // 2) * (SIDE * SIDE) + at_plane
-
-    def prepare(j, state):
-        most, masses = state
-        block = cols.at[j]
-        pts, sq, term = unpacked(block)
-        y1, y2 = split(pts)
-        bias = bias_lines((term - sq / epsilon) * LOG2E, 3)
-        at = pl.ds(pl.multiple_of(j * BLK, BLK), BLK)
-        y1 = y1.astype(jnp.bfloat16)
-        yk[0:64, at] = y1
-        yk[64:128, at] = y1
-        yk[128:192, at] = y2.astype(jnp.bfloat16)
-        yk[192:208, at] = bias.astype(jnp.bfloat16)
-        yk[208:256, at] = jnp.zeros((48, BLK), jnp.bfloat16)
-        return jnp.maximum(most, sq), masses + jnp.exp(block[128:136, :])
-
-    most, masses = lax.fori_loop(
-        0, ncol, prepare, (jnp.zeros((1, BLK), jnp.float32), jnp.zeros((8, 128), jnp.float32)), unroll=4
-    )
+def half_kernel(nrow, ncol, last, *refs):
+    blocks = blocks_of(refs[:nrow_refs(last)])
+    refs = refs[nrow_refs(last) :]
+    if last:
+        cols, xt, stats, yk, former, lines, out, own, rowacc, colacc, rmax, rsum, rlog = refs
+        most = former[1:2, 0:BLK]
+    else:
+        cols, xt, stats, yk, former, lines, rowacc, colacc, rmax, rsum, rlog = refs
+
+        def prepare(j, state):
+            most, masses = state
+            block = cols.at[j]
+            pts, sq, term = unpacked(block)
+            y1, y2 = split(pts)
+            bias = bias_lines((term - sq / epsilon) * LOG2E, 3)
+            at = pl.ds(pl.multiple_of(j * BLK, BLK), BLK)
+            y1 = y1.astype(jnp.bfloat16)
+            yk[0:64, at] = y1
+            yk[64:128, at] = y1
+            yk[128:192, at] = y2.astype(jnp.bfloat16)
+            yk[192:208, at] = bias.astype(jnp.bfloat16)
+            yk[208:256, at] = jnp.zeros((48, BLK), jnp.bfloat16)
+            return jnp.maximum(most, sq), masses + jnp.exp(block[128:136, :])
+
+        most, masses = lax.fori_loop(
+            0, ncol, prepare, (jnp.zeros((1, BLK), jnp.float32), jnp.zeros((8, 128), jnp.float32)), unroll=4
+        )
     rowacc[...] = jnp.zeros_like(rowacc)
     step = 512
+    first = 0 if last else nrow * BLK
 
     def sweep(j, _):
         at = pl.ds(pl.multiple_of(j * BLK, BLK), BLK)
@@ -160,13 +157,14 @@
         total = jnp.zeros((8, BLK), jnp.float32)
         for i in range(nrow * BLK // step):
             rows = slice(i * step, (i + 1) * step)
-            e = jnp.exp2(jnp.dot(xt[rows, :], right, preferred_element_type=jnp.float32))
+            held = slice(first + i * step, first + (i + 1) * step)
+            e = jnp.exp2(jnp.dot(xt[held, :], right, preferred_element_type=jnp.float32))
             rowacc[rows, :] += e[:, :128] + e[:, 128:]
             total += jnp.sum(e.reshape(step // 8, 8, BLK), 0)
         colacc[:, at] = total
         return 0
 
-    lax.fori_loop(0, ncol, sweep, 0, unroll=8)
+    lax.fori_loop(0, ncol, sweep, 0, unroll=True)
     s1, s2 = split(rowacc[...])
     parts = jnp.concatenate([s1, s2], 1).astype(jnp.bfloat16)
     rows = lax.dot_general(
@@ -223,46 +221,59 @@
 
         lax.fori_loop(0, ncol, finish, 0)
 
-    target_mass = jnp.sum(masses[2:4, :], keepdims=True)
-    source_mass = jnp.sum(masses[6:8, :], keepdims=True)
-    mass = jnp.concatenate(
-        [jnp.broadcast_to(source_mass, (1, 128)), jnp.broadcast_to(target_mass, (1, 128))], 1
-    )
-    before = lax.rem(at_plane + ncol - 1, ncol)
     for k in range(nrow):
-        out[k * ncol + before] = mass
-    for j in range(ncol):
-        out[at_group * ncol + j] = colacc[0:1, j * BLK : (j + 1) * BLK]
-    for k in range(nrow):
-        out[owner(k)] = rlog[:, k * BLK : (k + 1) * BLK]
-    own[0:1, :] = colacc[0:1, pl.ds(pl.multiple_of(at_plane * BLK, BLK), BLK)]
-    own[1:2, :] = mass
-    own[2:3, :] = wide(blocks[0], 128)
-    own[3:4, :] = wide(blocks[0], 132)
-    own[4:5, :] = wide(cols.at[at_plane], 128)
-    own[5:6, :] = wide(cols.at[at_plane], 132)
-
-
-def finish_kernel(nrow, ncol, got, own, source, target):
-    at_plane = lax.axis_index("mem_1") * SIDE + lax.axis_index("mem_2")
-    high, core, mem_0 = (lax.axis_index(n) for n in GROUP)
-    at_group = (high * 2 + core) * 2 + mem_0
-    after = lax.rem(at_plane + 1, ncol)
-
-    def total(pieces):
-        logs = jnp.concatenate(pieces, 0)
+        lines[k : k + 1, :] = rlog[:, k * BLK : (k + 1) * BLK]
+    if last:
+        lines[4:5, :] = former[1:2, BLK : 2 * BLK]
+        both = both_logs(colacc[0:1, :], former[0:1, :])
+        for j in range(ncol):
+            out[j] = both[:, j * BLK : (j + 1) * BLK]
+        at_plane = lax.axis_index("mem_1") * SIDE + lax.axis_index("mem_2")
+        own[0:1, :] = wide(blocks[0], 128)
+        own[1:2, :] = wide(blocks[0], 132)
+        own[2:3, :] = wide(cols.at[at_plane], 128)
+        own[3:4, :] = wide(cols.at[at_plane], 132)
+    else:
+        target_mass = jnp.sum(masses[2:4, :], keepdims=True)
+        source_mass = jnp.sum(masses[6:8, :], keepdims=True)
+        mass = jnp.concatenate(
+            [jnp.broadcast_to(source_mass, (1, 128)), jnp.broadcast_to(target_mass, (1, 128))], 1
+        )
+        lines[4:5, :] = mass
+        former[0:1, :] = colacc[0:1, :]
+        former[1:2, 0:BLK] = most
+        former[1:2, BLK : 2 * BLK] = mass
+
+
+def nrow_refs(last):
+    return SIDE if last else 1
+
+
+def both_logs(a, b):
+    peak = jnp.maximum(a, b)
+    return peak + jnp.log(jnp.exp(a - peak) + jnp.exp(b - peak))
+
+
+def merge_kernel(mine, other, *outs):
+    logs = both_logs(mine[0:4, :], other[0:4, :])
+    mass = mine[4:5, :] + other[4:5, :]
+    for k, out in enumerate(outs):
+        out[0:1, :] = logs[k : k + 1, :]
+        out[1:2, :] = mass
+
+
+def finish_kernel(got, own, *refs):
+    lines, (source, target) = refs[:-2], refs[-2:]
+
+    def total(logs):
         peak = jnp.max(logs, 0, keepdims=True)
         return peak + jnp.log(jnp.sum(jnp.exp(logs - peak), 0, keepdims=True))
 
-    mass = own[1:2, :]
-    for k in range(nrow):
-        mass = mass + jnp.where(at_group == k, 0.0, got[k * ncol + after])
-    mass = jnp.log(mass)
-    row_total = total([got[k * ncol + at_plane] for k in range(nrow)]) - own[2:3, :] - wide_of(mass, 1)
-    pieces = [jnp.where(at_plane == j, own[0:1, :], got[at_group * ncol + j]) for j in range(ncol)]
-    col_total = total(pieces) - own[4:5, :] - wide_of(mass, 0)
-    source[...] = (0.5 * (own[3:4, :] - epsilon * row_total)).reshape(BLK)
-    target[...] = (0.5 * (own[5:6, :] - epsilon * col_total)).reshape(BLK)
+    mass = jnp.log(sum(line[1:2, :] for line in lines))
+    row_total = total(jnp.concatenate([line[0:1, :] for line in lines], 0)) - own[0:1, :] - wide_of(mass, 1)
+    col_total = total(jnp.concatenate([got[j] for j in range(got.shape[0])], 0)) - own[2:3, :] - wide_of(mass, 0)
+    source[...] = (0.5 * (own[1:2, :] - epsilon * row_total)).reshape(BLK)
+    target[...] = (0.5 * (own[3:4, :] - epsilon * col_total)).reshape(BLK)
 
 
 def wide_of(mass, half):
@@ -295,29 +306,48 @@
         mine.append(lax.ppermute(rows, LINE, along(-k)))
     others = lax.ppermute(jnp.stack(mine), CORE, [(0, 1), (1, 0)])
     cols = lax.all_to_all(copies, PLANE, 0, 0, tiled=True)
+    nrow = nrow // 2
     size = nrow * ncol * BLK * BLK
+    cost = pl.CostEstimate(flops=512 * size, bytes_accessed=4 * 2**20, transcendentals=size)
     xt, stats = call(
         rows_kernel,
-        (jax.ShapeDtypeStruct((nrow * BLK, 256), jnp.bfloat16), f32(1, BLK)),
+        (jax.ShapeDtypeStruct((2 * nrow * BLK, 256), jnp.bfloat16), f32(1, BLK)),
         5,
         cost=pl.CostEstimate(flops=10**6, bytes_accessed=10**6, transcendentals=0),
     )(*mine, others)
-    out, own = call(
-        functools.partial(tile_kernel, nrow, ncol),
-        (f32(nrow * ncol, 1, BLK), f32(8, BLK)),
-        8,
-        scratch=[
-            pltpu.VMEM((256, ncol * BLK), jnp.bfloat16),
-            pltpu.VMEM((nrow * BLK, 128), jnp.float32),
-            pltpu.VMEM((8, ncol * BLK), jnp.float32),
-            pltpu.VMEM((BLK, 128), jnp.float32),
-            pltpu.VMEM((BLK, 128), jnp.float32),
-            pltpu.VMEM((1, nrow * BLK), jnp.float32),
-        ],
-        cost=pl.CostEstimate(flops=512 * size, bytes_accessed=4 * 2**20, transcendentals=size),
-    )(*mine, others, cols, xt, stats)
-    got = lax.all_to_all(out, GRP_MEM, 0, 0, tiled=True)
-    return call(functools.partial(finish_kernel, nrow, ncol), (f32(BLK), f32(BLK)), 2)(got, own)
+    scratch = [
+        pltpu.VMEM((nrow * BLK, 128), jnp.float32),
+        pltpu.VMEM((8, ncol * BLK), jnp.float32),
+        pltpu.VMEM((BLK, 128), jnp.float32),
+        pltpu.VMEM((BLK, 128), jnp.float32),
+        pltpu.VMEM((1, nrow * BLK), jnp.float32),
+    ]
+    yk, former, lines = call(
+        functools.partial(half_kernel, nrow, ncol, False),
+        (jax.ShapeDtypeStruct((256, ncol * BLK), jnp.bfloat16), f32(2, ncol * BLK), f32(8, BLK)),
+        4,
+        scratch=scratch,
+        cost=cost,
+    )(others, cols, xt, stats)
+    crossed = lax.ppermute(lines, CORE, [(0, 1), (1, 0)])
+    lines, out, own = call(
+        functools.partial(half_kernel, nrow, ncol, True),
+        (f32(8, BLK), f32(ncol, 1, BLK), f32(8, BLK)),
+        SIDE + 5,
+        scratch=scratch,
+        cost=cost,
+    )(*mine, cols, xt, stats, yk, former)
+    got = lax.all_to_all(out, PLANE, 0, 0, tiled=True)
+    merged = call(
+        merge_kernel,
+        (f32(8, BLK),) * SIDE,
+        2,
+        cost=pl.CostEstimate(flops=10**5, bytes_accessed=10**5, transcendentals=0),
+    )(lines, crossed)
+    parts = [merged[0]]
+    for k in range(1, SIDE):
+        parts.append(lax.ppermute(merged[k], LINE, along(k)))
+    return call(finish_kernel, (f32(BLK), f32(BLK)), 2 + SIDE)(got, own, *parts)
 
 
 def solution(mesh):

time: 132 us -> 128 us (0.970); the launches traced: 129 us -> 128 us
  blocking collectives: 18 us -> 0 us
  starting transfers between devices: 14.1 us -> 26.9 us
  waiting for transfers between devices: 8.75 us -> 11.4 us
    all_to_all x1 -> x0, blocking collectives: 18 us -> none  [local(): got = lax.all_to_all(out, GRP_MEM, 0, 0, tiled=True)]
    ppermute x0 -> x4, starting transfers between devices: none -> 6.65 us  [the longest x3 6.56 us: local(): parts.append(lax.ppermute(merged[k], LINE, along(k)))]
    all_to_all x0 -> x1, starting transfers between devices: none -> 6.14 us  [local(): got = lax.all_to_all(out, PLANE, 0, 0, tiled=True)]
    ppermute x0 -> x4, waiting for transfers between devices: none -> 2.65 us  [the longest x3 2.65 us: local(): parts.append(lax.ppermute(merged[k], LINE, along(k)))]
    pallas_call x3 -> x5, Pallas kernels: 85.8 us -> 86.9 us  [the longest x1 43 us: local(): call(functools.partial(half_kernel, nrow, ncol, True), (f32(8, BLK), f32(...]
  transfers between devices with their start and end apart: 5 -> 10, of which waited for: 5 -> 7; matrix products, arithmetic and copies ran while one was open for 0% -> 0% of each run, Pallas kernels for 0% -> 34%
where the time goes in v4:
time: 128 us
  Pallas kernels  88.9 us (69%)
  starting transfers between devices  26.9 us (21%)
  waiting for transfers between devices  11.4 us (9%)
    pallas_call x1, Pallas kernels, local(): call(functools.partial(half_kernel, nrow, ncol, True), (f32(8, BLK), f32(...  43 us
    pallas_call x1, Pallas kernels, local(): call(functools.partial(half_kernel, nrow, ncol, False), (jax.ShapeDtypeSt...  42.8 us
    all_to_all x1, starting transfers between devices, local(): cols = lax.all_to_all(copies, PLANE, 0, 0, tiled=True)  7.49 us
    ppermute x3, starting transfers between devices, local(): parts.append(lax.ppermute(merged[k], LINE, along(k)))  6.56 us
    ppermute x3, starting transfers between devices, local(): mine.append(lax.ppermute(rows, LINE, along(-k)))  6.51 us
    all_to_all x1, starting transfers between devices, local(): got = lax.all_to_all(out, PLANE, 0, 0, tiled=True)  6.14 us
    all_to_all x1, waiting for transfers between devices, local(): cols = lax.all_to_all(copies, PLANE, 0, 0, tiled=True)  3.9 us
    ppermute x3, waiting for transfers between devices, local(): mine.append(lax.ppermute(rows, LINE, along(-k)))  3.3 us
  transfers between devices with their start and end apart: 10, of which 7 were waited for; matrix products, arithmetic and copies ran while one was open for 0% of the time, Pallas kernels for 34%

profile of v4, /device:TPU:2, one launch (start us, length us, event | category | flops | bytes accessed | tf_op | source)
XLA Modules:
  0.0 127.9 jit_solution(2055460094064468779)
XLA Ops:
  0.6 2.0 %shard_map.77 = (f32[136,128]{1,0:T(8,128)S(1)}, f32[16,136,128]{2,1,0:T(8,128)}) custom-call(f32[64,256]{1,0:T(8,128)} %spts.1, f32[64,256]{1,0:T(8,128)} %tpts.1, f32[2,128]{1,0:T(2,128)} %bitcast.12, f32[2,128]{1,0:T(2,128)} %bitcast.13, f32[2,128]{1,0:T(2,128)} %bitcast.14, f32[2,128]{1,0:T(2,128)} %bitcast.15), custom_call_target="tpu_custom_call" | custom-call | tf_op jit(solution)/shard_map/pallas_call | solution.py:292
  2.7 7.5 %all-to-all-start = ((f32[16,136,128]{2,1,0:T(8,128)}), f32[16,136,128]{2,1,0:T(8,128)S(1)}, u32[]{:S(2)}, u32[]{:S(2)}) async-start(f32[16,136,128]{2,1,0:T(8,128)} %get-tuple-element.17), calls=%async_computation | async-start | bytes 2228224 | tf_op jit(solution)/shard_map/all_to_all | solution.py:308
  10.2 1.9 %collective-permute-start.2 = (f32[136,128]{1,0:T(8,128)S(1)}, f32[136,128]{1,0:T(8,128)S(1)}, u32[]{:S(2)}, u32[]{:S(2)}) collective-permute-start(f32[136,128]{1,0:T(8,128)S(1)} %get-tuple-element.16.refs_0_), channel_id=1, source_target_pairs={{0,64},{64,16},{16,80},{80,0},{1,65},{65,17},{17,81},{81,1},{2,66}... | collective-permute-start | bytes 208904 | tf_op jit(solution)/shard_map/ppermute | solution.py:306
  12.1 3.6 %collective-permute-start.1 = (f32[136,128]{1,0:T(8,128)S(1)}, f32[136,128]{1,0:T(8,128)S(1)}, u32[]{:S(2)}, u32[]{:S(2)}) collective-permute-start(f32[136,128]{1,0:T(8,128)S(1)} %get-tuple-element.16.refs_0_), channel_id=1, source_target_pairs={{0,16},{64,80},{16,0},{80,64},{1,17},{65,81},{17,1},{81,65},{2,18}... | collective-permute-start | bytes 208904 | tf_op jit(solution)/shard_map/ppermute | solution.py:306
  15.7 1.0 collective-permute-start
  16.7 0.6 collective-permute-done.2.refs_3_
  17.2 1.5 %collective-permute-done.1.refs_2_ = f32[136,128]{1,0:T(8,128)S(1)} collective-permute-done((f32[136,128]{1,0:T(8,128)S(1)}, f32[136,128]{1,0:T(8,128)S(1)}, u32[]{:S(2)}, u32[]{:S(2)}) %collective-permute-start.1) | collective-permute-done | bytes 69664 | tf_op jit(solution)/shard_map/ppermute | solution.py:306
  18.7 1.3 %collective-permute-done.refs_1_ = f32[136,128]{1,0:T(8,128)S(1)} collective-permute-done((f32[136,128]{1,0:T(8,128)S(1)}, f32[136,128]{1,0:T(8,128)S(1)}, u32[]{:S(2)}, u32[]{:S(2)}) %collective-permute-start) | collective-permute-done | bytes 69664 | tf_op jit(solution)/shard_map/ppermute | solution.py:306
  20.0 0.1 collective-permute-start.3
  20.1 1.5 %collective-permute-done.3.refs_4_.refs_0_ = f32[4,136,128]{2,1,0:T(8,128)S(1)} collective-permute-done((f32[4,136,128]{2,1,0:T(8,128)S(1)}, f32[4,136,128]{2,1,0:T(8,128)S(1)}, u32[]{:S(2)}, u32[]{:S(2)}) %collective-permute-start.3) | collective-permute-done | bytes 278560 | tf_op jit(solution)/shard_map/ppermute | solution.py:307
  21.6 0.4 shard_map.78
  22.0 3.9 %all-to-all-done.refs_1_.refs_4_ = f32[16,136,128]{2,1,0:T(8,128)S(1)} async-done(((f32[16,136,128]{2,1,0:T(8,128)}), f32[16,136,128]{2,1,0:T(8,128)S(1)}, u32[]{:S(2)}, u32[]{:S(2)}) %all-to-all-start) | async-done | bytes 1114144 | tf_op jit(solution)/shard_map/all_to_all | solution.py:308
  25.9 42.8 %shard_map.79 = (bf16[256,4096]{1,0:T(8,128)(2,1)S(1)}, f32[2,4096]{1,0:T(2,128)S(1)}, f32[8,256]{1,0:T(8,128)S(1)}) custom-call(f32[4,136,128]{2,1,0:T(8,128)S(1)} %collective-permute-done.3.refs_4_.refs_0_, f32[16,136,128]{2,1,0:T(8,128)S(1)} %all-to-all-done.refs_1_.refs_4_, bf16[2048,256]{1,0:T(8,128)(2,1)S(1)} %get-tuple-element.18.refs_2_.refs_5_, ...), custom_call_target="tpu_custom_call" | custom-call | flops 2147483648 | bytes 4194304 | tf_op jit(solution)/shard_map/pallas_call | solution.py:325
  68.8 0.1 collective-permute-start.4
  68.9 43.0 %shard_map.80 = (f32[8,256]{1,0:T(8,128)S(1)}, f32[16,1,256]{2,1,0:T(1,128)}, f32[8,256]{1,0:T(8,128)S(1)}) custom-call(f32[136,128]{1,0:T(8,128)S(1)} %get-tuple-element.16.refs_0_, f32[136,128]{1,0:T(8,128)S(1)} %collective-permute-done.refs_1_, f32[136,128]{1,0:T(8,128)S(1)} %collective-permute-done.1.refs_2_, ...), custom_call_target="tpu_custom_call" | custom-call | flops 2147483648 | bytes 4194304 | tf_op jit(solution)/shard_map/pallas_call | solution.py:333
  111.9 6.1 %all-to-all-start.1 = ((f32[16,1,256]{2,1,0:T(1,128)}), f32[16,1,256]{2,1,0:T(1,128)S(1)}, u32[]{:S(2)}, u32[]{:S(2)}) async-start(f32[16,1,256]{2,1,0:T(1,128)} %get-tuple-element.22), calls=%async_computation.1 | async-start | bytes 32768 | tf_op jit(solution)/shard_map/all_to_all | solution.py:340
  118.0 0.0 collective-permute-done.4.other
  118.0 2.0 %collective-permute-start.5 = (f32[8,256]{1,0:T(8,128)S(1)}, f32[8,256]{1,0:T(8,128)S(1)}, u32[]{:S(2)}, u32[]{:S(2)}) collective-permute-start(f32[8,256]{1,0:T(8,128)S(1)} %get-tuple-element.27), channel_id=1, source_target_pairs={{0,64},{64,16},{16,80},{80,0},{1,65},{65,17},{17,81},{81,1},{2,66}... | collective-permute-start | bytes 24584 | tf_op jit(solution)/shard_map/ppermute | solution.py:349
  120.0 3.6 %collective-permute-start.6 = (f32[8,256]{1,0:T(8,128)S(1)}, f32[8,256]{1,0:T(8,128)S(1)}, u32[]{:S(2)}, u32[]{:S(2)}) collective-permute-start(f32[8,256]{1,0:T(8,128)S(1)} %get-tuple-element.28), channel_id=1, source_target_pairs={{0,16},{64,80},{16,0},{80,64},{1,17},{65,81},{17,1},{81,65},{2,18}... | collective-permute-start | bytes 24584 | tf_op jit(solution)/shard_map/ppermute | solution.py:349
  123.6 1.0 collective-permute-start.7
  124.6 0.0 all-to-all-done.1.got
  124.6 0.7 collective-permute-done.6.refs_2_
  125.3 1.9 %collective-permute-done.7.refs_3_ = f32[8,256]{1,0:T(8,128)S(1)} collective-permute-done((f32[8,256]{1,0:T(8,128)S(1)}, f32[8,256]{1,0:T(8,128)S(1)}, u32[]{:S(2)}, u32[]{:S(2)}) %collective-permute-start.7) | collective-permute-done | bytes 8224 | tf_op jit(solution)/shard_map/ppermute | solution.py:349
  127.3 0.6 shard_map.82
  (3 shorter events, 0.0 us)
Async XLA Ops:
  2.7 23.3 %all-to-all-start = ((f32[16,136,128]{2,1,0:T(8,128)}), f32[16,136,128]{2,1,0:T(8,128)S(1)}, u32[]{:S(2)}, u32[]{:S(2)}) async-start(f32[16,136,128]{2,1,0:T(8,128)} %get-tuple-element.17), calls=%async_computation | async-start | bytes 2228224 | tf_op jit(solution)/shard_map/all_to_all | solution.py:308
  10.2 7.1 %collective-permute-start.2 = (f32[136,128]{1,0:T(8,128)S(1)}, f32[136,128]{1,0:T(8,128)S(1)}, u32[]{:S(2)}, u32[]{:S(2)}) collective-permute-start(f32[136,128]{1,0:T(8,128)S(1)} %get-tuple-element.16.refs_0_), channel_id=1, source_target_pairs={{0,64},{64,16},{16,80},{80,0},{1,65},{65,17},{17,81},{81,1},{2,66}... | collective-permute-start | bytes 208904 | tf_op jit(solution)/shard_map/ppermute | solution.py:306
  12.1 6.6 %collective-permute-start.1 = (f32[136,128]{1,0:T(8,128)S(1)}, f32[136,128]{1,0:T(8,128)S(1)}, u32[]{:S(2)}, u32[]{:S(2)}) collective-permute-start(f32[136,128]{1,0:T(8,128)S(1)} %get-tuple-element.16.refs_0_), channel_id=1, source_target_pairs={{0,16},{64,80},{16,0},{80,64},{1,17},{65,81},{17,1},{81,65},{2,18}... | collective-permute-start | bytes 208904 | tf_op jit(solution)/shard_map/ppermute | solution.py:306
  15.7 4.3 %collective-permute-start = (f32[136,128]{1,0:T(8,128)S(1)}, f32[136,128]{1,0:T(8,128)S(1)}, u32[]{:S(2)}, u32[]{:S(2)}) collective-permute-start(f32[136,128]{1,0:T(8,128)S(1)} %get-tuple-element.16.refs_0_), channel_id=1, source_target_pairs={{0,80},{64,0},{16,64},{80,16},{1,81},{65,1},{17,65},{81,17},{2,82}... | collective-permute-start | bytes 208904 | tf_op jit(solution)/shard_map/ppermute | solution.py:306
  20.0 1.6 %collective-permute-start.3 = (f32[4,136,128]{2,1,0:T(8,128)S(1)}, f32[4,136,128]{2,1,0:T(8,128)S(1)}, u32[]{:S(2)}, u32[]{:S(2)}) collective-permute-start(f32[4,136,128]{2,1,0:T(8,128)S(1)} %pad_maximum_fusion), channel_id=1, source_target_pairs={{0,32},{32,0},{1,33},{33,1},{2,34},{34,2},{3,35},{35,3},{4,36},{36... | collective-permute-start | bytes 835592 | tf_op jit(solution)/shard_map/ppermute | solution.py:307
  68.8 49.2 %collective-permute-start.4 = (f32[8,256]{1,0:T(8,128)S(1)}, f32[8,256]{1,0:T(8,128)S(1)}, u32[]{:S(2)}, u32[]{:S(2)}) collective-permute-start(f32[8,256]{1,0:T(8,128)S(1)} %get-tuple-element.25), channel_id=1, source_target_pairs={{0,32},{32,0},{1,33},{33,1},{2,34},{34,2},{3,35},{35,3},{4,36},{36... | collective-permute-start | bytes 24584 | tf_op jit(solution)/shard_map/ppermute | solution.py:332
  111.9 12.7 %all-to-all-start.1 = ((f32[16,1,256]{2,1,0:T(1,128)}), f32[16,1,256]{2,1,0:T(1,128)S(1)}, u32[]{:S(2)}, u32[]{:S(2)}) async-start(f32[16,1,256]{2,1,0:T(1,128)} %get-tuple-element.22), calls=%async_computation.1 | async-start | bytes 32768 | tf_op jit(solution)/shard_map/all_to_all | solution.py:340
  118.0 6.6 %collective-permute-start.5 = (f32[8,256]{1,0:T(8,128)S(1)}, f32[8,256]{1,0:T(8,128)S(1)}, u32[]{:S(2)}, u32[]{:S(2)}) collective-permute-start(f32[8,256]{1,0:T(8,128)S(1)} %get-tuple-element.27), channel_id=1, source_target_pairs={{0,64},{64,16},{16,80},{80,0},{1,65},{65,17},{17,81},{81,1},{2,66}... | collective-permute-start | bytes 24584 | tf_op jit(solution)/shard_map/ppermute | solution.py:349
  120.0 5.3 %collective-permute-start.6 = (f32[8,256]{1,0:T(8,128)S(1)}, f32[8,256]{1,0:T(8,128)S(1)}, u32[]{:S(2)}, u32[]{:S(2)}) collective-permute-start(f32[8,256]{1,0:T(8,128)S(1)} %get-tuple-element.28), channel_id=1, source_target_pairs={{0,16},{64,80},{16,0},{80,64},{1,17},{65,81},{17,1},{81,65},{2,18}... | collective-permute-start | bytes 24584 | tf_op jit(solution)/shard_map/ppermute | solution.py:349
  123.6 3.7 %collective-permute-start.7 = (f32[8,256]{1,0:T(8,128)S(1)}, f32[8,256]{1,0:T(8,128)S(1)}, u32[]{:S(2)}, u32[]{:S(2)}) collective-permute-start(f32[8,256]{1,0:T(8,128)S(1)} %get-tuple-element.29), channel_id=1, source_target_pairs={{0,80},{64,0},{16,64},{80,16},{1,81},{65,1},{17,65},{81,17},{2,82}... | collective-permute-start | bytes 24584 | tf_op jit(solution)/shard_map/ppermute | solution.py:349

commit v5 on v4

--- a/solution.py
+++ b/solution.py
@@ -23,7 +23,7 @@
 floor_value = -1e30
 LOW = 2.0**-90
 HIGH = 2.0**120
-NORMS = 2.0**15
+NORM = 90.5
 
 VMEM = pl.BlockSpec(memory_space=pltpu.VMEM)
 
@@ -120,6 +120,10 @@
     stats[...] = most
 
 
+def outside(v, low, high):
+    return jnp.where((v > low) & (v < high), 0.0, 1.0)
+
+
 def half_kernel(nrow, ncol, last, *refs):
     blocks = blocks_of(refs[:nrow_refs(last)])
     refs = refs[nrow_refs(last) :]
@@ -147,33 +151,34 @@
         most, masses = lax.fori_loop(
             0, ncol, prepare, (jnp.zeros((1, BLK), jnp.float32), jnp.zeros((8, 128), jnp.float32)), unroll=4
         )
-    rowacc[...] = jnp.zeros_like(rowacc)
     step = 512
     first = 0 if last else nrow * BLK
 
-    def sweep(j, _):
-        at = pl.ds(pl.multiple_of(j * BLK, BLK), BLK)
+    for j in range(ncol):
+        at = slice(j * BLK, (j + 1) * BLK)
         right = yk[:, at]
         total = jnp.zeros((8, BLK), jnp.float32)
         for i in range(nrow * BLK // step):
             rows = slice(i * step, (i + 1) * step)
             held = slice(first + i * step, first + (i + 1) * step)
             e = jnp.exp2(jnp.dot(xt[held, :], right, preferred_element_type=jnp.float32))
-            rowacc[rows, :] += e[:, :128] + e[:, 128:]
+            part = e[:, :128] + e[:, 128:]
+            rowacc[rows, :] = part if j == 0 else rowacc[rows, :] + part
             total += jnp.sum(e.reshape(step // 8, 8, BLK), 0)
         colacc[:, at] = total
-        return 0
-
-    lax.fori_loop(0, ncol, sweep, 0, unroll=True)
+
     s1, s2 = split(rowacc[...])
     parts = jnp.concatenate([s1, s2], 1).astype(jnp.bfloat16)
     rows = lax.dot_general(
         jnp.ones((16, 256), jnp.bfloat16), parts, (((1,), (1,)), ((), ())), preferred_element_type=jnp.float32
     )[:1]
     sums = jnp.sum(colacc[...], 0, keepdims=True)
-    low = jnp.minimum(jnp.min(rows), jnp.min(sums))
-    high = jnp.maximum(jnp.max(rows), jnp.max(sums))
-    fast = (low > LOW) & (high < HIGH) & (4.0 * jnp.max(stats[...]) * jnp.max(most) < NORMS)
+    ill = outside(stats[...], floor_value, NORM) + outside(most, floor_value, NORM)
+    for j in range(nrow):
+        ill = ill + outside(rows[:, j * BLK : (j + 1) * BLK], LOW, HIGH)
+    for j in range(ncol):
+        ill = ill + outside(sums[:, j * BLK : (j + 1) * BLK], LOW, HIGH)
+    fast = jnp.max(ill) < 0.5
     rlog[...] = jnp.log(rows)
     colacc[0:1, :] = jnp.log(sums)
 
@@ -254,12 +259,22 @@
     return peak + jnp.log(jnp.exp(a - peak) + jnp.exp(b - peak))
 
 
-def merge_kernel(mine, other, *outs):
+def first_kernel(mine, other, keep, send):
+    low = lax.axis_index("grp_0")
     logs = both_logs(mine[0:4, :], other[0:4, :])
-    mass = mine[4:5, :] + other[4:5, :]
-    for k, out in enumerate(outs):
-        out[0:1, :] = logs[k : k + 1, :]
-        out[1:2, :] = mass
+    up, down = logs[1:2, :], logs[3:4, :]
+    send[0:1, :] = jnp.where(low == 0, up, down)
+    send[1:2, :] = logs[2:3, :]
+    keep[0:1, :] = logs[0:1, :]
+    keep[1:2, :] = jnp.where(low == 0, down, up)
+    send[2:3, :] = keep[2:3, :] = mine[4:5, :] + other[4:5, :]
+
+
+def second_kernel(kept, got, keep, send):
+    logs = both_logs(kept[0:2, :], got[0:2, :])
+    keep[0:1, :] = logs[0:1, :]
+    send[0:1, :] = logs[1:2, :]
+    send[1:2, :] = keep[1:2, :] = kept[2:3, :] + got[2:3, :]
 
 
 def finish_kernel(got, own, *refs):
@@ -338,16 +353,12 @@
         cost=cost,
     )(*mine, cols, xt, stats, yk, former)
     got = lax.all_to_all(out, PLANE, 0, 0, tiled=True)
-    merged = call(
-        merge_kernel,
-        (f32(8, BLK),) * SIDE,
-        2,
-        cost=pl.CostEstimate(flops=10**5, bytes_accessed=10**5, transcendentals=0),
-    )(lines, crossed)
-    parts = [merged[0]]
-    for k in range(1, SIDE):
-        parts.append(lax.ppermute(merged[k], LINE, along(k)))
-    return call(finish_kernel, (f32(BLK), f32(BLK)), 2 + SIDE)(got, own, *parts)
+    small = pl.CostEstimate(flops=10**5, bytes_accessed=10**5, transcendentals=0)
+    keep, send = call(first_kernel, (f32(8, BLK), f32(8, BLK)), 2, cost=small)(lines, crossed)
+    send = lax.ppermute(send, LINE[0], [(0, 1), (1, 0)])
+    keep, send = call(second_kernel, (f32(8, BLK), f32(8, BLK)), 2, cost=small)(keep, send)
+    send = lax.ppermute(send, LINE, [(i, SIDE - 1 - i) for i in range(SIDE)])
+    return call(finish_kernel, (f32(BLK), f32(BLK)), 4)(got, own, keep, send)
 
 
 def solution(mesh):

time: 128 us -> 128 us (level)
  starting transfers between devices: 26.9 us -> 24.9 us
    all_to_all x1, waiting for transfers between devices: 0.01 us -> 3.66 us  [local(): got = lax.all_to_all(out, PLANE, 0, 0, tiled=True)]
    ppermute x3 -> x2, waiting for transfers between devices: 2.65 us -> 0.01 us  [the longest x1 0.01 us: local(): send = lax.ppermute(send, LINE[0], [(0, 1), (1, 0)])]
    ppermute x3 -> x2, starting transfers between devices: 6.56 us -> 4.59 us  [the longest x1 2.6 us: local(): send = lax.ppermute(send, LINE, [(i, SIDE - 1 - i) for i in range(SIDE)])]
  transfers between devices with their start and end apart: 10 -> 9, of which waited for: 7 -> 6; matrix products, arithmetic and copies ran while one was open for 0% -> 0% of each run, Pallas kernels for 34% -> 34%
where the time goes in v5:
time: 128 us; the launch traced here: 127 us
  Pallas kernels  89.2 us (70%)
  starting transfers between devices  24.9 us (19%)
  waiting for transfers between devices  12.4 us (10%)
    pallas_call x1, Pallas kernels, local(): call(functools.partial(half_kernel, nrow, ncol, True), (f32(8, BLK), f32(...  43.1 us
    pallas_call x1, Pallas kernels, local(): call(functools.partial(half_kernel, nrow, ncol, False), (jax.ShapeDtypeSt...  42.9 us
    all_to_all x1, starting transfers between devices, local(): cols = lax.all_to_all(copies, PLANE, 0, 0, tiled=True)  7.49 us
    ppermute x3, starting transfers between devices, local(): mine.append(lax.ppermute(rows, LINE, along(-k)))  6.51 us
    all_to_all x1, starting transfers between devices, local(): got = lax.all_to_all(out, PLANE, 0, 0, tiled=True)  6.12 us
    all_to_all x1, waiting for transfers between devices, local(): cols = lax.all_to_all(copies, PLANE, 0, 0, tiled=True)  3.9 us
    all_to_all x1, waiting for transfers between devices, local(): got = lax.all_to_all(out, PLANE, 0, 0, tiled=True)  3.66 us
    ppermute x3, waiting for transfers between devices, local(): mine.append(lax.ppermute(rows, LINE, along(-k)))  3.3 us
  transfers between devices with their start and end apart: 9, of which 6 were waited for; matrix products, arithmetic and copies ran while one was open for 0% of the time, Pallas kernels for 34%

profile of v5, /device:TPU:2, one launch (start us, length us, event | category | flops | bytes accessed | tf_op | source)
XLA Modules:
  0.0 127.2 jit_solution(9545826048880085964)
XLA Ops:
  0.6 2.0 %shard_map.77 = (f32[136,128]{1,0:T(8,128)S(1)}, f32[16,136,128]{2,1,0:T(8,128)}) custom-call(f32[64,256]{1,0:T(8,128)} %spts.1, f32[64,256]{1,0:T(8,128)} %tpts.1, f32[2,128]{1,0:T(2,128)} %bitcast.12, f32[2,128]{1,0:T(2,128)} %bitcast.13, f32[2,128]{1,0:T(2,128)} %bitcast.14, f32[2,128]{1,0:T(2,128)} %bitcast.15), custom_call_target="tpu_custom_call" | custom-call | tf_op jit(solution)/shard_map/pallas_call | solution.py:307
  2.7 7.5 %all-to-all-start = ((f32[16,136,128]{2,1,0:T(8,128)}), f32[16,136,128]{2,1,0:T(8,128)S(1)}, u32[]{:S(2)}, u32[]{:S(2)}) async-start(f32[16,136,128]{2,1,0:T(8,128)} %get-tuple-element.17), calls=%async_computation | async-start | bytes 2228224 | tf_op jit(solution)/shard_map/all_to_all | solution.py:323
  10.2 1.9 %collective-permute-start.2 = (f32[136,128]{1,0:T(8,128)S(1)}, f32[136,128]{1,0:T(8,128)S(1)}, u32[]{:S(2)}, u32[]{:S(2)}) collective-permute-start(f32[136,128]{1,0:T(8,128)S(1)} %get-tuple-element.16.refs_0_), channel_id=1, source_target_pairs={{0,64},{64,16},{16,80},{80,0},{1,65},{65,17},{17,81},{81,1},{2,66}... | collective-permute-start | bytes 208904 | tf_op jit(solution)/shard_map/ppermute | solution.py:321
  12.1 3.6 %collective-permute-start.1 = (f32[136,128]{1,0:T(8,128)S(1)}, f32[136,128]{1,0:T(8,128)S(1)}, u32[]{:S(2)}, u32[]{:S(2)}) collective-permute-start(f32[136,128]{1,0:T(8,128)S(1)} %get-tuple-element.16.refs_0_), channel_id=1, source_target_pairs={{0,16},{64,80},{16,0},{80,64},{1,17},{65,81},{17,1},{81,65},{2,18}... | collective-permute-start | bytes 208904 | tf_op jit(solution)/shard_map/ppermute | solution.py:321
  15.7 1.0 collective-permute-start
  16.7 0.6 collective-permute-done.2.refs_3_
  17.2 1.5 %collective-permute-done.1.refs_2_ = f32[136,128]{1,0:T(8,128)S(1)} collective-permute-done((f32[136,128]{1,0:T(8,128)S(1)}, f32[136,128]{1,0:T(8,128)S(1)}, u32[]{:S(2)}, u32[]{:S(2)}) %collective-permute-start.1) | collective-permute-done | bytes 69664 | tf_op jit(solution)/shard_map/ppermute | solution.py:321
  18.7 1.3 %collective-permute-done.refs_1_ = f32[136,128]{1,0:T(8,128)S(1)} collective-permute-done((f32[136,128]{1,0:T(8,128)S(1)}, f32[136,128]{1,0:T(8,128)S(1)}, u32[]{:S(2)}, u32[]{:S(2)}) %collective-permute-start) | collective-permute-done | bytes 69664 | tf_op jit(solution)/shard_map/ppermute | solution.py:321
  20.0 0.1 collective-permute-start.3
  20.1 1.5 %collective-permute-done.3.refs_4_.refs_0_ = f32[4,136,128]{2,1,0:T(8,128)S(1)} collective-permute-done((f32[4,136,128]{2,1,0:T(8,128)S(1)}, f32[4,136,128]{2,1,0:T(8,128)S(1)}, u32[]{:S(2)}, u32[]{:S(2)}) %collective-permute-start.3) | collective-permute-done | bytes 278560 | tf_op jit(solution)/shard_map/ppermute | solution.py:322
  21.6 0.4 shard_map.78
  22.0 3.9 %all-to-all-done.refs_1_.refs_4_ = f32[16,136,128]{2,1,0:T(8,128)S(1)} async-done(((f32[16,136,128]{2,1,0:T(8,128)}), f32[16,136,128]{2,1,0:T(8,128)S(1)}, u32[]{:S(2)}, u32[]{:S(2)}) %all-to-all-start) | async-done | bytes 1114144 | tf_op jit(solution)/shard_map/all_to_all | solution.py:323
  25.9 42.9 %shard_map.79 = (bf16[256,4096]{1,0:T(8,128)(2,1)S(1)}, f32[2,4096]{1,0:T(2,128)S(1)}, f32[8,256]{1,0:T(8,128)S(1)}) custom-call(f32[4,136,128]{2,1,0:T(8,128)S(1)} %collective-permute-done.3.refs_4_.refs_0_, f32[16,136,128]{2,1,0:T(8,128)S(1)} %all-to-all-done.refs_1_.refs_4_, bf16[2048,256]{1,0:T(8,128)(2,1)S(1)} %get-tuple-element.18.refs_2_.refs_5_, ...), custom_call_target="tpu_custom_call" | custom-call | flops 2147483648 | bytes 4194304 | tf_op jit(solution)/shard_map/pallas_call | solution.py:340
  68.9 0.1 collective-permute-start.4
  69.0 43.1 %shard_map.80 = (f32[8,256]{1,0:T(8,128)S(1)}, f32[16,1,256]{2,1,0:T(1,128)}, f32[8,256]{1,0:T(8,128)S(1)}) custom-call(f32[136,128]{1,0:T(8,128)S(1)} %get-tuple-element.16.refs_0_, f32[136,128]{1,0:T(8,128)S(1)} %collective-permute-done.refs_1_, f32[136,128]{1,0:T(8,128)S(1)} %collective-permute-done.1.refs_2_, ...), custom_call_target="tpu_custom_call" | custom-call | flops 2147483648 | bytes 4194304 | tf_op jit(solution)/shard_map/pallas_call | solution.py:348
  112.1 0.0 collective-permute-done.4.other
  112.1 2.0 %collective-permute-start.5 = (f32[8,256]{1,0:T(8,128)S(1)}, f32[8,256]{1,0:T(8,128)S(1)}, u32[]{:S(2)}, u32[]{:S(2)}) collective-permute-start(f32[8,256]{1,0:T(8,128)S(1)} %get-tuple-element.27), channel_id=1, source_target_pairs={{0,64},{64,0},{1,65},{65,1},{2,66},{66,2},{3,67},{67,3},{4,68},{68... | collective-permute-start | bytes 24584 | tf_op jit(solution)/shard_map/ppermute | solution.py:358
  114.1 6.1 %all-to-all-start.1 = ((f32[16,1,256]{2,1,0:T(1,128)}), f32[16,1,256]{2,1,0:T(1,128)S(1)}, u32[]{:S(2)}, u32[]{:S(2)}) async-start(f32[16,1,256]{2,1,0:T(1,128)} %get-tuple-element.22), calls=%async_computation.1 | async-start | bytes 32768 | tf_op jit(solution)/shard_map/all_to_all | solution.py:355
  120.3 0.0 collective-permute-done.5.got
  120.3 2.6 %collective-permute-start.6 = (f32[8,256]{1,0:T(8,128)S(1)}, f32[8,256]{1,0:T(8,128)S(1)}, u32[]{:S(2)}, u32[]{:S(2)}) collective-permute-start(f32[8,256]{1,0:T(8,128)S(1)} %get-tuple-element.29), channel_id=1, source_target_pairs={{0,80},{16,64},{64,16},{80,0},{1,81},{17,65},{65,17},{81,1},{2,82}... | collective-permute-start | bytes 24584 | tf_op jit(solution)/shard_map/ppermute | solution.py:360
  122.9 3.7 %all-to-all-done.1.got = f32[16,1,256]{2,1,0:T(1,128)S(1)} async-done(((f32[16,1,256]{2,1,0:T(1,128)}), f32[16,1,256]{2,1,0:T(1,128)S(1)}, u32[]{:S(2)}, u32[]{:S(2)}) %all-to-all-start.1) | async-done | bytes 16416 | tf_op jit(solution)/shard_map/all_to_all | solution.py:355
  126.5 0.0 collective-permute-done.6.refs_1_
  126.5 0.6 shard_map.83
  (3 shorter events, 0.1 us)
Async XLA Ops:
  2.7 23.3 %all-to-all-start = ((f32[16,136,128]{2,1,0:T(8,128)}), f32[16,136,128]{2,1,0:T(8,128)S(1)}, u32[]{:S(2)}, u32[]{:S(2)}) async-start(f32[16,136,128]{2,1,0:T(8,128)} %get-tuple-element.17), calls=%async_computation | async-start | bytes 2228224 | tf_op jit(solution)/shard_map/all_to_all | solution.py:323
  10.2 7.1 %collective-permute-start.2 = (f32[136,128]{1,0:T(8,128)S(1)}, f32[136,128]{1,0:T(8,128)S(1)}, u32[]{:S(2)}, u32[]{:S(2)}) collective-permute-start(f32[136,128]{1,0:T(8,128)S(1)} %get-tuple-element.16.refs_0_), channel_id=1, source_target_pairs={{0,64},{64,16},{16,80},{80,0},{1,65},{65,17},{17,81},{81,1},{2,66}... | collective-permute-start | bytes 208904 | tf_op jit(solution)/shard_map/ppermute | solution.py:321
  12.1 6.6 %collective-permute-start.1 = (f32[136,128]{1,0:T(8,128)S(1)}, f32[136,128]{1,0:T(8,128)S(1)}, u32[]{:S(2)}, u32[]{:S(2)}) collective-permute-start(f32[136,128]{1,0:T(8,128)S(1)} %get-tuple-element.16.refs_0_), channel_id=1, source_target_pairs={{0,16},{64,80},{16,0},{80,64},{1,17},{65,81},{17,1},{81,65},{2,18}... | collective-permute-start | bytes 208904 | tf_op jit(solution)/shard_map/ppermute | solution.py:321
  15.7 4.3 %collective-permute-start = (f32[136,128]{1,0:T(8,128)S(1)}, f32[136,128]{1,0:T(8,128)S(1)}, u32[]{:S(2)}, u32[]{:S(2)}) collective-permute-start(f32[136,128]{1,0:T(8,128)S(1)} %get-tuple-element.16.refs_0_), channel_id=1, source_target_pairs={{0,80},{64,0},{16,64},{80,16},{1,81},{65,1},{17,65},{81,17},{2,82}... | collective-permute-start | bytes 208904 | tf_op jit(solution)/shard_map/ppermute | solution.py:321
  20.0 1.6 %collective-permute-start.3 = (f32[4,136,128]{2,1,0:T(8,128)S(1)}, f32[4,136,128]{2,1,0:T(8,128)S(1)}, u32[]{:S(2)}, u32[]{:S(2)}) collective-permute-start(f32[4,136,128]{2,1,0:T(8,128)S(1)} %pad_maximum_fusion), channel_id=1, source_target_pairs={{0,32},{32,0},{1,33},{33,1},{2,34},{34,2},{3,35},{35,3},{4,36},{36... | collective-permute-start | bytes 835592 | tf_op jit(solution)/shard_map/ppermute | solution.py:322
  68.9 43.2 %collective-permute-start.4 = (f32[8,256]{1,0:T(8,128)S(1)}, f32[8,256]{1,0:T(8,128)S(1)}, u32[]{:S(2)}, u32[]{:S(2)}) collective-permute-start(f32[8,256]{1,0:T(8,128)S(1)} %get-tuple-element.25), channel_id=1, source_target_pairs={{0,32},{32,0},{1,33},{33,1},{2,34},{34,2},{3,35},{35,3},{4,36},{36... | collective-permute-start | bytes 24584 | tf_op jit(solution)/shard_map/ppermute | solution.py:347
  112.1 8.1 %collective-permute-start.5 = (f32[8,256]{1,0:T(8,128)S(1)}, f32[8,256]{1,0:T(8,128)S(1)}, u32[]{:S(2)}, u32[]{:S(2)}) collective-permute-start(f32[8,256]{1,0:T(8,128)S(1)} %get-tuple-element.27), channel_id=1, source_target_pairs={{0,64},{64,0},{1,65},{65,1},{2,66},{66,2},{3,67},{67,3},{4,68},{68... | collective-permute-start | bytes 24584 | tf_op jit(solution)/shard_map/ppermute | solution.py:358
  114.1 12.4 %all-to-all-start.1 = ((f32[16,1,256]{2,1,0:T(1,128)}), f32[16,1,256]{2,1,0:T(1,128)S(1)}, u32[]{:S(2)}, u32[]{:S(2)}) async-start(f32[16,1,256]{2,1,0:T(1,128)} %get-tuple-element.22), calls=%async_computation.1 | async-start | bytes 32768 | tf_op jit(solution)/shard_map/all_to_all | solution.py:355
  120.3 6.3 %collective-permute-start.6 = (f32[8,256]{1,0:T(8,128)S(1)}, f32[8,256]{1,0:T(8,128)S(1)}, u32[]{:S(2)}, u32[]{:S(2)}) collective-permute-start(f32[8,256]{1,0:T(8,128)S(1)} %get-tuple-element.29), channel_id=1, source_target_pairs={{0,80},{16,64},{64,16},{80,0},{1,81},{17,65},{65,17},{81,1},{2,82}... | collective-permute-start | bytes 24584 | tf_op jit(solution)/shard_map/ppermute | solution.py:360

commit v6 on v5

--- a/solution.py
+++ b/solution.py
@@ -356,7 +356,7 @@
     small = pl.CostEstimate(flops=10**5, bytes_accessed=10**5, transcendentals=0)
     keep, send = call(first_kernel, (f32(8, BLK), f32(8, BLK)), 2, cost=small)(lines, crossed)
     send = lax.ppermute(send, LINE[0], [(0, 1), (1, 0)])
-    keep, send = call(second_kernel, (f32(8, BLK), f32(8, BLK)), 2, cost=small)(keep, send)
+    keep, send = call(second_kernel, (f32(2, BLK), f32(2, BLK)), 2, cost=small)(keep, send)
     send = lax.ppermute(send, LINE, [(i, SIDE - 1 - i) for i in range(SIDE)])
     return call(finish_kernel, (f32(BLK), f32(BLK)), 4)(got, own, keep, send)
 

time: 128 us -> 128 us (level)
  starting transfers between devices: 24.9 us -> 26.4 us
    all_to_all x1, waiting for transfers between devices: 3.66 us -> 0.01 us  [local(): got = lax.all_to_all(out, PLANE, 0, 0, tiled=True)]
    ppermute x1, waiting for transfers between devices: 0.01 us -> 1.73 us  [local(): send = lax.ppermute(send, LINE[0], [(0, 1), (1, 0)])]
    ppermute x1, waiting for transfers between devices: 0.01 us -> 1.56 us  [local(): send = lax.ppermute(send, LINE, [(i, SIDE - 1 - i) for i in range(SIDE)])]
    ppermute x1, starting transfers between devices: 2.6 us -> 4.12 us  [local(): send = lax.ppermute(send, LINE, [(i, SIDE - 1 - i) for i in range(SIDE)])]
  transfers between devices with their start and end apart: 9 -> 9, of which waited for: 6 -> 7; matrix products, arithmetic and copies ran while one was open for 0% -> 0% of each run, Pallas kernels for 34% -> 34%
where the time goes in v6:
time: 128 us
  Pallas kernels  89 us (70%)
  starting transfers between devices  26.4 us (21%)
  waiting for transfers between devices  12 us (9%)
    pallas_call x1, Pallas kernels, local(): call(functools.partial(half_kernel, nrow, ncol, True), (f32(8, BLK), f32(...  43 us
    pallas_call x1, Pallas kernels, local(): call(functools.partial(half_kernel, nrow, ncol, False), (jax.ShapeDtypeSt...  42.8 us
    all_to_all x1, starting transfers between devices, local(): cols = lax.all_to_all(copies, PLANE, 0, 0, tiled=True)  7.49 us
    ppermute x3, starting transfers between devices, local(): mine.append(lax.ppermute(rows, LINE, along(-k)))  6.51 us
    all_to_all x1, starting transfers between devices, local(): got = lax.all_to_all(out, PLANE, 0, 0, tiled=True)  6.11 us
    ppermute x1, starting transfers between devices, local(): send = lax.ppermute(send, LINE, [(i, SIDE - 1 - i) for i in range(SIDE)])  4.12 us
    all_to_all x1, waiting for transfers between devices, local(): cols = lax.all_to_all(copies, PLANE, 0, 0, tiled=True)  3.9 us
    ppermute x3, waiting for transfers between devices, local(): mine.append(lax.ppermute(rows, LINE, along(-k)))  3.3 us
  transfers between devices with their start and end apart: 9, of which 7 were waited for; matrix products, arithmetic and copies ran while one was open for 0% of the time, Pallas kernels for 34%

profile of v6, /device:TPU:2, one launch (start us, length us, event | category | flops | bytes accessed | tf_op | source)
XLA Modules:
  0.0 128.1 jit_solution(2170493921764221059)
XLA Ops:
  0.6 2.0 %shard_map.77 = (f32[136,128]{1,0:T(8,128)S(1)}, f32[16,136,128]{2,1,0:T(8,128)}) custom-call(f32[64,256]{1,0:T(8,128)} %spts.1, f32[64,256]{1,0:T(8,128)} %tpts.1, f32[2,128]{1,0:T(2,128)} %bitcast.12, f32[2,128]{1,0:T(2,128)} %bitcast.13, f32[2,128]{1,0:T(2,128)} %bitcast.14, f32[2,128]{1,0:T(2,128)} %bitcast.15), custom_call_target="tpu_custom_call" | custom-call | tf_op jit(solution)/shard_map/pallas_call | solution.py:307
  2.7 7.5 %all-to-all-start = ((f32[16,136,128]{2,1,0:T(8,128)}), f32[16,136,128]{2,1,0:T(8,128)S(1)}, u32[]{:S(2)}, u32[]{:S(2)}) async-start(f32[16,136,128]{2,1,0:T(8,128)} %get-tuple-element.17), calls=%async_computation | async-start | bytes 2228224 | tf_op jit(solution)/shard_map/all_to_all | solution.py:323
  10.2 1.9 %collective-permute-start.2 = (f32[136,128]{1,0:T(8,128)S(1)}, f32[136,128]{1,0:T(8,128)S(1)}, u32[]{:S(2)}, u32[]{:S(2)}) collective-permute-start(f32[136,128]{1,0:T(8,128)S(1)} %get-tuple-element.16.refs_0_), channel_id=1, source_target_pairs={{0,64},{64,16},{16,80},{80,0},{1,65},{65,17},{17,81},{81,1},{2,66}... | collective-permute-start | bytes 208904 | tf_op jit(solution)/shard_map/ppermute | solution.py:321
  12.1 3.6 %collective-permute-start.1 = (f32[136,128]{1,0:T(8,128)S(1)}, f32[136,128]{1,0:T(8,128)S(1)}, u32[]{:S(2)}, u32[]{:S(2)}) collective-permute-start(f32[136,128]{1,0:T(8,128)S(1)} %get-tuple-element.16.refs_0_), channel_id=1, source_target_pairs={{0,16},{64,80},{16,0},{80,64},{1,17},{65,81},{17,1},{81,65},{2,18}... | collective-permute-start | bytes 208904 | tf_op jit(solution)/shard_map/ppermute | solution.py:321
  15.7 1.0 collective-permute-start
  16.7 0.6 collective-permute-done.2.refs_3_
  17.2 1.5 %collective-permute-done.1.refs_2_ = f32[136,128]{1,0:T(8,128)S(1)} collective-permute-done((f32[136,128]{1,0:T(8,128)S(1)}, f32[136,128]{1,0:T(8,128)S(1)}, u32[]{:S(2)}, u32[]{:S(2)}) %collective-permute-start.1) | collective-permute-done | bytes 69664 | tf_op jit(solution)/shard_map/ppermute | solution.py:321
  18.7 1.3 collective-permute-done.refs_1_
  20.0 0.1 collective-permute-start.3
  20.1 1.5 %collective-permute-done.3.refs_4_.refs_0_ = f32[4,136,128]{2,1,0:T(8,128)S(1)} collective-permute-done((f32[4,136,128]{2,1,0:T(8,128)S(1)}, f32[4,136,128]{2,1,0:T(8,128)S(1)}, u32[]{:S(2)}, u32[]{:S(2)}) %collective-permute-start.3) | collective-permute-done | bytes 278560 | tf_op jit(solution)/shard_map/ppermute | solution.py:322
  21.6 0.4 shard_map.78
  22.0 3.9 %all-to-all-done.refs_1_.refs_4_ = f32[16,136,128]{2,1,0:T(8,128)S(1)} async-done(((f32[16,136,128]{2,1,0:T(8,128)}), f32[16,136,128]{2,1,0:T(8,128)S(1)}, u32[]{:S(2)}, u32[]{:S(2)}) %all-to-all-start) | async-done | bytes 1114144 | tf_op jit(solution)/shard_map/all_to_all | solution.py:323
  25.9 42.8 %shard_map.79 = (bf16[256,4096]{1,0:T(8,128)(2,1)S(1)}, f32[2,4096]{1,0:T(2,128)S(1)}, f32[8,256]{1,0:T(8,128)S(1)}) custom-call(f32[4,136,128]{2,1,0:T(8,128)S(1)} %collective-permute-done.3.refs_4_.refs_0_, f32[16,136,128]{2,1,0:T(8,128)S(1)} %all-to-all-done.refs_1_.refs_4_, bf16[2048,256]{1,0:T(8,128)(2,1)S(1)} %get-tuple-element.18.refs_2_.refs_5_, ...), custom_call_target="tpu_custom_call" | custom-call | flops 2147483648 | bytes 4194304 | tf_op jit(solution)/shard_map/pallas_call | solution.py:340
  68.8 0.1 collective-permute-start.4
  68.9 43.0 %shard_map.80 = (f32[8,256]{1,0:T(8,128)S(1)}, f32[16,1,256]{2,1,0:T(1,128)}, f32[8,256]{1,0:T(8,128)S(1)}) custom-call(f32[136,128]{1,0:T(8,128)S(1)} %get-tuple-element.16.refs_0_, f32[136,128]{1,0:T(8,128)S(1)} %collective-permute-done.refs_1_, f32[136,128]{1,0:T(8,128)S(1)} %collective-permute-done.1.refs_2_, ...), custom_call_target="tpu_custom_call" | custom-call | flops 2147483648 | bytes 4194304 | tf_op jit(solution)/shard_map/pallas_call | solution.py:348
  111.9 6.1 %all-to-all-start.1 = ((f32[16,1,256]{2,1,0:T(1,128)}), f32[16,1,256]{2,1,0:T(1,128)S(1)}, u32[]{:S(2)}, u32[]{:S(2)}) async-start(f32[16,1,256]{2,1,0:T(1,128)} %get-tuple-element.22), calls=%async_computation.1 | async-start | bytes 32768 | tf_op jit(solution)/shard_map/all_to_all | solution.py:355
  118.0 0.0 collective-permute-done.4.other
  118.1 2.0 %collective-permute-start.5 = (f32[8,256]{1,0:T(8,128)S(1)}, f32[8,256]{1,0:T(8,128)S(1)}, u32[]{:S(2)}, u32[]{:S(2)}) collective-permute-start(f32[8,256]{1,0:T(8,128)S(1)} %get-tuple-element.27), channel_id=1, source_target_pairs={{0,64},{64,0},{1,65},{65,1},{2,66},{66,2},{3,67},{67,3},{4,68},{68... | collective-permute-start | bytes 24584 | tf_op jit(solution)/shard_map/ppermute | solution.py:358
  120.1 1.7 %collective-permute-done.5.got = f32[8,256]{1,0:T(8,128)S(1)} collective-permute-done((f32[8,256]{1,0:T(8,128)S(1)}, f32[8,256]{1,0:T(8,128)S(1)}, u32[]{:S(2)}, u32[]{:S(2)}) %collective-permute-start.5) | collective-permute-done | bytes 8224 | tf_op jit(solution)/shard_map/ppermute | solution.py:358
  121.8 4.1 %collective-permute-start.6 = (f32[2,256]{1,0:T(2,128)S(1)}, f32[2,256]{1,0:T(2,128)S(1)}, u32[]{:S(2)}, u32[]{:S(2)}) collective-permute-start(f32[2,256]{1,0:T(2,128)S(1)} %get-tuple-element.29), channel_id=1, source_target_pairs={{0,80},{16,64},{64,16},{80,0},{1,81},{17,65},{65,17},{81,1},{2,82}... | collective-permute-start | bytes 6152 | tf_op jit(solution)/shard_map/ppermute | solution.py:360
  125.9 0.0 all-to-all-done.1.got
  125.9 1.6 %collective-permute-done.6.refs_1_ = f32[2,256]{1,0:T(2,128)S(1)} collective-permute-done((f32[2,256]{1,0:T(2,128)S(1)}, f32[2,256]{1,0:T(2,128)S(1)}, u32[]{:S(2)}, u32[]{:S(2)}) %collective-permute-start.6) | collective-permute-done | bytes 2080 | tf_op jit(solution)/shard_map/ppermute | solution.py:360
  127.5 0.6 shard_map.83
  (3 shorter events, 0.1 us)
Async XLA Ops:
  2.7 23.3 %all-to-all-start = ((f32[16,136,128]{2,1,0:T(8,128)}), f32[16,136,128]{2,1,0:T(8,128)S(1)}, u32[]{:S(2)}, u32[]{:S(2)}) async-start(f32[16,136,128]{2,1,0:T(8,128)} %get-tuple-element.17), calls=%async_computation | async-start | bytes 2228224 | tf_op jit(solution)/shard_map/all_to_all | solution.py:323
  10.2 7.1 %collective-permute-start.2 = (f32[136,128]{1,0:T(8,128)S(1)}, f32[136,128]{1,0:T(8,128)S(1)}, u32[]{:S(2)}, u32[]{:S(2)}) collective-permute-start(f32[136,128]{1,0:T(8,128)S(1)} %get-tuple-element.16.refs_0_), channel_id=1, source_target_pairs={{0,64},{64,16},{16,80},{80,0},{1,65},{65,17},{17,81},{81,1},{2,66}... | collective-permute-start | bytes 208904 | tf_op jit(solution)/shard_map/ppermute | solution.py:321
  12.1 6.6 %collective-permute-start.1 = (f32[136,128]{1,0:T(8,128)S(1)}, f32[136,128]{1,0:T(8,128)S(1)}, u32[]{:S(2)}, u32[]{:S(2)}) collective-permute-start(f32[136,128]{1,0:T(8,128)S(1)} %get-tuple-element.16.refs_0_), channel_id=1, source_target_pairs={{0,16},{64,80},{16,0},{80,64},{1,17},{65,81},{17,1},{81,65},{2,18}... | collective-permute-start | bytes 208904 | tf_op jit(solution)/shard_map/ppermute | solution.py:321
  15.7 4.3 %collective-permute-start = (f32[136,128]{1,0:T(8,128)S(1)}, f32[136,128]{1,0:T(8,128)S(1)}, u32[]{:S(2)}, u32[]{:S(2)}) collective-permute-start(f32[136,128]{1,0:T(8,128)S(1)} %get-tuple-element.16.refs_0_), channel_id=1, source_target_pairs={{0,80},{64,0},{16,64},{80,16},{1,81},{65,1},{17,65},{81,17},{2,82}... | collective-permute-start | bytes 208904 | tf_op jit(solution)/shard_map/ppermute | solution.py:321
  20.0 1.6 %collective-permute-start.3 = (f32[4,136,128]{2,1,0:T(8,128)S(1)}, f32[4,136,128]{2,1,0:T(8,128)S(1)}, u32[]{:S(2)}, u32[]{:S(2)}) collective-permute-start(f32[4,136,128]{2,1,0:T(8,128)S(1)} %pad_maximum_fusion), channel_id=1, source_target_pairs={{0,32},{32,0},{1,33},{33,1},{2,34},{34,2},{3,35},{35,3},{4,36},{36... | collective-permute-start | bytes 835592 | tf_op jit(solution)/shard_map/ppermute | solution.py:322
  68.8 49.2 %collective-permute-start.4 = (f32[8,256]{1,0:T(8,128)S(1)}, f32[8,256]{1,0:T(8,128)S(1)}, u32[]{:S(2)}, u32[]{:S(2)}) collective-permute-start(f32[8,256]{1,0:T(8,128)S(1)} %get-tuple-element.25), channel_id=1, source_target_pairs={{0,32},{32,0},{1,33},{33,1},{2,34},{34,2},{3,35},{35,3},{4,36},{36... | collective-permute-start | bytes 24584 | tf_op jit(solution)/shard_map/ppermute | solution.py:347
  111.9 14.0 %all-to-all-start.1 = ((f32[16,1,256]{2,1,0:T(1,128)}), f32[16,1,256]{2,1,0:T(1,128)S(1)}, u32[]{:S(2)}, u32[]{:S(2)}) async-start(f32[16,1,256]{2,1,0:T(1,128)} %get-tuple-element.22), calls=%async_computation.1 | async-start | bytes 32768 | tf_op jit(solution)/shard_map/all_to_all | solution.py:355
  118.1 3.7 %collective-permute-start.5 = (f32[8,256]{1,0:T(8,128)S(1)}, f32[8,256]{1,0:T(8,128)S(1)}, u32[]{:S(2)}, u32[]{:S(2)}) collective-permute-start(f32[8,256]{1,0:T(8,128)S(1)} %get-tuple-element.27), channel_id=1, source_target_pairs={{0,64},{64,0},{1,65},{65,1},{2,66},{66,2},{3,67},{67,3},{4,68},{68... | collective-permute-start | bytes 24584 | tf_op jit(solution)/shard_map/ppermute | solution.py:358
  121.8 5.7 %collective-permute-start.6 = (f32[2,256]{1,0:T(2,128)S(1)}, f32[2,256]{1,0:T(2,128)S(1)}, u32[]{:S(2)}, u32[]{:S(2)}) collective-permute-start(f32[2,256]{1,0:T(2,128)S(1)} %get-tuple-element.29), channel_id=1, source_target_pairs={{0,80},{16,64},{64,16},{80,0},{1,81},{17,65},{65,17},{81,1},{2,82}... | collective-permute-start | bytes 6152 | tf_op jit(solution)/shard_map/ppermute | solution.py:360

commit v7 on v6

--- a/solution.py
+++ b/solution.py
@@ -49,7 +49,7 @@
 
 def pack_kernel(spts, tpts, spot, tpot, slogw, tlogw, rows, copies, cols, lines, sems, out_sems):
     loads = []
-    for pts, block in ((spts, rows), (tpts, cols)):
+    for pts, block in ((tpts, cols), (spts, rows)):
         for half in range(2):
             loads.append((pts.at[:, 128 * half : 128 * (half + 1)], block.at[64 * half : 64 * (half + 1), :]))
     for k, ref in enumerate((slogw, spot, tlogw, tpot)):
@@ -59,16 +59,18 @@
         load.start()
     for k in range(4, 8):
         loads[k].wait()
-    for block, logw, pot, other in ((rows, lines[0], lines[1], lines[2]), (cols, lines[2], lines[3], lines[0])):
-        tail = (logw + pot / epsilon, logw, pot, other)
-        block[128:136, :] = jnp.concatenate(tail, 0)
-    loads[2].wait()
-    loads[3].wait()
+    tails = []
+    for logw, pot, other in ((lines[0], lines[1], lines[2]), (lines[2], lines[3], lines[0])):
+        tails.append(jnp.concatenate((logw + pot / epsilon, logw, pot, other), 0))
+    cols[128:136, :] = tails[1]
+    loads[0].wait()
+    loads[1].wait()
     stores = [pltpu.make_async_copy(cols, copies.at[k], out_sems.at[k]) for k in range(copies.shape[0])]
     for store in stores:
         store.start()
-    loads[0].wait()
-    loads[1].wait()
+    rows[128:136, :] = tails[0]
+    loads[2].wait()
+    loads[3].wait()
     for store in stores:
         store.wait()
 
@@ -133,30 +135,25 @@
     else:
         cols, xt, stats, yk, former, lines, rowacc, colacc, rmax, rsum, rlog = refs
 
-        def prepare(j, state):
-            most, masses = state
+        most = jnp.zeros((1, BLK), jnp.float32)
+        masses = jnp.zeros((8, 128), jnp.float32)
+    step = 512
+    first = 0 if last else nrow * BLK
+
+    for j in range(ncol):
+        at = slice(j * BLK, (j + 1) * BLK)
+        if last:
+            right = yk[:, at]
+        else:
             block = cols.at[j]
             pts, sq, term = unpacked(block)
             y1, y2 = split(pts)
-            bias = bias_lines((term - sq / epsilon) * LOG2E, 3)
-            at = pl.ds(pl.multiple_of(j * BLK, BLK), BLK)
+            bias = bias_lines((term - sq / epsilon) * LOG2E, 3).astype(jnp.bfloat16)
             y1 = y1.astype(jnp.bfloat16)
-            yk[0:64, at] = y1
-            yk[64:128, at] = y1
-            yk[128:192, at] = y2.astype(jnp.bfloat16)
-            yk[192:208, at] = bias.astype(jnp.bfloat16)
-            yk[208:256, at] = jnp.zeros((48, BLK), jnp.bfloat16)
-            return jnp.maximum(most, sq), masses + jnp.exp(block[128:136, :])
-
-        most, masses = lax.fori_loop(
-            0, ncol, prepare, (jnp.zeros((1, BLK), jnp.float32), jnp.zeros((8, 128), jnp.float32)), unroll=4
-        )
-    step = 512
-    first = 0 if last else nrow * BLK
-
-    for j in range(ncol):
-        at = slice(j * BLK, (j + 1) * BLK)
-        right = yk[:, at]
+            right = jnp.concatenate([y1, y1, y2.astype(jnp.bfloat16), bias, jnp.zeros((48, BLK), jnp.bfloat16)], 0)
+            yk[:, at] = right
+            most = jnp.maximum(most, sq)
+            masses = masses + jnp.exp(block[128:136, :])
         total = jnp.zeros((8, BLK), jnp.float32)
         for i in range(nrow * BLK // step):
             rows = slice(i * step, (i + 1) * step)

time: 128 us -> 128 us (level)
  no operation moved by 1% of the time
where the time goes in v7:
time: 128 us
  Pallas kernels  88.5 us (69%)
  starting transfers between devices  26.4 us (21%)
  waiting for transfers between devices  12 us (9%)
    pallas_call x1, Pallas kernels, local(): call(functools.partial(half_kernel, nrow, ncol, True), (f32(8, BLK), f32(...  43 us
    pallas_call x1, Pallas kernels, local(): call(functools.partial(half_kernel, nrow, ncol, False), (jax.ShapeDtypeSt...  42.4 us
    all_to_all x1, starting transfers between devices, local(): cols = lax.all_to_all(copies, PLANE, 0, 0, tiled=True)  7.49 us
    ppermute x3, starting transfers between devices, local(): mine.append(lax.ppermute(rows, LINE, along(-k)))  6.51 us
    all_to_all x1, starting transfers between devices, local(): got = lax.all_to_all(out, PLANE, 0, 0, tiled=True)  6.11 us
    ppermute x1, starting transfers between devices, local(): send = lax.ppermute(send, LINE, [(i, SIDE - 1 - i) for i in range(SIDE)])  4.14 us
    all_to_all x1, waiting for transfers between devices, local(): cols = lax.all_to_all(copies, PLANE, 0, 0, tiled=True)  3.9 us
    ppermute x3, waiting for transfers between devices, local(): mine.append(lax.ppermute(rows, LINE, along(-k)))  3.3 us
  transfers between devices with their start and end apart: 9, of which 7 were waited for; matrix products, arithmetic and copies ran while one was open for 0% of the time, Pallas kernels for 34%

profile of v7, /device:TPU:2, one launch (start us, length us, event | category | flops | bytes accessed | tf_op | source)
XLA Modules:
  0.0 127.7 jit_solution(17621136309003027031)
XLA Ops:
  0.6 2.0 %shard_map.77 = (f32[136,128]{1,0:T(8,128)S(1)}, f32[16,136,128]{2,1,0:T(8,128)}) custom-call(f32[64,256]{1,0:T(8,128)} %spts.1, f32[64,256]{1,0:T(8,128)} %tpts.1, f32[2,128]{1,0:T(2,128)} %bitcast.12, f32[2,128]{1,0:T(2,128)} %bitcast.13, f32[2,128]{1,0:T(2,128)} %bitcast.14, f32[2,128]{1,0:T(2,128)} %bitcast.15), custom_call_target="tpu_custom_call" | custom-call | tf_op jit(solution)/shard_map/pallas_call | solution.py:304
  2.7 7.5 %all-to-all-start = ((f32[16,136,128]{2,1,0:T(8,128)}), f32[16,136,128]{2,1,0:T(8,128)S(1)}, u32[]{:S(2)}, u32[]{:S(2)}) async-start(f32[16,136,128]{2,1,0:T(8,128)} %get-tuple-element.17), calls=%async_computation | async-start | bytes 2228224 | tf_op jit(solution)/shard_map/all_to_all | solution.py:320
  10.2 1.9 %collective-permute-start.2 = (f32[136,128]{1,0:T(8,128)S(1)}, f32[136,128]{1,0:T(8,128)S(1)}, u32[]{:S(2)}, u32[]{:S(2)}) collective-permute-start(f32[136,128]{1,0:T(8,128)S(1)} %get-tuple-element.16.refs_0_), channel_id=1, source_target_pairs={{0,64},{64,16},{16,80},{80,0},{1,65},{65,17},{17,81},{81,1},{2,66}... | collective-permute-start | bytes 208904 | tf_op jit(solution)/shard_map/ppermute | solution.py:318
  12.1 3.6 %collective-permute-start.1 = (f32[136,128]{1,0:T(8,128)S(1)}, f32[136,128]{1,0:T(8,128)S(1)}, u32[]{:S(2)}, u32[]{:S(2)}) collective-permute-start(f32[136,128]{1,0:T(8,128)S(1)} %get-tuple-element.16.refs_0_), channel_id=1, source_target_pairs={{0,16},{64,80},{16,0},{80,64},{1,17},{65,81},{17,1},{81,65},{2,18}... | collective-permute-start | bytes 208904 | tf_op jit(solution)/shard_map/ppermute | solution.py:318
  15.7 1.0 collective-permute-start
  16.7 0.6 collective-permute-done.2.refs_3_
  17.2 1.5 %collective-permute-done.1.refs_2_ = f32[136,128]{1,0:T(8,128)S(1)} collective-permute-done((f32[136,128]{1,0:T(8,128)S(1)}, f32[136,128]{1,0:T(8,128)S(1)}, u32[]{:S(2)}, u32[]{:S(2)}) %collective-permute-start.1) | collective-permute-done | bytes 69664 | tf_op jit(solution)/shard_map/ppermute | solution.py:318
  18.7 1.3 %collective-permute-done.refs_1_ = f32[136,128]{1,0:T(8,128)S(1)} collective-permute-done((f32[136,128]{1,0:T(8,128)S(1)}, f32[136,128]{1,0:T(8,128)S(1)}, u32[]{:S(2)}, u32[]{:S(2)}) %collective-permute-start) | collective-permute-done | bytes 69664 | tf_op jit(solution)/shard_map/ppermute | solution.py:318
  20.0 0.1 collective-permute-start.3
  20.1 1.5 %collective-permute-done.3.refs_4_.refs_0_ = f32[4,136,128]{2,1,0:T(8,128)S(1)} collective-permute-done((f32[4,136,128]{2,1,0:T(8,128)S(1)}, f32[4,136,128]{2,1,0:T(8,128)S(1)}, u32[]{:S(2)}, u32[]{:S(2)}) %collective-permute-start.3) | collective-permute-done | bytes 278560 | tf_op jit(solution)/shard_map/ppermute | solution.py:319
  21.6 0.4 shard_map.78
  22.0 3.9 %all-to-all-done.refs_1_.refs_4_ = f32[16,136,128]{2,1,0:T(8,128)S(1)} async-done(((f32[16,136,128]{2,1,0:T(8,128)}), f32[16,136,128]{2,1,0:T(8,128)S(1)}, u32[]{:S(2)}, u32[]{:S(2)}) %all-to-all-start) | async-done | bytes 1114144 | tf_op jit(solution)/shard_map/all_to_all | solution.py:320
  25.9 42.4 %shard_map.79 = (bf16[256,4096]{1,0:T(8,128)(2,1)S(1)}, f32[2,4096]{1,0:T(2,128)S(1)}, f32[8,256]{1,0:T(8,128)S(1)}) custom-call(f32[4,136,128]{2,1,0:T(8,128)S(1)} %collective-permute-done.3.refs_4_.refs_0_, f32[16,136,128]{2,1,0:T(8,128)S(1)} %all-to-all-done.refs_1_.refs_4_, bf16[2048,256]{1,0:T(8,128)(2,1)S(1)} %get-tuple-element.18.refs_2_.refs_5_, ...), custom_call_target="tpu_custom_call" | custom-call | flops 2147483648 | bytes 4194304 | tf_op jit(solution)/shard_map/pallas_call | solution.py:337
  68.3 0.1 collective-permute-start.4
  68.4 43.0 %shard_map.80 = (f32[8,256]{1,0:T(8,128)S(1)}, f32[16,1,256]{2,1,0:T(1,128)}, f32[8,256]{1,0:T(8,128)S(1)}) custom-call(f32[136,128]{1,0:T(8,128)S(1)} %get-tuple-element.16.refs_0_, f32[136,128]{1,0:T(8,128)S(1)} %collective-permute-done.refs_1_, f32[136,128]{1,0:T(8,128)S(1)} %collective-permute-done.1.refs_2_, ...), custom_call_target="tpu_custom_call" | custom-call | flops 2147483648 | bytes 4194304 | tf_op jit(solution)/shard_map/pallas_call | solution.py:345
  111.5 6.1 %all-to-all-start.1 = ((f32[16,1,256]{2,1,0:T(1,128)}), f32[16,1,256]{2,1,0:T(1,128)S(1)}, u32[]{:S(2)}, u32[]{:S(2)}) async-start(f32[16,1,256]{2,1,0:T(1,128)} %get-tuple-element.22), calls=%async_computation.1 | async-start | bytes 32768 | tf_op jit(solution)/shard_map/all_to_all | solution.py:352
  117.6 0.0 collective-permute-done.4.other
  117.6 2.0 %collective-permute-start.5 = (f32[8,256]{1,0:T(8,128)S(1)}, f32[8,256]{1,0:T(8,128)S(1)}, u32[]{:S(2)}, u32[]{:S(2)}) collective-permute-start(f32[8,256]{1,0:T(8,128)S(1)} %get-tuple-element.27), channel_id=1, source_target_pairs={{0,64},{64,0},{1,65},{65,1},{2,66},{66,2},{3,67},{67,3},{4,68},{68... | collective-permute-start | bytes 24584 | tf_op jit(solution)/shard_map/ppermute | solution.py:355
  119.6 1.7 %collective-permute-done.5.got = f32[8,256]{1,0:T(8,128)S(1)} collective-permute-done((f32[8,256]{1,0:T(8,128)S(1)}, f32[8,256]{1,0:T(8,128)S(1)}, u32[]{:S(2)}, u32[]{:S(2)}) %collective-permute-start.5) | collective-permute-done | bytes 8224 | tf_op jit(solution)/shard_map/ppermute | solution.py:355
  121.4 4.1 %collective-permute-start.6 = (f32[2,256]{1,0:T(2,128)S(1)}, f32[2,256]{1,0:T(2,128)S(1)}, u32[]{:S(2)}, u32[]{:S(2)}) collective-permute-start(f32[2,256]{1,0:T(2,128)S(1)} %get-tuple-element.29), channel_id=1, source_target_pairs={{0,80},{16,64},{64,16},{80,0},{1,81},{17,65},{65,17},{81,1},{2,82}... | collective-permute-start | bytes 6152 | tf_op jit(solution)/shard_map/ppermute | solution.py:357
  125.5 0.0 all-to-all-done.1.got
  125.5 1.6 %collective-permute-done.6.refs_1_ = f32[2,256]{1,0:T(2,128)S(1)} collective-permute-done((f32[2,256]{1,0:T(2,128)S(1)}, f32[2,256]{1,0:T(2,128)S(1)}, u32[]{:S(2)}, u32[]{:S(2)}) %collective-permute-start.6) | collective-permute-done | bytes 2080 | tf_op jit(solution)/shard_map/ppermute | solution.py:357
  127.1 0.6 shard_map.83
  (3 shorter events, 0.1 us)
Async XLA Ops:
  2.7 23.3 %all-to-all-start = ((f32[16,136,128]{2,1,0:T(8,128)}), f32[16,136,128]{2,1,0:T(8,128)S(1)}, u32[]{:S(2)}, u32[]{:S(2)}) async-start(f32[16,136,128]{2,1,0:T(8,128)} %get-tuple-element.17), calls=%async_computation | async-start | bytes 2228224 | tf_op jit(solution)/shard_map/all_to_all | solution.py:320
  10.2 7.1 %collective-permute-start.2 = (f32[136,128]{1,0:T(8,128)S(1)}, f32[136,128]{1,0:T(8,128)S(1)}, u32[]{:S(2)}, u32[]{:S(2)}) collective-permute-start(f32[136,128]{1,0:T(8,128)S(1)} %get-tuple-element.16.refs_0_), channel_id=1, source_target_pairs={{0,64},{64,16},{16,80},{80,0},{1,65},{65,17},{17,81},{81,1},{2,66}... | collective-permute-start | bytes 208904 | tf_op jit(solution)/shard_map/ppermute | solution.py:318
  12.1 6.6 %collective-permute-start.1 = (f32[136,128]{1,0:T(8,128)S(1)}, f32[136,128]{1,0:T(8,128)S(1)}, u32[]{:S(2)}, u32[]{:S(2)}) collective-permute-start(f32[136,128]{1,0:T(8,128)S(1)} %get-tuple-element.16.refs_0_), channel_id=1, source_target_pairs={{0,16},{64,80},{16,0},{80,64},{1,17},{65,81},{17,1},{81,65},{2,18}... | collective-permute-start | bytes 208904 | tf_op jit(solution)/shard_map/ppermute | solution.py:318
  15.7 4.3 %collective-permute-start = (f32[136,128]{1,0:T(8,128)S(1)}, f32[136,128]{1,0:T(8,128)S(1)}, u32[]{:S(2)}, u32[]{:S(2)}) collective-permute-start(f32[136,128]{1,0:T(8,128)S(1)} %get-tuple-element.16.refs_0_), channel_id=1, source_target_pairs={{0,80},{64,0},{16,64},{80,16},{1,81},{65,1},{17,65},{81,17},{2,82}... | collective-permute-start | bytes 208904 | tf_op jit(solution)/shard_map/ppermute | solution.py:318
  20.0 1.6 %collective-permute-start.3 = (f32[4,136,128]{2,1,0:T(8,128)S(1)}, f32[4,136,128]{2,1,0:T(8,128)S(1)}, u32[]{:S(2)}, u32[]{:S(2)}) collective-permute-start(f32[4,136,128]{2,1,0:T(8,128)S(1)} %pad_maximum_fusion), channel_id=1, source_target_pairs={{0,32},{32,0},{1,33},{33,1},{2,34},{34,2},{3,35},{35,3},{4,36},{36... | collective-permute-start | bytes 835592 | tf_op jit(solution)/shard_map/ppermute | solution.py:319
  68.3 49.3 %collective-permute-start.4 = (f32[8,256]{1,0:T(8,128)S(1)}, f32[8,256]{1,0:T(8,128)S(1)}, u32[]{:S(2)}, u32[]{:S(2)}) collective-permute-start(f32[8,256]{1,0:T(8,128)S(1)} %get-tuple-element.25), channel_id=1, source_target_pairs={{0,32},{32,0},{1,33},{33,1},{2,34},{34,2},{3,35},{35,3},{4,36},{36... | collective-permute-start | bytes 24584 | tf_op jit(solution)/shard_map/ppermute | solution.py:344
  111.5 14.0 %all-to-all-start.1 = ((f32[16,1,256]{2,1,0:T(1,128)}), f32[16,1,256]{2,1,0:T(1,128)S(1)}, u32[]{:S(2)}, u32[]{:S(2)}) async-start(f32[16,1,256]{2,1,0:T(1,128)} %get-tuple-element.22), calls=%async_computation.1 | async-start | bytes 32768 | tf_op jit(solution)/shard_map/all_to_all | solution.py:352
  117.6 3.7 %collective-permute-start.5 = (f32[8,256]{1,0:T(8,128)S(1)}, f32[8,256]{1,0:T(8,128)S(1)}, u32[]{:S(2)}, u32[]{:S(2)}) collective-permute-start(f32[8,256]{1,0:T(8,128)S(1)} %get-tuple-element.27), channel_id=1, source_target_pairs={{0,64},{64,0},{1,65},{65,1},{2,66},{66,2},{3,67},{67,3},{4,68},{68... | collective-permute-start | bytes 24584 | tf_op jit(solution)/shard_map/ppermute | solution.py:355
  121.4 5.7 %collective-permute-start.6 = (f32[2,256]{1,0:T(2,128)S(1)}, f32[2,256]{1,0:T(2,128)S(1)}, u32[]{:S(2)}, u32[]{:S(2)}) collective-permute-start(f32[2,256]{1,0:T(2,128)S(1)} %get-tuple-element.29), channel_id=1, source_target_pairs={{0,80},{16,64},{64,16},{80,0},{1,81},{17,65},{65,17},{81,1},{2,82}... | collective-permute-start | bytes 6152 | tf_op jit(solution)/shard_map/ppermute | solution.py:357

commit v8 on v7

--- a/solution.py
+++ b/solution.py
@@ -8,11 +8,10 @@
 from jax.sharding import Mesh
 from jax.sharding import PartitionSpec as P
 
-GRP_MEM = ("grp_0", "grp_1", "mem_0", "mem_1", "mem_2")
-GROUP = ("grp_0", "grp_1", "mem_0")
-PLANE = ("mem_1", "mem_2")
+GRP_MEM = ("grp_0", "grp_1", "mem_0", "mem_1", "mem_2", "mem_3")
+COLS = ("grp_1", "mem_1", "mem_3")
 LINE = ("grp_0", "mem_0")
-CORE = "grp_1"
+FACE = ("mem_2", "mem_3")
 SIDE = 4
 
 epsilon = 4.0
@@ -108,6 +107,7 @@
 
 def rows_kernel(*refs):
     blocks = blocks_of(refs[:-2])
+    blocks = blocks[0::2] + blocks[1::2]
     xt, stats = refs[-2:]
     most = jnp.zeros((1, BLK), jnp.float32)
     for k, block in enumerate(blocks):
@@ -127,8 +127,8 @@
 
 
 def half_kernel(nrow, ncol, last, *refs):
-    blocks = blocks_of(refs[:nrow_refs(last)])
-    refs = refs[nrow_refs(last) :]
+    blocks = blocks_of(refs[:SIDE])[0 if last else 1 :: 2]
+    refs = refs[SIDE:]
     if last:
         cols, xt, stats, yk, former, lines, out, own, rowacc, colacc, rmax, rsum, rlog = refs
         most = former[1:2, 0:BLK]
@@ -230,11 +230,12 @@
         both = both_logs(colacc[0:1, :], former[0:1, :])
         for j in range(ncol):
             out[j] = both[:, j * BLK : (j + 1) * BLK]
-        at_plane = lax.axis_index("mem_1") * SIDE + lax.axis_index("mem_2")
+        core, x, low = (lax.axis_index(n) for n in COLS)
+        here = (core * SIDE + x) * 2 + low
         own[0:1, :] = wide(blocks[0], 128)
         own[1:2, :] = wide(blocks[0], 132)
-        own[2:3, :] = wide(cols.at[at_plane], 128)
-        own[3:4, :] = wide(cols.at[at_plane], 132)
+        own[2:3, :] = wide(cols.at[here], 128)
+        own[3:4, :] = wide(cols.at[here], 132)
     else:
         target_mass = jnp.sum(masses[2:4, :], keepdims=True)
         source_mass = jnp.sum(masses[6:8, :], keepdims=True)
@@ -247,10 +248,6 @@
         former[1:2, BLK : 2 * BLK] = mass
 
 
-def nrow_refs(last):
-    return SIDE if last else 1
-
-
 def both_logs(a, b):
     peak = jnp.maximum(a, b)
     return peak + jnp.log(jnp.exp(a - peak) + jnp.exp(b - peak))
@@ -299,7 +296,7 @@
 
 
 def local(source_pts, target_pts, source_pot, target_pot, source_logw, target_logw):
-    nrow, ncol = lax.axis_size(GROUP), lax.axis_size(PLANE)
+    nrow, ncol = SIDE, lax.axis_size(COLS)
     lines = [v.reshape(2, 128) for v in (source_pot, target_pot, source_logw, target_logw)]
     rows, copies = call(
         pack_kernel,
@@ -313,20 +310,20 @@
         ],
         specs=(VMEM, HBM),
     )(*(pltpu.with_memory_space_constraint(v, pltpu.HBM) for v in (source_pts, target_pts, *lines)))
-    mine = [rows]
+    turned = [(i, SIDE - 1 - i) for i in range(SIDE)]
+    pair = jnp.stack([rows, lax.ppermute(rows, FACE, turned)])
+    mine = [pair]
     for k in range(1, SIDE):
-        mine.append(lax.ppermute(rows, LINE, along(-k)))
-    others = lax.ppermute(jnp.stack(mine), CORE, [(0, 1), (1, 0)])
-    cols = lax.all_to_all(copies, PLANE, 0, 0, tiled=True)
-    nrow = nrow // 2
+        mine.append(lax.ppermute(pair, LINE, along(-k)))
+    cols = lax.all_to_all(copies, COLS, 0, 0, tiled=True)
     size = nrow * ncol * BLK * BLK
     cost = pl.CostEstimate(flops=512 * size, bytes_accessed=4 * 2**20, transcendentals=size)
     xt, stats = call(
         rows_kernel,
         (jax.ShapeDtypeStruct((2 * nrow * BLK, 256), jnp.bfloat16), f32(1, BLK)),
-        5,
+        SIDE,
         cost=pl.CostEstimate(flops=10**6, bytes_accessed=10**6, transcendentals=0),
-    )(*mine, others)
+    )(*mine)
     scratch = [
         pltpu.VMEM((nrow * BLK, 128), jnp.float32),
         pltpu.VMEM((8, ncol * BLK), jnp.float32),
@@ -337,11 +334,11 @@
     yk, former, lines = call(
         functools.partial(half_kernel, nrow, ncol, False),
         (jax.ShapeDtypeStruct((256, ncol * BLK), jnp.bfloat16), f32(2, ncol * BLK), f32(8, BLK)),
-        4,
+        SIDE + 3,
         scratch=scratch,
         cost=cost,
-    )(others, cols, xt, stats)
-    crossed = lax.ppermute(lines, CORE, [(0, 1), (1, 0)])
+    )(*mine, cols, xt, stats)
+    crossed = lax.ppermute(lines, FACE, turned)
     lines, out, own = call(
         functools.partial(half_kernel, nrow, ncol, True),
         (f32(8, BLK), f32(ncol, 1, BLK), f32(8, BLK)),
@@ -349,17 +346,17 @@
         scratch=scratch,
         cost=cost,
     )(*mine, cols, xt, stats, yk, former)
-    got = lax.all_to_all(out, PLANE, 0, 0, tiled=True)
+    got = lax.all_to_all(out, COLS, 0, 0, tiled=True)
     small = pl.CostEstimate(flops=10**5, bytes_accessed=10**5, transcendentals=0)
     keep, send = call(first_kernel, (f32(8, BLK), f32(8, BLK)), 2, cost=small)(lines, crossed)
     send = lax.ppermute(send, LINE[0], [(0, 1), (1, 0)])
     keep, send = call(second_kernel, (f32(2, BLK), f32(2, BLK)), 2, cost=small)(keep, send)
-    send = lax.ppermute(send, LINE, [(i, SIDE - 1 - i) for i in range(SIDE)])
+    send = lax.ppermute(send, LINE, turned)
     return call(finish_kernel, (f32(BLK), f32(BLK)), 4)(got, own, keep, send)
 
 
 def solution(mesh):
-    finer = Mesh(mesh.devices.reshape(2, 2, 2, 4, 4), GRP_MEM)
+    finer = Mesh(mesh.devices.reshape(2, 2, 2, 4, 2, 2), GRP_MEM)
     return jax.shard_map(
         local,
         mesh=finer,

time: 128 us -> 129 us (level)
  starting transfers between devices: 26.4 us -> 27.8 us
    ppermute x6, starting transfers between devices: 10.8 us -> 15.7 us  [the longest x3 6.58 us: local(): mine.append(lax.ppermute(pair, LINE, along(-k)))]
    all_to_all x2, waiting for transfers between devices: 3.91 us -> 0.01 us  [the longest x1 0.01 us: local(): cols = lax.all_to_all(copies, COLS, 0, 0, tiled=True)]
    all_to_all x2, starting transfers between devices: 13.6 us -> 10.8 us  [the longest x1 5.87 us: local(): cols = lax.all_to_all(copies, COLS, 0, 0, tiled=True)]
    ppermute x6, waiting for transfers between devices: 6.41 us -> 8.78 us  [the longest x3 4.53 us: local(): mine.append(lax.ppermute(pair, LINE, along(-k)))]
  transfers between devices with their start and end apart: 9 -> 9, of which waited for: 7 -> 5; matrix products, arithmetic and copies ran while one was open for 0% -> 0% of each run, Pallas kernels for 34% -> 34%
where the time goes in v8:
time: 129 us
  Pallas kernels  88.9 us (69%)
  starting transfers between devices  27.8 us (22%)
  waiting for transfers between devices  11.2 us (9%)
    pallas_call x1, Pallas kernels, local(): call(functools.partial(half_kernel, nrow, ncol, True), (f32(8, BLK), f32(...  43.2 us
    pallas_call x1, Pallas kernels, local(): call(functools.partial(half_kernel, nrow, ncol, False), (jax.ShapeDtypeSt...  42.6 us
    ppermute x3, starting transfers between devices, local(): mine.append(lax.ppermute(pair, LINE, along(-k)))  6.58 us
    all_to_all x1, starting transfers between devices, local(): cols = lax.all_to_all(copies, COLS, 0, 0, tiled=True)  5.87 us
    all_to_all x1, starting transfers between devices, local(): got = lax.all_to_all(out, COLS, 0, 0, tiled=True)  4.95 us
    ppermute x3, waiting for transfers between devices, local(): mine.append(lax.ppermute(pair, LINE, along(-k)))  4.53 us
    ppermute x1, starting transfers between devices, local(): send = lax.ppermute(send, LINE, turned)  3.24 us
    ppermute x1, starting transfers between devices, local(): crossed = lax.ppermute(lines, FACE, turned)  2.99 us
  transfers between devices with their start and end apart: 9, of which 5 were waited for; matrix products, arithmetic and copies ran while one was open for 0% of the time, Pallas kernels for 34%

profile of v8, /device:TPU:2, one launch (start us, length us, event | category | flops | bytes accessed | tf_op | source)
XLA Modules:
  0.0 128.7 jit_solution(1053187139846886163)
XLA Ops:
  0.6 2.0 %shard_map.77 = (f32[136,128]{1,0:T(8,128)S(1)}, f32[16,136,128]{2,1,0:T(8,128)}) custom-call(f32[64,256]{1,0:T(8,128)} %spts.1, f32[64,256]{1,0:T(8,128)} %tpts.1, f32[2,128]{1,0:T(2,128)} %bitcast.8, f32[2,128]{1,0:T(2,128)} %bitcast.9, f32[2,128]{1,0:T(2,128)} %bitcast.10, f32[2,128]{1,0:T(2,128)} %bitcast.11), custom_call_target="tpu_custom_call" | custom-call | tf_op jit(solution)/shard_map/pallas_call | solution.py:301
  2.7 5.9 %all-to-all-start = ((f32[16,136,128]{2,1,0:T(8,128)}), f32[16,136,128]{2,1,0:T(8,128)S(1)}, u32[]{:S(2)}, u32[]{:S(2)}) async-start(f32[16,136,128]{2,1,0:T(8,128)} %get-tuple-element.17), calls=%async_computation | async-start | bytes 2228224 | tf_op jit(solution)/shard_map/all_to_all | solution.py:318
  8.5 2.9 %collective-permute-start = (f32[136,128]{1,0:T(8,128)S(1)}, f32[136,128]{1,0:T(8,128)S(1)}, u32[]{:S(2)}, u32[]{:S(2)}) collective-permute-start(f32[136,128]{1,0:T(8,128)S(1)} %get-tuple-element.16), channel_id=1, source_target_pairs={{0,3},{1,2},{2,1},{3,0},{4,7},{5,6},{6,5},{7,4},{8,11},{9,10},{10,... | collective-permute-start | bytes 208904 | tf_op jit(solution)/shard_map/ppermute | solution.py:314
  11.4 2.6 %collective-permute-done = f32[136,128]{1,0:T(8,128)S(1)} collective-permute-done((f32[136,128]{1,0:T(8,128)S(1)}, f32[136,128]{1,0:T(8,128)S(1)}, u32[]{:S(2)}, u32[]{:S(2)}) %collective-permute-start) | collective-permute-done | bytes 69664 | tf_op jit(solution)/shard_map/ppermute | solution.py:314
  14.1 2.0 %collective-permute-start.3 = (f32[2,136,128]{2,1,0:T(8,128)S(1)}, f32[2,136,128]{2,1,0:T(8,128)S(1)}, u32[]{:S(2)}, u32[]{:S(2)}) collective-permute-start(f32[2,136,128]{2,1,0:T(8,128)S(1)} %pad_maximum_fusion.refs_0_), channel_id=1, source_target_pairs={{0,64},{64,16},{16,80},{80,0},{1,65},{65,17},{17,81},{81,1},{2,66}... | collective-permute-start | bytes 417800 | tf_op jit(solution)/shard_map/ppermute | solution.py:317
  16.1 3.6 %collective-permute-start.2 = (f32[2,136,128]{2,1,0:T(8,128)S(1)}, f32[2,136,128]{2,1,0:T(8,128)S(1)}, u32[]{:S(2)}, u32[]{:S(2)}) collective-permute-start(f32[2,136,128]{2,1,0:T(8,128)S(1)} %pad_maximum_fusion.refs_0_), channel_id=1, source_target_pairs={{0,16},{64,80},{16,0},{80,64},{1,17},{65,81},{17,1},{81,65},{2,18}... | collective-permute-start | bytes 417800 | tf_op jit(solution)/shard_map/ppermute | solution.py:317
  19.6 1.0 collective-permute-start.1
  20.6 1.6 %collective-permute-done.3.refs_3_ = f32[2,136,128]{2,1,0:T(8,128)S(1)} collective-permute-done((f32[2,136,128]{2,1,0:T(8,128)S(1)}, f32[2,136,128]{2,1,0:T(8,128)S(1)}, u32[]{:S(2)}, u32[]{:S(2)}) %collective-permute-start.3) | collective-permute-done | bytes 139296 | tf_op jit(solution)/shard_map/ppermute | solution.py:317
  22.3 2.9 %collective-permute-done.2.refs_2_ = f32[2,136,128]{2,1,0:T(8,128)S(1)} collective-permute-done((f32[2,136,128]{2,1,0:T(8,128)S(1)}, f32[2,136,128]{2,1,0:T(8,128)S(1)}, u32[]{:S(2)}, u32[]{:S(2)}) %collective-permute-start.2) | collective-permute-done | bytes 139296 | tf_op jit(solution)/shard_map/ppermute | solution.py:317
  25.2 0.0 collective-permute-done.1.refs_1_
  25.2 0.4 shard_map.78
  25.6 0.0 all-to-all-done.refs_4_
  25.6 42.6 %shard_map.79 = (bf16[256,4096]{1,0:T(8,128)(2,1)S(1)}, f32[2,4096]{1,0:T(2,128)S(1)}, f32[8,256]{1,0:T(8,128)S(1)}) custom-call(f32[2,136,128]{2,1,0:T(8,128)S(1)} %pad_maximum_fusion.refs_0_, f32[2,136,128]{2,1,0:T(8,128)S(1)} %collective-permute-done.1.refs_1_, f32[2,136,128]{2,1,0:T(8,128)S(1)} %collective-permute-done.2.refs_2_, ...), custom_call_target="tpu_custom_call" | custom-call | flops 2147483648 | bytes 4194304 | tf_op jit(solution)/shard_map/pallas_call | solution.py:334
  68.2 3.0 %collective-permute-start.4 = (f32[8,256]{1,0:T(8,128)S(1)}, f32[8,256]{1,0:T(8,128)S(1)}, u32[]{:S(2)}, u32[]{:S(2)}) collective-permute-start(f32[8,256]{1,0:T(8,128)S(1)} %get-tuple-element.25), channel_id=1, source_target_pairs={{0,3},{1,2},{2,1},{3,0},{4,7},{5,6},{6,5},{7,4},{8,11},{9,10},{10,... | collective-permute-start | bytes 24584 | tf_op jit(solution)/shard_map/ppermute | solution.py:341
  71.2 43.2 %shard_map.80 = (f32[8,256]{1,0:T(8,128)S(1)}, f32[16,1,256]{2,1,0:T(1,128)}, f32[8,256]{1,0:T(8,128)S(1)}) custom-call(f32[2,136,128]{2,1,0:T(8,128)S(1)} %pad_maximum_fusion.refs_0_, f32[2,136,128]{2,1,0:T(8,128)S(1)} %collective-permute-done.1.refs_1_, f32[2,136,128]{2,1,0:T(8,128)S(1)} %collective-permute-done.2.refs_2_, ...), custom_call_target="tpu_custom_call" | custom-call | flops 2147483648 | bytes 4194304 | tf_op jit(solution)/shard_map/pallas_call | solution.py:342
  114.4 5.0 %all-to-all-start.1 = ((f32[16,1,256]{2,1,0:T(1,128)}), f32[16,1,256]{2,1,0:T(1,128)S(1)}, u32[]{:S(2)}, u32[]{:S(2)}) async-start(f32[16,1,256]{2,1,0:T(1,128)} %get-tuple-element.22), calls=%async_computation.1 | async-start | bytes 32768 | tf_op jit(solution)/shard_map/all_to_all | solution.py:349
  119.4 0.0 collective-permute-done.4.other
  119.4 1.3 %collective-permute-start.5 = (f32[8,256]{1,0:T(8,128)S(1)}, f32[8,256]{1,0:T(8,128)S(1)}, u32[]{:S(2)}, u32[]{:S(2)}) collective-permute-start(f32[8,256]{1,0:T(8,128)S(1)} %get-tuple-element.27), channel_id=1, source_target_pairs={{0,64},{64,0},{1,65},{65,1},{2,66},{66,2},{3,67},{67,3},{4,68},{68... | collective-permute-start | bytes 24584 | tf_op jit(solution)/shard_map/ppermute | solution.py:352
  120.7 2.4 %collective-permute-done.5.got = f32[8,256]{1,0:T(8,128)S(1)} collective-permute-done((f32[8,256]{1,0:T(8,128)S(1)}, f32[8,256]{1,0:T(8,128)S(1)}, u32[]{:S(2)}, u32[]{:S(2)}) %collective-permute-start.5) | collective-permute-done | bytes 8224 | tf_op jit(solution)/shard_map/ppermute | solution.py:352
  123.2 3.2 %collective-permute-start.6 = (f32[2,256]{1,0:T(2,128)S(1)}, f32[2,256]{1,0:T(2,128)S(1)}, u32[]{:S(2)}, u32[]{:S(2)}) collective-permute-start(f32[2,256]{1,0:T(2,128)S(1)} %get-tuple-element.29), channel_id=1, source_target_pairs={{0,80},{16,64},{64,16},{80,0},{1,81},{17,65},{65,17},{81,1},{2,82}... | collective-permute-start | bytes 6152 | tf_op jit(solution)/shard_map/ppermute | solution.py:354
  126.4 0.0 all-to-all-done.1.got
  126.4 1.6 %collective-permute-done.6.refs_1_ = f32[2,256]{1,0:T(2,128)S(1)} collective-permute-done((f32[2,256]{1,0:T(2,128)S(1)}, f32[2,256]{1,0:T(2,128)S(1)}, u32[]{:S(2)}, u32[]{:S(2)}) %collective-permute-start.6) | collective-permute-done | bytes 2080 | tf_op jit(solution)/shard_map/ppermute | solution.py:354
  128.0 0.6 shard_map.83
  (3 shorter events, 0.1 us)
Async XLA Ops:
  2.7 22.9 %all-to-all-start = ((f32[16,136,128]{2,1,0:T(8,128)}), f32[16,136,128]{2,1,0:T(8,128)S(1)}, u32[]{:S(2)}, u32[]{:S(2)}) async-start(f32[16,136,128]{2,1,0:T(8,128)} %get-tuple-element.17), calls=%async_computation | async-start | bytes 2228224 | tf_op jit(solution)/shard_map/all_to_all | solution.py:318
  8.5 5.5 %collective-permute-start = (f32[136,128]{1,0:T(8,128)S(1)}, f32[136,128]{1,0:T(8,128)S(1)}, u32[]{:S(2)}, u32[]{:S(2)}) collective-permute-start(f32[136,128]{1,0:T(8,128)S(1)} %get-tuple-element.16), channel_id=1, source_target_pairs={{0,3},{1,2},{2,1},{3,0},{4,7},{5,6},{6,5},{7,4},{8,11},{9,10},{10,... | collective-permute-start | bytes 208904 | tf_op jit(solution)/shard_map/ppermute | solution.py:314
  14.1 8.2 %collective-permute-start.3 = (f32[2,136,128]{2,1,0:T(8,128)S(1)}, f32[2,136,128]{2,1,0:T(8,128)S(1)}, u32[]{:S(2)}, u32[]{:S(2)}) collective-permute-start(f32[2,136,128]{2,1,0:T(8,128)S(1)} %pad_maximum_fusion.refs_0_), channel_id=1, source_target_pairs={{0,64},{64,16},{16,80},{80,0},{1,65},{65,17},{17,81},{81,1},{2,66}... | collective-permute-start | bytes 417800 | tf_op jit(solution)/shard_map/ppermute | solution.py:317
  16.1 9.1 %collective-permute-start.2 = (f32[2,136,128]{2,1,0:T(8,128)S(1)}, f32[2,136,128]{2,1,0:T(8,128)S(1)}, u32[]{:S(2)}, u32[]{:S(2)}) collective-permute-start(f32[2,136,128]{2,1,0:T(8,128)S(1)} %pad_maximum_fusion.refs_0_), channel_id=1, source_target_pairs={{0,16},{64,80},{16,0},{80,64},{1,17},{65,81},{17,1},{81,65},{2,18}... | collective-permute-start | bytes 417800 | tf_op jit(solution)/shard_map/ppermute | solution.py:317
  19.6 5.5 %collective-permute-start.1 = (f32[2,136,128]{2,1,0:T(8,128)S(1)}, f32[2,136,128]{2,1,0:T(8,128)S(1)}, u32[]{:S(2)}, u32[]{:S(2)}) collective-permute-start(f32[2,136,128]{2,1,0:T(8,128)S(1)} %pad_maximum_fusion.refs_0_), channel_id=1, source_target_pairs={{0,80},{64,0},{16,64},{80,16},{1,81},{65,1},{17,65},{81,17},{2,82}... | collective-permute-start | bytes 417800 | tf_op jit(solution)/shard_map/ppermute | solution.py:317
  68.2 51.2 %collective-permute-start.4 = (f32[8,256]{1,0:T(8,128)S(1)}, f32[8,256]{1,0:T(8,128)S(1)}, u32[]{:S(2)}, u32[]{:S(2)}) collective-permute-start(f32[8,256]{1,0:T(8,128)S(1)} %get-tuple-element.25), channel_id=1, source_target_pairs={{0,3},{1,2},{2,1},{3,0},{4,7},{5,6},{6,5},{7,4},{8,11},{9,10},{10,... | collective-permute-start | bytes 24584 | tf_op jit(solution)/shard_map/ppermute | solution.py:341
  114.4 12.0 %all-to-all-start.1 = ((f32[16,1,256]{2,1,0:T(1,128)}), f32[16,1,256]{2,1,0:T(1,128)S(1)}, u32[]{:S(2)}, u32[]{:S(2)}) async-start(f32[16,1,256]{2,1,0:T(1,128)} %get-tuple-element.22), calls=%async_computation.1 | async-start | bytes 32768 | tf_op jit(solution)/shard_map/all_to_all | solution.py:349
  119.4 3.7 %collective-permute-start.5 = (f32[8,256]{1,0:T(8,128)S(1)}, f32[8,256]{1,0:T(8,128)S(1)}, u32[]{:S(2)}, u32[]{:S(2)}) collective-permute-start(f32[8,256]{1,0:T(8,128)S(1)} %get-tuple-element.27), channel_id=1, source_target_pairs={{0,64},{64,0},{1,65},{65,1},{2,66},{66,2},{3,67},{67,3},{4,68},{68... | collective-permute-start | bytes 24584 | tf_op jit(solution)/shard_map/ppermute | solution.py:352
  123.2 4.9 %collective-permute-start.6 = (f32[2,256]{1,0:T(2,128)S(1)}, f32[2,256]{1,0:T(2,128)S(1)}, u32[]{:S(2)}, u32[]{:S(2)}) collective-permute-start(f32[2,256]{1,0:T(2,128)S(1)} %get-tuple-element.29), channel_id=1, source_target_pairs={{0,80},{16,64},{64,16},{80,0},{1,81},{17,65},{65,17},{81,1},{2,82}... | collective-permute-start | bytes 6152 | tf_op jit(solution)/shard_map/ppermute | solution.py:354

commit v9 on v7

--- a/solution.py
+++ b/solution.py
@@ -14,6 +14,7 @@
 LINE = ("grp_0", "mem_0")
 CORE = "grp_1"
 SIDE = 4
+LINES = 8
 
 epsilon = 4.0
 LOG2E = 1.4426950408889634
@@ -126,39 +127,27 @@
     return jnp.where((v > low) & (v < high), 0.0, 1.0)
 
 
-def half_kernel(nrow, ncol, last, *refs):
-    blocks = blocks_of(refs[:nrow_refs(last)])
-    refs = refs[nrow_refs(last) :]
-    if last:
-        cols, xt, stats, yk, former, lines, out, own, rowacc, colacc, rmax, rsum, rlog = refs
-        most = former[1:2, 0:BLK]
-    else:
-        cols, xt, stats, yk, former, lines, rowacc, colacc, rmax, rsum, rlog = refs
-
-        most = jnp.zeros((1, BLK), jnp.float32)
-        masses = jnp.zeros((8, 128), jnp.float32)
+def tile_kernel(nrow, ncol, *refs):
+    blocks = blocks_of(refs[: SIDE + 1])
+    cols, xt, stats, lines, cross, out, own, rowacc, colacc, rmax, rsum, rlog = refs[SIDE + 1 :]
+    most = jnp.zeros((1, BLK), jnp.float32)
+    masses = jnp.zeros((8, 128), jnp.float32)
     step = 512
-    first = 0 if last else nrow * BLK
 
     for j in range(ncol):
         at = slice(j * BLK, (j + 1) * BLK)
-        if last:
-            right = yk[:, at]
-        else:
-            block = cols.at[j]
-            pts, sq, term = unpacked(block)
-            y1, y2 = split(pts)
-            bias = bias_lines((term - sq / epsilon) * LOG2E, 3).astype(jnp.bfloat16)
-            y1 = y1.astype(jnp.bfloat16)
-            right = jnp.concatenate([y1, y1, y2.astype(jnp.bfloat16), bias, jnp.zeros((48, BLK), jnp.bfloat16)], 0)
-            yk[:, at] = right
-            most = jnp.maximum(most, sq)
-            masses = masses + jnp.exp(block[128:136, :])
+        block = cols.at[j]
+        pts, sq, term = unpacked(block)
+        y1, y2 = split(pts)
+        bias = bias_lines((term - sq / epsilon) * LOG2E, 3).astype(jnp.bfloat16)
+        y1 = y1.astype(jnp.bfloat16)
+        right = jnp.concatenate([y1, y1, y2.astype(jnp.bfloat16), bias, jnp.zeros((48, BLK), jnp.bfloat16)], 0)
+        most = jnp.maximum(most, sq)
+        masses = masses + jnp.exp(block[128:136, :])
         total = jnp.zeros((8, BLK), jnp.float32)
         for i in range(nrow * BLK // step):
             rows = slice(i * step, (i + 1) * step)
-            held = slice(first + i * step, first + (i + 1) * step)
-            e = jnp.exp2(jnp.dot(xt[held, :], right, preferred_element_type=jnp.float32))
+            e = jnp.exp2(jnp.dot(xt[rows, :], right, preferred_element_type=jnp.float32))
             part = e[:, :128] + e[:, 128:]
             rowacc[rows, :] = part if j == 0 else rowacc[rows, :] + part
             total += jnp.sum(e.reshape(step // 8, 8, BLK), 0)
@@ -223,32 +212,22 @@
 
         lax.fori_loop(0, ncol, finish, 0)
 
-    for k in range(nrow):
-        lines[k : k + 1, :] = rlog[:, k * BLK : (k + 1) * BLK]
-    if last:
-        lines[4:5, :] = former[1:2, BLK : 2 * BLK]
-        both = both_logs(colacc[0:1, :], former[0:1, :])
-        for j in range(ncol):
-            out[j] = both[:, j * BLK : (j + 1) * BLK]
-        at_plane = lax.axis_index("mem_1") * SIDE + lax.axis_index("mem_2")
-        own[0:1, :] = wide(blocks[0], 128)
-        own[1:2, :] = wide(blocks[0], 132)
-        own[2:3, :] = wide(cols.at[at_plane], 128)
-        own[3:4, :] = wide(cols.at[at_plane], 132)
-    else:
-        target_mass = jnp.sum(masses[2:4, :], keepdims=True)
-        source_mass = jnp.sum(masses[6:8, :], keepdims=True)
-        mass = jnp.concatenate(
-            [jnp.broadcast_to(source_mass, (1, 128)), jnp.broadcast_to(target_mass, (1, 128))], 1
-        )
-        lines[4:5, :] = mass
-        former[0:1, :] = colacc[0:1, :]
-        former[1:2, 0:BLK] = most
-        former[1:2, BLK : 2 * BLK] = mass
-
-
-def nrow_refs(last):
-    return SIDE if last else 1
+    target_mass = jnp.sum(masses[2:4, :], keepdims=True)
+    source_mass = jnp.sum(masses[6:8, :], keepdims=True)
+    mass = jnp.concatenate(
+        [jnp.broadcast_to(source_mass, (1, 128)), jnp.broadcast_to(target_mass, (1, 128))], 1
+    )
+    for to, base in ((lines, 0), (cross, SIDE)):
+        for k in range(SIDE):
+            to[k : k + 1, :] = rlog[:, (base + k) * BLK : (base + k + 1) * BLK]
+        to[4:5, :] = mass
+    for j in range(ncol):
+        out[j] = colacc[0:1, j * BLK : (j + 1) * BLK]
+    at_plane = lax.axis_index("mem_1") * SIDE + lax.axis_index("mem_2")
+    own[0:1, :] = wide(blocks[0], 128)
+    own[1:2, :] = wide(blocks[0], 132)
+    own[2:3, :] = wide(cols.at[at_plane], 128)
+    own[3:4, :] = wide(cols.at[at_plane], 132)
 
 
 def both_logs(a, b):
@@ -318,12 +297,11 @@
         mine.append(lax.ppermute(rows, LINE, along(-k)))
     others = lax.ppermute(jnp.stack(mine), CORE, [(0, 1), (1, 0)])
     cols = lax.all_to_all(copies, PLANE, 0, 0, tiled=True)
-    nrow = nrow // 2
     size = nrow * ncol * BLK * BLK
     cost = pl.CostEstimate(flops=512 * size, bytes_accessed=4 * 2**20, transcendentals=size)
     xt, stats = call(
         rows_kernel,
-        (jax.ShapeDtypeStruct((2 * nrow * BLK, 256), jnp.bfloat16), f32(1, BLK)),
+        (jax.ShapeDtypeStruct((nrow * BLK, 256), jnp.bfloat16), f32(1, BLK)),
         5,
         cost=pl.CostEstimate(flops=10**6, bytes_accessed=10**6, transcendentals=0),
     )(*mine, others)
@@ -334,21 +312,14 @@
         pltpu.VMEM((BLK, 128), jnp.float32),
         pltpu.VMEM((1, nrow * BLK), jnp.float32),
     ]
-    yk, former, lines = call(
-        functools.partial(half_kernel, nrow, ncol, False),
-        (jax.ShapeDtypeStruct((256, ncol * BLK), jnp.bfloat16), f32(2, ncol * BLK), f32(8, BLK)),
-        4,
+    lines, cross, out, own = call(
+        functools.partial(tile_kernel, nrow, ncol),
+        (f32(LINES, BLK), f32(LINES, BLK), f32(ncol, 1, BLK), f32(8, BLK)),
+        SIDE + 4,
         scratch=scratch,
         cost=cost,
-    )(others, cols, xt, stats)
-    crossed = lax.ppermute(lines, CORE, [(0, 1), (1, 0)])
-    lines, out, own = call(
-        functools.partial(half_kernel, nrow, ncol, True),
-        (f32(8, BLK), f32(ncol, 1, BLK), f32(8, BLK)),
-        SIDE + 5,
-        scratch=scratch,
-        cost=cost,
-    )(*mine, cols, xt, stats, yk, former)
+    )(*mine, others, cols, xt, stats)
+    crossed = lax.ppermute(cross, CORE, [(0, 1), (1, 0)])
     got = lax.all_to_all(out, PLANE, 0, 0, tiled=True)
     small = pl.CostEstimate(flops=10**5, bytes_accessed=10**5, transcendentals=0)
     keep, send = call(first_kernel, (f32(8, BLK), f32(8, BLK)), 2, cost=small)(lines, crossed)

time: 128 us -> 127 us (level)
    pallas_call x3 -> x2, Pallas kernels: 85.8 us -> 85 us  [the longest x1 84.6 us: local(): call(functools.partial(tile_kernel, nrow, ncol), (f32(LINES, BLK), f32(LI...]
  transfers between devices with their start and end apart: 9 -> 9, of which waited for: 7 -> 7; matrix products, arithmetic and copies ran while one was open for 0% -> 0% of each run, Pallas kernels for 34% -> 0%
where the time goes in v9:
time: 127 us
  Pallas kernels  87.7 us (69%)
  starting transfers between devices  26.3 us (21%)
  waiting for transfers between devices  12.1 us (10%)
    pallas_call x1, Pallas kernels, local(): call(functools.partial(tile_kernel, nrow, ncol), (f32(LINES, BLK), f32(LI...  84.6 us
    all_to_all x1, starting transfers between devices, local(): cols = lax.all_to_all(copies, PLANE, 0, 0, tiled=True)  7.49 us
    ppermute x3, starting transfers between devices, local(): mine.append(lax.ppermute(rows, LINE, along(-k)))  6.51 us
    all_to_all x1, starting transfers between devices, local(): got = lax.all_to_all(out, PLANE, 0, 0, tiled=True)  6.11 us
    ppermute x1, starting transfers between devices, local(): send = lax.ppermute(send, LINE, [(i, SIDE - 1 - i) for i in range(SIDE)])  4.11 us
    all_to_all x1, waiting for transfers between devices, local(): cols = lax.all_to_all(copies, PLANE, 0, 0, tiled=True)  3.9 us
    ppermute x3, waiting for transfers between devices, local(): mine.append(lax.ppermute(rows, LINE, along(-k)))  3.3 us
  transfers between devices with their start and end apart: 9, of which 7 were waited for; matrix products, arithmetic and copies ran while one was open for 0% of the time, Pallas kernels for 0%

profile of v9, /device:TPU:2, one launch (start us, length us, event | category | flops | bytes accessed | tf_op | source)
XLA Modules:
  0.0 126.7 jit_solution(16190987152706742717)
XLA Ops:
  0.6 2.0 %shard_map.77 = (f32[136,128]{1,0:T(8,128)S(1)}, f32[16,136,128]{2,1,0:T(8,128)}) custom-call(f32[64,256]{1,0:T(8,128)} %spts.1, f32[64,256]{1,0:T(8,128)} %tpts.1, f32[2,128]{1,0:T(2,128)} %bitcast.12, f32[2,128]{1,0:T(2,128)} %bitcast.13, f32[2,128]{1,0:T(2,128)} %bitcast.14, f32[2,128]{1,0:T(2,128)} %bitcast.15), custom_call_target="tpu_custom_call" | custom-call | tf_op jit(solution)/shard_map/pallas_call | solution.py:283
  2.6 7.5 %all-to-all-start = ((f32[16,136,128]{2,1,0:T(8,128)}), f32[16,136,128]{2,1,0:T(8,128)S(1)}, u32[]{:S(2)}, u32[]{:S(2)}) async-start(f32[16,136,128]{2,1,0:T(8,128)} %get-tuple-element.15), calls=%async_computation | async-start | bytes 2228224 | tf_op jit(solution)/shard_map/all_to_all | solution.py:299
  10.1 1.9 %collective-permute-start.2 = (f32[136,128]{1,0:T(8,128)S(1)}, f32[136,128]{1,0:T(8,128)S(1)}, u32[]{:S(2)}, u32[]{:S(2)}) collective-permute-start(f32[136,128]{1,0:T(8,128)S(1)} %get-tuple-element.14.refs_0_), channel_id=1, source_target_pairs={{0,64},{64,16},{16,80},{80,0},{1,65},{65,17},{17,81},{81,1},{2,66}... | collective-permute-start | bytes 208904 | tf_op jit(solution)/shard_map/ppermute | solution.py:297
  12.1 3.6 %collective-permute-start.1 = (f32[136,128]{1,0:T(8,128)S(1)}, f32[136,128]{1,0:T(8,128)S(1)}, u32[]{:S(2)}, u32[]{:S(2)}) collective-permute-start(f32[136,128]{1,0:T(8,128)S(1)} %get-tuple-element.14.refs_0_), channel_id=1, source_target_pairs={{0,16},{64,80},{16,0},{80,64},{1,17},{65,81},{17,1},{81,65},{2,18}... | collective-permute-start | bytes 208904 | tf_op jit(solution)/shard_map/ppermute | solution.py:297
  15.6 1.0 collective-permute-start
  16.6 0.6 collective-permute-done.2.refs_3_
  17.2 1.5 %collective-permute-done.1.refs_2_ = f32[136,128]{1,0:T(8,128)S(1)} collective-permute-done((f32[136,128]{1,0:T(8,128)S(1)}, f32[136,128]{1,0:T(8,128)S(1)}, u32[]{:S(2)}, u32[]{:S(2)}) %collective-permute-start.1) | collective-permute-done | bytes 69664 | tf_op jit(solution)/shard_map/ppermute | solution.py:297
  18.7 1.3 %collective-permute-done.refs_1_ = f32[136,128]{1,0:T(8,128)S(1)} collective-permute-done((f32[136,128]{1,0:T(8,128)S(1)}, f32[136,128]{1,0:T(8,128)S(1)}, u32[]{:S(2)}, u32[]{:S(2)}) %collective-permute-start) | collective-permute-done | bytes 69664 | tf_op jit(solution)/shard_map/ppermute | solution.py:297
  20.0 0.1 collective-permute-start.3
  20.1 1.5 %collective-permute-done.3.refs_4_ = f32[4,136,128]{2,1,0:T(8,128)S(1)} collective-permute-done((f32[4,136,128]{2,1,0:T(8,128)S(1)}, f32[4,136,128]{2,1,0:T(8,128)S(1)}, u32[]{:S(2)}, u32[]{:S(2)}) %collective-permute-start.3) | collective-permute-done | bytes 278560 | tf_op jit(solution)/shard_map/ppermute | solution.py:298
  21.6 0.4 shard_map.78
  22.0 3.9 %all-to-all-done.refs_5_ = f32[16,136,128]{2,1,0:T(8,128)S(1)} async-done(((f32[16,136,128]{2,1,0:T(8,128)}), f32[16,136,128]{2,1,0:T(8,128)S(1)}, u32[]{:S(2)}, u32[]{:S(2)}) %all-to-all-start) | async-done | bytes 1114144 | tf_op jit(solution)/shard_map/all_to_all | solution.py:299
  25.9 84.6 %shard_map.79 = (f32[8,256]{1,0:T(8,128)S(1)}, f32[8,256]{1,0:T(8,128)S(1)}, f32[16,1,256]{2,1,0:T(1,128)}, f32[8,256]{1,0:T(8,128)S(1)}) custom-call(f32[136,128]{1,0:T(8,128)S(1)} %get-tuple-element.14.refs_0_, f32[136,128]{1,0:T(8,128)S(1)} %collective-permute-done.refs_1_, f32[136,128]{1,0:T(8,128)S(1)} %collective-permute-done.1.refs_2_, ...), custom_call_target="tpu_custom_call" | custom-call | flops 4294967296 | bytes 4194304 | tf_op jit(solution)/shard_map/pallas_call | solution.py:315
  110.5 0.0 collective-permute-start.4
  110.5 6.1 %all-to-all-start.1 = ((f32[16,1,256]{2,1,0:T(1,128)}), f32[16,1,256]{2,1,0:T(1,128)S(1)}, u32[]{:S(2)}, u32[]{:S(2)}) async-start(f32[16,1,256]{2,1,0:T(1,128)} %get-tuple-element.18), calls=%async_computation.1 | async-start | bytes 32768 | tf_op jit(solution)/shard_map/all_to_all | solution.py:323
  116.7 0.0 collective-permute-done.4.other
  116.7 2.0 %collective-permute-start.5 = (f32[8,256]{1,0:T(8,128)S(1)}, f32[8,256]{1,0:T(8,128)S(1)}, u32[]{:S(2)}, u32[]{:S(2)}) collective-permute-start(f32[8,256]{1,0:T(8,128)S(1)} %get-tuple-element.23), channel_id=1, source_target_pairs={{0,64},{64,0},{1,65},{65,1},{2,66},{66,2},{3,67},{67,3},{4,68},{68... | collective-permute-start | bytes 24584 | tf_op jit(solution)/shard_map/ppermute | solution.py:326
  118.7 1.7 %collective-permute-done.5.got = f32[8,256]{1,0:T(8,128)S(1)} collective-permute-done((f32[8,256]{1,0:T(8,128)S(1)}, f32[8,256]{1,0:T(8,128)S(1)}, u32[]{:S(2)}, u32[]{:S(2)}) %collective-permute-start.5) | collective-permute-done | bytes 8224 | tf_op jit(solution)/shard_map/ppermute | solution.py:326
  120.4 4.1 %collective-permute-start.6 = (f32[2,256]{1,0:T(2,128)S(1)}, f32[2,256]{1,0:T(2,128)S(1)}, u32[]{:S(2)}, u32[]{:S(2)}) collective-permute-start(f32[2,256]{1,0:T(2,128)S(1)} %get-tuple-element.25), channel_id=1, source_target_pairs={{0,80},{16,64},{64,16},{80,0},{1,81},{17,65},{65,17},{81,1},{2,82}... | collective-permute-start | bytes 6152 | tf_op jit(solution)/shard_map/ppermute | solution.py:328
  124.6 0.0 all-to-all-done.1.got
  124.6 1.6 %collective-permute-done.6.refs_1_ = f32[2,256]{1,0:T(2,128)S(1)} collective-permute-done((f32[2,256]{1,0:T(2,128)S(1)}, f32[2,256]{1,0:T(2,128)S(1)}, u32[]{:S(2)}, u32[]{:S(2)}) %collective-permute-start.6) | collective-permute-done | bytes 2080 | tf_op jit(solution)/shard_map/ppermute | solution.py:328
  126.1 0.6 shard_map.82
  (3 shorter events, 0.1 us)
Async XLA Ops:
  2.6 23.3 %all-to-all-start = ((f32[16,136,128]{2,1,0:T(8,128)}), f32[16,136,128]{2,1,0:T(8,128)S(1)}, u32[]{:S(2)}, u32[]{:S(2)}) async-start(f32[16,136,128]{2,1,0:T(8,128)} %get-tuple-element.15), calls=%async_computation | async-start | bytes 2228224 | tf_op jit(solution)/shard_map/all_to_all | solution.py:299
  10.1 7.1 %collective-permute-start.2 = (f32[136,128]{1,0:T(8,128)S(1)}, f32[136,128]{1,0:T(8,128)S(1)}, u32[]{:S(2)}, u32[]{:S(2)}) collective-permute-start(f32[136,128]{1,0:T(8,128)S(1)} %get-tuple-element.14.refs_0_), channel_id=1, source_target_pairs={{0,64},{64,16},{16,80},{80,0},{1,65},{65,17},{17,81},{81,1},{2,66}... | collective-permute-start | bytes 208904 | tf_op jit(solution)/shard_map/ppermute | solution.py:297
  12.1 6.6 %collective-permute-start.1 = (f32[136,128]{1,0:T(8,128)S(1)}, f32[136,128]{1,0:T(8,128)S(1)}, u32[]{:S(2)}, u32[]{:S(2)}) collective-permute-start(f32[136,128]{1,0:T(8,128)S(1)} %get-tuple-element.14.refs_0_), channel_id=1, source_target_pairs={{0,16},{64,80},{16,0},{80,64},{1,17},{65,81},{17,1},{81,65},{2,18}... | collective-permute-start | bytes 208904 | tf_op jit(solution)/shard_map/ppermute | solution.py:297
  15.6 4.3 %collective-permute-start = (f32[136,128]{1,0:T(8,128)S(1)}, f32[136,128]{1,0:T(8,128)S(1)}, u32[]{:S(2)}, u32[]{:S(2)}) collective-permute-start(f32[136,128]{1,0:T(8,128)S(1)} %get-tuple-element.14.refs_0_), channel_id=1, source_target_pairs={{0,80},{64,0},{16,64},{80,16},{1,81},{65,1},{17,65},{81,17},{2,82}... | collective-permute-start | bytes 208904 | tf_op jit(solution)/shard_map/ppermute | solution.py:297
  20.0 1.6 %collective-permute-start.3 = (f32[4,136,128]{2,1,0:T(8,128)S(1)}, f32[4,136,128]{2,1,0:T(8,128)S(1)}, u32[]{:S(2)}, u32[]{:S(2)}) collective-permute-start(f32[4,136,128]{2,1,0:T(8,128)S(1)} %pad_maximum_fusion), channel_id=1, source_target_pairs={{0,32},{32,0},{1,33},{33,1},{2,34},{34,2},{3,35},{35,3},{4,36},{36... | collective-permute-start | bytes 835592 | tf_op jit(solution)/shard_map/ppermute | solution.py:298
  110.5 6.1 %collective-permute-start.4 = (f32[8,256]{1,0:T(8,128)S(1)}, f32[8,256]{1,0:T(8,128)S(1)}, u32[]{:S(2)}, u32[]{:S(2)}) collective-permute-start(f32[8,256]{1,0:T(8,128)S(1)} %get-tuple-element.21), channel_id=1, source_target_pairs={{0,32},{32,0},{1,33},{33,1},{2,34},{34,2},{3,35},{35,3},{4,36},{36... | collective-permute-start | bytes 24584 | tf_op jit(solution)/shard_map/ppermute | solution.py:322
  110.5 14.0 %all-to-all-start.1 = ((f32[16,1,256]{2,1,0:T(1,128)}), f32[16,1,256]{2,1,0:T(1,128)S(1)}, u32[]{:S(2)}, u32[]{:S(2)}) async-start(f32[16,1,256]{2,1,0:T(1,128)} %get-tuple-element.18), calls=%async_computation.1 | async-start | bytes 32768 | tf_op jit(solution)/shard_map/all_to_all | solution.py:323
  116.7 3.7 %collective-permute-start.5 = (f32[8,256]{1,0:T(8,128)S(1)}, f32[8,256]{1,0:T(8,128)S(1)}, u32[]{:S(2)}, u32[]{:S(2)}) collective-permute-start(f32[8,256]{1,0:T(8,128)S(1)} %get-tuple-element.23), channel_id=1, source_target_pairs={{0,64},{64,0},{1,65},{65,1},{2,66},{66,2},{3,67},{67,3},{4,68},{68... | collective-permute-start | bytes 24584 | tf_op jit(solution)/shard_map/ppermute | solution.py:326
  120.4 5.7 %collective-permute-start.6 = (f32[2,256]{1,0:T(2,128)S(1)}, f32[2,256]{1,0:T(2,128)S(1)}, u32[]{:S(2)}, u32[]{:S(2)}) collective-permute-start(f32[2,256]{1,0:T(2,128)S(1)} %get-tuple-element.25), channel_id=1, source_target_pairs={{0,80},{16,64},{64,16},{80,0},{1,81},{17,65},{65,17},{81,1},{2,82}... | collective-permute-start | bytes 6152 | tf_op jit(solution)/shard_map/ppermute | solution.py:328

commit v10 on v9

--- a/solution.py
+++ b/solution.py
@@ -15,6 +15,7 @@
 CORE = "grp_1"
 SIDE = 4
 LINES = 8
+SENT = 8
 
 epsilon = 4.0
 LOG2E = 1.4426950408889634
@@ -132,7 +133,7 @@
     cols, xt, stats, lines, cross, out, own, rowacc, colacc, rmax, rsum, rlog = refs[SIDE + 1 :]
     most = jnp.zeros((1, BLK), jnp.float32)
     masses = jnp.zeros((8, 128), jnp.float32)
-    step = 512
+    step = 2048
 
     for j in range(ncol):
         at = slice(j * BLK, (j + 1) * BLK)
@@ -235,22 +236,12 @@
     return peak + jnp.log(jnp.exp(a - peak) + jnp.exp(b - peak))
 
 
-def first_kernel(mine, other, keep, send):
-    low = lax.axis_index("grp_0")
+def merge_kernel(mine, other, *outs):
     logs = both_logs(mine[0:4, :], other[0:4, :])
-    up, down = logs[1:2, :], logs[3:4, :]
-    send[0:1, :] = jnp.where(low == 0, up, down)
-    send[1:2, :] = logs[2:3, :]
-    keep[0:1, :] = logs[0:1, :]
-    keep[1:2, :] = jnp.where(low == 0, down, up)
-    send[2:3, :] = keep[2:3, :] = mine[4:5, :] + other[4:5, :]
-
-
-def second_kernel(kept, got, keep, send):
-    logs = both_logs(kept[0:2, :], got[0:2, :])
-    keep[0:1, :] = logs[0:1, :]
-    send[0:1, :] = logs[1:2, :]
-    send[1:2, :] = keep[1:2, :] = kept[2:3, :] + got[2:3, :]
+    mass = mine[4:5, :] + other[4:5, :]
+    for k, out in enumerate(outs):
+        out[0:1, :] = logs[k : k + 1, :]
+        out[1:2, :] = mass
 
 
 def finish_kernel(got, own, *refs):
@@ -322,11 +313,10 @@
     crossed = lax.ppermute(cross, CORE, [(0, 1), (1, 0)])
     got = lax.all_to_all(out, PLANE, 0, 0, tiled=True)
     small = pl.CostEstimate(flops=10**5, bytes_accessed=10**5, transcendentals=0)
-    keep, send = call(first_kernel, (f32(8, BLK), f32(8, BLK)), 2, cost=small)(lines, crossed)
-    send = lax.ppermute(send, LINE[0], [(0, 1), (1, 0)])
-    keep, send = call(second_kernel, (f32(2, BLK), f32(2, BLK)), 2, cost=small)(keep, send)
-    send = lax.ppermute(send, LINE, [(i, SIDE - 1 - i) for i in range(SIDE)])
-    return call(finish_kernel, (f32(BLK), f32(BLK)), 4)(got, own, keep, send)
+    parts = list(call(merge_kernel, (f32(SENT, BLK),) * SIDE, 2, cost=small)(lines, crossed))
+    for k in range(1, SIDE):
+        parts[k] = lax.ppermute(parts[k], LINE, along(k))
+    return call(finish_kernel, (f32(BLK), f32(BLK)), 2 + SIDE)(got, own, *parts)
 
 
 def solution(mesh):

time: 127 us -> 127 us (level)
    ppermute x2 -> x3, waiting for transfers between devices: 3.3 us -> 2.63 us  [local(): parts[k] = lax.ppermute(parts[k], LINE, along(k))]
    ppermute x2 -> x3, starting transfers between devices: 6.11 us -> 6.58 us  [local(): parts[k] = lax.ppermute(parts[k], LINE, along(k))]
  transfers between devices with their start and end apart: 9 -> 10, of which waited for: 7 -> 7; matrix products, arithmetic and copies ran while one was open for 0% -> 0% of each run, Pallas kernels for 0% -> 0%
where the time goes in v10:
time: 127 us; the launch traced here: 126 us
  Pallas kernels  87.6 us (69%)
  starting transfers between devices  26.8 us (21%)
  waiting for transfers between devices  11.4 us (9%)
    pallas_call x1, Pallas kernels, local(): call(functools.partial(tile_kernel, nrow, ncol), (f32(LINES, BLK), f32(LI...  84.5 us
    all_to_all x1, starting transfers between devices, local(): cols = lax.all_to_all(copies, PLANE, 0, 0, tiled=True)  7.49 us
    ppermute x3, starting transfers between devices, local(): parts[k] = lax.ppermute(parts[k], LINE, along(k))  6.58 us
    ppermute x3, starting transfers between devices, local(): mine.append(lax.ppermute(rows, LINE, along(-k)))  6.51 us
    all_to_all x1, starting transfers between devices, local(): got = lax.all_to_all(out, PLANE, 0, 0, tiled=True)  6.13 us
    all_to_all x1, waiting for transfers between devices, local(): cols = lax.all_to_all(copies, PLANE, 0, 0, tiled=True)  3.9 us
    ppermute x3, waiting for transfers between devices, local(): mine.append(lax.ppermute(rows, LINE, along(-k)))  3.3 us
    ppermute x3, waiting for transfers between devices, local(): parts[k] = lax.ppermute(parts[k], LINE, along(k))  2.63 us
  transfers between devices with their start and end apart: 10, of which 7 were waited for; matrix products, arithmetic and copies ran while one was open for 0% of the time, Pallas kernels for 0%

profile of v10, /device:TPU:2, one launch (start us, length us, event | category | flops | bytes accessed | tf_op | source)
XLA Modules:
  0.0 126.5 jit_solution(4480136132091429339)
XLA Ops:
  0.6 2.0 %shard_map.77 = (f32[136,128]{1,0:T(8,128)S(1)}, f32[16,136,128]{2,1,0:T(8,128)}) custom-call(f32[64,256]{1,0:T(8,128)} %spts.1, f32[64,256]{1,0:T(8,128)} %tpts.1, f32[2,128]{1,0:T(2,128)} %bitcast.12, f32[2,128]{1,0:T(2,128)} %bitcast.13, f32[2,128]{1,0:T(2,128)} %bitcast.14, f32[2,128]{1,0:T(2,128)} %bitcast.15), custom_call_target="tpu_custom_call" | custom-call | tf_op jit(solution)/shard_map/pallas_call | solution.py:274
  2.6 7.5 %all-to-all-start = ((f32[16,136,128]{2,1,0:T(8,128)}), f32[16,136,128]{2,1,0:T(8,128)S(1)}, u32[]{:S(2)}, u32[]{:S(2)}) async-start(f32[16,136,128]{2,1,0:T(8,128)} %get-tuple-element.15), calls=%async_computation | async-start | bytes 2228224 | tf_op jit(solution)/shard_map/all_to_all | solution.py:290
  10.1 1.9 %collective-permute-start.2 = (f32[136,128]{1,0:T(8,128)S(1)}, f32[136,128]{1,0:T(8,128)S(1)}, u32[]{:S(2)}, u32[]{:S(2)}) collective-permute-start(f32[136,128]{1,0:T(8,128)S(1)} %get-tuple-element.14.refs_0_), channel_id=1, source_target_pairs={{0,64},{64,16},{16,80},{80,0},{1,65},{65,17},{17,81},{81,1},{2,66}... | collective-permute-start | bytes 208904 | tf_op jit(solution)/shard_map/ppermute | solution.py:288
  12.1 3.6 %collective-permute-start.1 = (f32[136,128]{1,0:T(8,128)S(1)}, f32[136,128]{1,0:T(8,128)S(1)}, u32[]{:S(2)}, u32[]{:S(2)}) collective-permute-start(f32[136,128]{1,0:T(8,128)S(1)} %get-tuple-element.14.refs_0_), channel_id=1, source_target_pairs={{0,16},{64,80},{16,0},{80,64},{1,17},{65,81},{17,1},{81,65},{2,18}... | collective-permute-start | bytes 208904 | tf_op jit(solution)/shard_map/ppermute | solution.py:288
  15.6 1.0 collective-permute-start
  16.6 0.6 collective-permute-done.2.refs_3_
  17.2 1.5 %collective-permute-done.1.refs_2_ = f32[136,128]{1,0:T(8,128)S(1)} collective-permute-done((f32[136,128]{1,0:T(8,128)S(1)}, f32[136,128]{1,0:T(8,128)S(1)}, u32[]{:S(2)}, u32[]{:S(2)}) %collective-permute-start.1) | collective-permute-done | bytes 69664 | tf_op jit(solution)/shard_map/ppermute | solution.py:288
  18.7 1.3 %collective-permute-done.refs_1_ = f32[136,128]{1,0:T(8,128)S(1)} collective-permute-done((f32[136,128]{1,0:T(8,128)S(1)}, f32[136,128]{1,0:T(8,128)S(1)}, u32[]{:S(2)}, u32[]{:S(2)}) %collective-permute-start) | collective-permute-done | bytes 69664 | tf_op jit(solution)/shard_map/ppermute | solution.py:288
  20.0 0.1 collective-permute-start.3
  20.1 1.5 %collective-permute-done.3.refs_4_ = f32[4,136,128]{2,1,0:T(8,128)S(1)} collective-permute-done((f32[4,136,128]{2,1,0:T(8,128)S(1)}, f32[4,136,128]{2,1,0:T(8,128)S(1)}, u32[]{:S(2)}, u32[]{:S(2)}) %collective-permute-start.3) | collective-permute-done | bytes 278560 | tf_op jit(solution)/shard_map/ppermute | solution.py:289
  21.6 0.4 shard_map.78
  22.0 3.9 %all-to-all-done.refs_5_ = f32[16,136,128]{2,1,0:T(8,128)S(1)} async-done(((f32[16,136,128]{2,1,0:T(8,128)}), f32[16,136,128]{2,1,0:T(8,128)S(1)}, u32[]{:S(2)}, u32[]{:S(2)}) %all-to-all-start) | async-done | bytes 1114144 | tf_op jit(solution)/shard_map/all_to_all | solution.py:290
  25.9 84.5 %shard_map.79 = (f32[8,256]{1,0:T(8,128)S(1)}, f32[8,256]{1,0:T(8,128)S(1)}, f32[16,1,256]{2,1,0:T(1,128)}, f32[8,256]{1,0:T(8,128)S(1)}) custom-call(f32[136,128]{1,0:T(8,128)S(1)} %get-tuple-element.14.refs_0_, f32[136,128]{1,0:T(8,128)S(1)} %collective-permute-done.refs_1_, f32[136,128]{1,0:T(8,128)S(1)} %collective-permute-done.1.refs_2_, ...), custom_call_target="tpu_custom_call" | custom-call | flops 4294967296 | bytes 4194304 | tf_op jit(solution)/shard_map/pallas_call | solution.py:306
  110.5 0.0 collective-permute-start.4
  110.5 6.1 %all-to-all-start.1 = ((f32[16,1,256]{2,1,0:T(1,128)}), f32[16,1,256]{2,1,0:T(1,128)S(1)}, u32[]{:S(2)}, u32[]{:S(2)}) async-start(f32[16,1,256]{2,1,0:T(1,128)} %get-tuple-element.18), calls=%async_computation.1 | async-start | bytes 32768 | tf_op jit(solution)/shard_map/all_to_all | solution.py:314
  116.6 0.0 collective-permute-done.4.other
  116.6 2.0 %collective-permute-start.5 = (f32[8,256]{1,0:T(8,128)S(1)}, f32[8,256]{1,0:T(8,128)S(1)}, u32[]{:S(2)}, u32[]{:S(2)}) collective-permute-start(f32[8,256]{1,0:T(8,128)S(1)} %get-tuple-element.23), channel_id=1, source_target_pairs={{0,64},{64,16},{16,80},{80,0},{1,65},{65,17},{17,81},{81,1},{2,66}... | collective-permute-start | bytes 24584 | tf_op jit(solution)/shard_map/ppermute | solution.py:318
  118.6 3.6 %collective-permute-start.6 = (f32[8,256]{1,0:T(8,128)S(1)}, f32[8,256]{1,0:T(8,128)S(1)}, u32[]{:S(2)}, u32[]{:S(2)}) collective-permute-start(f32[8,256]{1,0:T(8,128)S(1)} %get-tuple-element.24), channel_id=1, source_target_pairs={{0,16},{64,80},{16,0},{80,64},{1,17},{65,81},{17,1},{81,65},{2,18}... | collective-permute-start | bytes 24584 | tf_op jit(solution)/shard_map/ppermute | solution.py:318
  122.2 1.0 collective-permute-start.7
  123.2 0.0 all-to-all-done.1.got
  123.2 0.0 collective-permute-done.5.refs_1_
  123.2 0.7 collective-permute-done.6.refs_2_
  123.9 1.9 %collective-permute-done.7.refs_3_ = f32[8,256]{1,0:T(8,128)S(1)} collective-permute-done((f32[8,256]{1,0:T(8,128)S(1)}, f32[8,256]{1,0:T(8,128)S(1)}, u32[]{:S(2)}, u32[]{:S(2)}) %collective-permute-start.7) | collective-permute-done | bytes 8224 | tf_op jit(solution)/shard_map/ppermute | solution.py:318
  125.8 0.6 shard_map.81
  (2 shorter events, 0.0 us)
Async XLA Ops:
  2.6 23.3 %all-to-all-start = ((f32[16,136,128]{2,1,0:T(8,128)}), f32[16,136,128]{2,1,0:T(8,128)S(1)}, u32[]{:S(2)}, u32[]{:S(2)}) async-start(f32[16,136,128]{2,1,0:T(8,128)} %get-tuple-element.15), calls=%async_computation | async-start | bytes 2228224 | tf_op jit(solution)/shard_map/all_to_all | solution.py:290
  10.1 7.1 %collective-permute-start.2 = (f32[136,128]{1,0:T(8,128)S(1)}, f32[136,128]{1,0:T(8,128)S(1)}, u32[]{:S(2)}, u32[]{:S(2)}) collective-permute-start(f32[136,128]{1,0:T(8,128)S(1)} %get-tuple-element.14.refs_0_), channel_id=1, source_target_pairs={{0,64},{64,16},{16,80},{80,0},{1,65},{65,17},{17,81},{81,1},{2,66}... | collective-permute-start | bytes 208904 | tf_op jit(solution)/shard_map/ppermute | solution.py:288
  12.1 6.6 %collective-permute-start.1 = (f32[136,128]{1,0:T(8,128)S(1)}, f32[136,128]{1,0:T(8,128)S(1)}, u32[]{:S(2)}, u32[]{:S(2)}) collective-permute-start(f32[136,128]{1,0:T(8,128)S(1)} %get-tuple-element.14.refs_0_), channel_id=1, source_target_pairs={{0,16},{64,80},{16,0},{80,64},{1,17},{65,81},{17,1},{81,65},{2,18}... | collective-permute-start | bytes 208904 | tf_op jit(solution)/shard_map/ppermute | solution.py:288
  15.6 4.3 %collective-permute-start = (f32[136,128]{1,0:T(8,128)S(1)}, f32[136,128]{1,0:T(8,128)S(1)}, u32[]{:S(2)}, u32[]{:S(2)}) collective-permute-start(f32[136,128]{1,0:T(8,128)S(1)} %get-tuple-element.14.refs_0_), channel_id=1, source_target_pairs={{0,80},{64,0},{16,64},{80,16},{1,81},{65,1},{17,65},{81,17},{2,82}... | collective-permute-start | bytes 208904 | tf_op jit(solution)/shard_map/ppermute | solution.py:288
  20.0 1.6 %collective-permute-start.3 = (f32[4,136,128]{2,1,0:T(8,128)S(1)}, f32[4,136,128]{2,1,0:T(8,128)S(1)}, u32[]{:S(2)}, u32[]{:S(2)}) collective-permute-start(f32[4,136,128]{2,1,0:T(8,128)S(1)} %pad_maximum_fusion), channel_id=1, source_target_pairs={{0,32},{32,0},{1,33},{33,1},{2,34},{34,2},{3,35},{35,3},{4,36},{36... | collective-permute-start | bytes 835592 | tf_op jit(solution)/shard_map/ppermute | solution.py:289
  110.5 6.1 %collective-permute-start.4 = (f32[8,256]{1,0:T(8,128)S(1)}, f32[8,256]{1,0:T(8,128)S(1)}, u32[]{:S(2)}, u32[]{:S(2)}) collective-permute-start(f32[8,256]{1,0:T(8,128)S(1)} %get-tuple-element.21), channel_id=1, source_target_pairs={{0,32},{32,0},{1,33},{33,1},{2,34},{34,2},{3,35},{35,3},{4,36},{36... | collective-permute-start | bytes 24584 | tf_op jit(solution)/shard_map/ppermute | solution.py:313
  110.5 12.7 %all-to-all-start.1 = ((f32[16,1,256]{2,1,0:T(1,128)}), f32[16,1,256]{2,1,0:T(1,128)S(1)}, u32[]{:S(2)}, u32[]{:S(2)}) async-start(f32[16,1,256]{2,1,0:T(1,128)} %get-tuple-element.18), calls=%async_computation.1 | async-start | bytes 32768 | tf_op jit(solution)/shard_map/all_to_all | solution.py:314
  116.6 6.6 %collective-permute-start.5 = (f32[8,256]{1,0:T(8,128)S(1)}, f32[8,256]{1,0:T(8,128)S(1)}, u32[]{:S(2)}, u32[]{:S(2)}) collective-permute-start(f32[8,256]{1,0:T(8,128)S(1)} %get-tuple-element.23), channel_id=1, source_target_pairs={{0,64},{64,16},{16,80},{80,0},{1,65},{65,17},{17,81},{81,1},{2,66}... | collective-permute-start | bytes 24584 | tf_op jit(solution)/shard_map/ppermute | solution.py:318
  118.6 5.3 %collective-permute-start.6 = (f32[8,256]{1,0:T(8,128)S(1)}, f32[8,256]{1,0:T(8,128)S(1)}, u32[]{:S(2)}, u32[]{:S(2)}) collective-permute-start(f32[8,256]{1,0:T(8,128)S(1)} %get-tuple-element.24), channel_id=1, source_target_pairs={{0,16},{64,80},{16,0},{80,64},{1,17},{65,81},{17,1},{81,65},{2,18}... | collective-permute-start | bytes 24584 | tf_op jit(solution)/shard_map/ppermute | solution.py:318
  122.2 3.7 %collective-permute-start.7 = (f32[8,256]{1,0:T(8,128)S(1)}, f32[8,256]{1,0:T(8,128)S(1)}, u32[]{:S(2)}, u32[]{:S(2)}) collective-permute-start(f32[8,256]{1,0:T(8,128)S(1)} %get-tuple-element.25), channel_id=1, source_target_pairs={{0,80},{64,0},{16,64},{80,16},{1,81},{65,1},{17,65},{81,17},{2,82}... | collective-permute-start | bytes 24584 | tf_op jit(solution)/shard_map/ppermute | solution.py:318

commit v11 on v10

--- a/solution.py
+++ b/solution.py
@@ -15,7 +15,7 @@
 CORE = "grp_1"
 SIDE = 4
 LINES = 8
-SENT = 8
+SENT = 2
 
 epsilon = 4.0
 LOG2E = 1.4426950408889634

time: 127 us -> 128 us (level)
  transfers between devices with their start and end apart: 10 -> 10, of which waited for: 7 -> 8; matrix products, arithmetic and copies ran while one was open for 0% -> 0% of each run, Pallas kernels for 0% -> 0%
where the time goes in v11:
time: 128 us
  Pallas kernels  87.6 us (68%)
  starting transfers between devices  26.8 us (21%)
  waiting for transfers between devices  12.5 us (10%)
    pallas_call x1, Pallas kernels, local(): call(functools.partial(tile_kernel, nrow, ncol), (f32(LINES, BLK), f32(LI...  84.5 us
    all_to_all x1, starting transfers between devices, local(): cols = lax.all_to_all(copies, PLANE, 0, 0, tiled=True)  7.49 us
    ppermute x3, starting transfers between devices, local(): parts[k] = lax.ppermute(parts[k], LINE, along(k))  6.58 us
    ppermute x3, starting transfers between devices, local(): mine.append(lax.ppermute(rows, LINE, along(-k)))  6.51 us
    all_to_all x1, starting transfers between devices, local(): got = lax.all_to_all(out, PLANE, 0, 0, tiled=True)  6.13 us
    all_to_all x1, waiting for transfers between devices, local(): cols = lax.all_to_all(copies, PLANE, 0, 0, tiled=True)  3.9 us
    ppermute x3, waiting for transfers between devices, local(): mine.append(lax.ppermute(rows, LINE, along(-k)))  3.3 us
    ppermute x3, waiting for transfers between devices, local(): parts[k] = lax.ppermute(parts[k], LINE, along(k))  2.57 us
  transfers between devices with their start and end apart: 10, of which 8 were waited for; matrix products, arithmetic and copies ran while one was open for 0% of the time, Pallas kernels for 0%

profile of v11, /device:TPU:2, one launch (start us, length us, event | category | flops | bytes accessed | tf_op | source)
XLA Modules:
  0.0 127.6 jit_solution(12815466304413464564)
XLA Ops:
  0.6 2.0 %shard_map.77 = (f32[136,128]{1,0:T(8,128)S(1)}, f32[16,136,128]{2,1,0:T(8,128)}) custom-call(f32[64,256]{1,0:T(8,128)} %spts.1, f32[64,256]{1,0:T(8,128)} %tpts.1, f32[2,128]{1,0:T(2,128)} %bitcast.12, f32[2,128]{1,0:T(2,128)} %bitcast.13, f32[2,128]{1,0:T(2,128)} %bitcast.14, f32[2,128]{1,0:T(2,128)} %bitcast.15), custom_call_target="tpu_custom_call" | custom-call | tf_op jit(solution)/shard_map/pallas_call | solution.py:274
  2.6 7.5 %all-to-all-start = ((f32[16,136,128]{2,1,0:T(8,128)}), f32[16,136,128]{2,1,0:T(8,128)S(1)}, u32[]{:S(2)}, u32[]{:S(2)}) async-start(f32[16,136,128]{2,1,0:T(8,128)} %get-tuple-element.15), calls=%async_computation | async-start | bytes 2228224 | tf_op jit(solution)/shard_map/all_to_all | solution.py:290
  10.1 1.9 %collective-permute-start.2 = (f32[136,128]{1,0:T(8,128)S(1)}, f32[136,128]{1,0:T(8,128)S(1)}, u32[]{:S(2)}, u32[]{:S(2)}) collective-permute-start(f32[136,128]{1,0:T(8,128)S(1)} %get-tuple-element.14.refs_0_), channel_id=1, source_target_pairs={{0,64},{64,16},{16,80},{80,0},{1,65},{65,17},{17,81},{81,1},{2,66}... | collective-permute-start | bytes 208904 | tf_op jit(solution)/shard_map/ppermute | solution.py:288
  12.1 3.6 %collective-permute-start.1 = (f32[136,128]{1,0:T(8,128)S(1)}, f32[136,128]{1,0:T(8,128)S(1)}, u32[]{:S(2)}, u32[]{:S(2)}) collective-permute-start(f32[136,128]{1,0:T(8,128)S(1)} %get-tuple-element.14.refs_0_), channel_id=1, source_target_pairs={{0,16},{64,80},{16,0},{80,64},{1,17},{65,81},{17,1},{81,65},{2,18}... | collective-permute-start | bytes 208904 | tf_op jit(solution)/shard_map/ppermute | solution.py:288
  15.6 1.0 collective-permute-start
  16.6 0.6 collective-permute-done.2.refs_3_
  17.2 1.5 %collective-permute-done.1.refs_2_ = f32[136,128]{1,0:T(8,128)S(1)} collective-permute-done((f32[136,128]{1,0:T(8,128)S(1)}, f32[136,128]{1,0:T(8,128)S(1)}, u32[]{:S(2)}, u32[]{:S(2)}) %collective-permute-start.1) | collective-permute-done | bytes 69664 | tf_op jit(solution)/shard_map/ppermute | solution.py:288
  18.7 1.3 %collective-permute-done.refs_1_ = f32[136,128]{1,0:T(8,128)S(1)} collective-permute-done((f32[136,128]{1,0:T(8,128)S(1)}, f32[136,128]{1,0:T(8,128)S(1)}, u32[]{:S(2)}, u32[]{:S(2)}) %collective-permute-start) | collective-permute-done | bytes 69664 | tf_op jit(solution)/shard_map/ppermute | solution.py:288
  20.0 0.1 collective-permute-start.3
  20.1 1.5 %collective-permute-done.3.refs_4_ = f32[4,136,128]{2,1,0:T(8,128)S(1)} collective-permute-done((f32[4,136,128]{2,1,0:T(8,128)S(1)}, f32[4,136,128]{2,1,0:T(8,128)S(1)}, u32[]{:S(2)}, u32[]{:S(2)}) %collective-permute-start.3) | collective-permute-done | bytes 278560 | tf_op jit(solution)/shard_map/ppermute | solution.py:289
  21.6 0.4 shard_map.78
  22.0 3.9 %all-to-all-done.refs_5_ = f32[16,136,128]{2,1,0:T(8,128)S(1)} async-done(((f32[16,136,128]{2,1,0:T(8,128)}), f32[16,136,128]{2,1,0:T(8,128)S(1)}, u32[]{:S(2)}, u32[]{:S(2)}) %all-to-all-start) | async-done | bytes 1114144 | tf_op jit(solution)/shard_map/all_to_all | solution.py:290
  25.9 84.5 %shard_map.79 = (f32[8,256]{1,0:T(8,128)S(1)}, f32[8,256]{1,0:T(8,128)S(1)}, f32[16,1,256]{2,1,0:T(1,128)}, f32[8,256]{1,0:T(8,128)S(1)}) custom-call(f32[136,128]{1,0:T(8,128)S(1)} %get-tuple-element.14.refs_0_, f32[136,128]{1,0:T(8,128)S(1)} %collective-permute-done.refs_1_, f32[136,128]{1,0:T(8,128)S(1)} %collective-permute-done.1.refs_2_, ...), custom_call_target="tpu_custom_call" | custom-call | flops 4294967296 | bytes 4194304 | tf_op jit(solution)/shard_map/pallas_call | solution.py:306
  110.5 6.1 %all-to-all-start.1 = ((f32[16,1,256]{2,1,0:T(1,128)}), f32[16,1,256]{2,1,0:T(1,128)S(1)}, u32[]{:S(2)}, u32[]{:S(2)}) async-start(f32[16,1,256]{2,1,0:T(1,128)} %get-tuple-element.18), calls=%async_computation.1 | async-start | bytes 32768 | tf_op jit(solution)/shard_map/all_to_all | solution.py:314
  116.6 0.0 collective-permute-start.4
  116.6 1.2 collective-permute-done.4.other
  117.8 2.0 %collective-permute-start.5 = (f32[2,256]{1,0:T(2,128)S(1)}, f32[2,256]{1,0:T(2,128)S(1)}, u32[]{:S(2)}, u32[]{:S(2)}) collective-permute-start(f32[2,256]{1,0:T(2,128)S(1)} %get-tuple-element.23), channel_id=1, source_target_pairs={{0,64},{64,16},{16,80},{80,0},{1,65},{65,17},{17,81},{81,1},{2,66}... | collective-permute-start | bytes 6152 | tf_op jit(solution)/shard_map/ppermute | solution.py:318
  119.7 3.6 %collective-permute-start.6 = (f32[2,256]{1,0:T(2,128)S(1)}, f32[2,256]{1,0:T(2,128)S(1)}, u32[]{:S(2)}, u32[]{:S(2)}) collective-permute-start(f32[2,256]{1,0:T(2,128)S(1)} %get-tuple-element.24), channel_id=1, source_target_pairs={{0,16},{64,80},{16,0},{80,64},{1,17},{65,81},{17,1},{81,65},{2,18}... | collective-permute-start | bytes 6152 | tf_op jit(solution)/shard_map/ppermute | solution.py:318
  123.3 1.0 collective-permute-start.7
  124.4 0.0 collective-permute-done.5.refs_1_
  124.4 0.6 collective-permute-done.6.refs_2_
  124.9 2.0 %collective-permute-done.7.refs_3_ = f32[2,256]{1,0:T(2,128)S(1)} collective-permute-done((f32[2,256]{1,0:T(2,128)S(1)}, f32[2,256]{1,0:T(2,128)S(1)}, u32[]{:S(2)}, u32[]{:S(2)}) %collective-permute-start.7) | collective-permute-done | bytes 2080 | tf_op jit(solution)/shard_map/ppermute | solution.py:318
  126.9 0.0 all-to-all-done.1.got
  126.9 0.6 shard_map.81
  (2 shorter events, 0.0 us)
Async XLA Ops:
  2.6 23.3 %all-to-all-start = ((f32[16,136,128]{2,1,0:T(8,128)}), f32[16,136,128]{2,1,0:T(8,128)S(1)}, u32[]{:S(2)}, u32[]{:S(2)}) async-start(f32[16,136,128]{2,1,0:T(8,128)} %get-tuple-element.15), calls=%async_computation | async-start | bytes 2228224 | tf_op jit(solution)/shard_map/all_to_all | solution.py:290
  10.1 7.1 %collective-permute-start.2 = (f32[136,128]{1,0:T(8,128)S(1)}, f32[136,128]{1,0:T(8,128)S(1)}, u32[]{:S(2)}, u32[]{:S(2)}) collective-permute-start(f32[136,128]{1,0:T(8,128)S(1)} %get-tuple-element.14.refs_0_), channel_id=1, source_target_pairs={{0,64},{64,16},{16,80},{80,0},{1,65},{65,17},{17,81},{81,1},{2,66}... | collective-permute-start | bytes 208904 | tf_op jit(solution)/shard_map/ppermute | solution.py:288
  12.1 6.6 %collective-permute-start.1 = (f32[136,128]{1,0:T(8,128)S(1)}, f32[136,128]{1,0:T(8,128)S(1)}, u32[]{:S(2)}, u32[]{:S(2)}) collective-permute-start(f32[136,128]{1,0:T(8,128)S(1)} %get-tuple-element.14.refs_0_), channel_id=1, source_target_pairs={{0,16},{64,80},{16,0},{80,64},{1,17},{65,81},{17,1},{81,65},{2,18}... | collective-permute-start | bytes 208904 | tf_op jit(solution)/shard_map/ppermute | solution.py:288
  15.6 4.3 %collective-permute-start = (f32[136,128]{1,0:T(8,128)S(1)}, f32[136,128]{1,0:T(8,128)S(1)}, u32[]{:S(2)}, u32[]{:S(2)}) collective-permute-start(f32[136,128]{1,0:T(8,128)S(1)} %get-tuple-element.14.refs_0_), channel_id=1, source_target_pairs={{0,80},{64,0},{16,64},{80,16},{1,81},{65,1},{17,65},{81,17},{2,82}... | collective-permute-start | bytes 208904 | tf_op jit(solution)/shard_map/ppermute | solution.py:288
  20.0 1.6 %collective-permute-start.3 = (f32[4,136,128]{2,1,0:T(8,128)S(1)}, f32[4,136,128]{2,1,0:T(8,128)S(1)}, u32[]{:S(2)}, u32[]{:S(2)}) collective-permute-start(f32[4,136,128]{2,1,0:T(8,128)S(1)} %pad_maximum_fusion), channel_id=1, source_target_pairs={{0,32},{32,0},{1,33},{33,1},{2,34},{34,2},{3,35},{35,3},{4,36},{36... | collective-permute-start | bytes 835592 | tf_op jit(solution)/shard_map/ppermute | solution.py:289
  110.5 16.5 %all-to-all-start.1 = ((f32[16,1,256]{2,1,0:T(1,128)}), f32[16,1,256]{2,1,0:T(1,128)S(1)}, u32[]{:S(2)}, u32[]{:S(2)}) async-start(f32[16,1,256]{2,1,0:T(1,128)} %get-tuple-element.18), calls=%async_computation.1 | async-start | bytes 32768 | tf_op jit(solution)/shard_map/all_to_all | solution.py:314
  116.6 1.2 collective-permute-start.4
  117.8 6.6 %collective-permute-start.5 = (f32[2,256]{1,0:T(2,128)S(1)}, f32[2,256]{1,0:T(2,128)S(1)}, u32[]{:S(2)}, u32[]{:S(2)}) collective-permute-start(f32[2,256]{1,0:T(2,128)S(1)} %get-tuple-element.23), channel_id=1, source_target_pairs={{0,64},{64,16},{16,80},{80,0},{1,65},{65,17},{17,81},{81,1},{2,66}... | collective-permute-start | bytes 6152 | tf_op jit(solution)/shard_map/ppermute | solution.py:318
  119.7 5.2 %collective-permute-start.6 = (f32[2,256]{1,0:T(2,128)S(1)}, f32[2,256]{1,0:T(2,128)S(1)}, u32[]{:S(2)}, u32[]{:S(2)}) collective-permute-start(f32[2,256]{1,0:T(2,128)S(1)} %get-tuple-element.24), channel_id=1, source_target_pairs={{0,16},{64,80},{16,0},{80,64},{1,17},{65,81},{17,1},{81,65},{2,18}... | collective-permute-start | bytes 6152 | tf_op jit(solution)/shard_map/ppermute | solution.py:318
  123.3 3.6 %collective-permute-start.7 = (f32[2,256]{1,0:T(2,128)S(1)}, f32[2,256]{1,0:T(2,128)S(1)}, u32[]{:S(2)}, u32[]{:S(2)}) collective-permute-start(f32[2,256]{1,0:T(2,128)S(1)} %get-tuple-element.25), channel_id=1, source_target_pairs={{0,80},{64,0},{16,64},{80,16},{1,81},{65,1},{17,65},{81,17},{2,82}... | collective-permute-start | bytes 6152 | tf_op jit(solution)/shard_map/ppermute | solution.py:318

commit v12 on v10

--- a/solution.py
+++ b/solution.py
@@ -314,7 +314,7 @@
     got = lax.all_to_all(out, PLANE, 0, 0, tiled=True)
     small = pl.CostEstimate(flops=10**5, bytes_accessed=10**5, transcendentals=0)
     parts = list(call(merge_kernel, (f32(SENT, BLK),) * SIDE, 2, cost=small)(lines, crossed))
-    for k in range(1, SIDE):
+    for k in (2, 1, 3):
         parts[k] = lax.ppermute(parts[k], LINE, along(k))
     return call(finish_kernel, (f32(BLK), f32(BLK)), 2 + SIDE)(got, own, *parts)
 

time: 127 us -> 127 us (level)
  no operation moved by 1% of the time
where the time goes in v12:
time: 127 us; the launch traced here: 126 us
  Pallas kernels  87.6 us (69%)
  starting transfers between devices  26.8 us (21%)
  waiting for transfers between devices  11.4 us (9%)
    pallas_call x1, Pallas kernels, local(): call(functools.partial(tile_kernel, nrow, ncol), (f32(LINES, BLK), f32(LI...  84.5 us
    all_to_all x1, starting transfers between devices, local(): cols = lax.all_to_all(copies, PLANE, 0, 0, tiled=True)  7.49 us
    ppermute x3, starting transfers between devices, local(): parts[k] = lax.ppermute(parts[k], LINE, along(k))  6.58 us
    ppermute x3, starting transfers between devices, local(): mine.append(lax.ppermute(rows, LINE, along(-k)))  6.51 us
    all_to_all x1, starting transfers between devices, local(): got = lax.all_to_all(out, PLANE, 0, 0, tiled=True)  6.13 us
    all_to_all x1, waiting for transfers between devices, local(): cols = lax.all_to_all(copies, PLANE, 0, 0, tiled=True)  3.9 us
    ppermute x3, waiting for transfers between devices, local(): mine.append(lax.ppermute(rows, LINE, along(-k)))  3.3 us
    ppermute x3, waiting for transfers between devices, local(): parts[k] = lax.ppermute(parts[k], LINE, along(k))  2.63 us
  transfers between devices with their start and end apart: 10, of which 7 were waited for; matrix products, arithmetic and copies ran while one was open for 0% of the time, Pallas kernels for 0%

profile of v12, /device:TPU:2, one launch (start us, length us, event | category | flops | bytes accessed | tf_op | source)
XLA Modules:
  0.0 126.5 jit_solution(4480136132091429339)
XLA Ops:
  0.6 2.0 %shard_map.77 = (f32[136,128]{1,0:T(8,128)S(1)}, f32[16,136,128]{2,1,0:T(8,128)}) custom-call(f32[64,256]{1,0:T(8,128)} %spts.1, f32[64,256]{1,0:T(8,128)} %tpts.1, f32[2,128]{1,0:T(2,128)} %bitcast.12, f32[2,128]{1,0:T(2,128)} %bitcast.13, f32[2,128]{1,0:T(2,128)} %bitcast.14, f32[2,128]{1,0:T(2,128)} %bitcast.15), custom_call_target="tpu_custom_call" | custom-call | tf_op jit(solution)/shard_map/pallas_call | solution.py:274
  2.6 7.5 %all-to-all-start = ((f32[16,136,128]{2,1,0:T(8,128)}), f32[16,136,128]{2,1,0:T(8,128)S(1)}, u32[]{:S(2)}, u32[]{:S(2)}) async-start(f32[16,136,128]{2,1,0:T(8,128)} %get-tuple-element.15), calls=%async_computation | async-start | bytes 2228224 | tf_op jit(solution)/shard_map/all_to_all | solution.py:290
  10.1 1.9 %collective-permute-start.2 = (f32[136,128]{1,0:T(8,128)S(1)}, f32[136,128]{1,0:T(8,128)S(1)}, u32[]{:S(2)}, u32[]{:S(2)}) collective-permute-start(f32[136,128]{1,0:T(8,128)S(1)} %get-tuple-element.14.refs_0_), channel_id=1, source_target_pairs={{0,64},{64,16},{16,80},{80,0},{1,65},{65,17},{17,81},{81,1},{2,66}... | collective-permute-start | bytes 208904 | tf_op jit(solution)/shard_map/ppermute | solution.py:288
  12.1 3.6 %collective-permute-start.1 = (f32[136,128]{1,0:T(8,128)S(1)}, f32[136,128]{1,0:T(8,128)S(1)}, u32[]{:S(2)}, u32[]{:S(2)}) collective-permute-start(f32[136,128]{1,0:T(8,128)S(1)} %get-tuple-element.14.refs_0_), channel_id=1, source_target_pairs={{0,16},{64,80},{16,0},{80,64},{1,17},{65,81},{17,1},{81,65},{2,18}... | collective-permute-start | bytes 208904 | tf_op jit(solution)/shard_map/ppermute | solution.py:288
  15.6 1.0 collective-permute-start
  16.6 0.6 collective-permute-done.2.refs_3_
  17.2 1.5 %collective-permute-done.1.refs_2_ = f32[136,128]{1,0:T(8,128)S(1)} collective-permute-done((f32[136,128]{1,0:T(8,128)S(1)}, f32[136,128]{1,0:T(8,128)S(1)}, u32[]{:S(2)}, u32[]{:S(2)}) %collective-permute-start.1) | collective-permute-done | bytes 69664 | tf_op jit(solution)/shard_map/ppermute | solution.py:288
  18.7 1.3 %collective-permute-done.refs_1_ = f32[136,128]{1,0:T(8,128)S(1)} collective-permute-done((f32[136,128]{1,0:T(8,128)S(1)}, f32[136,128]{1,0:T(8,128)S(1)}, u32[]{:S(2)}, u32[]{:S(2)}) %collective-permute-start) | collective-permute-done | bytes 69664 | tf_op jit(solution)/shard_map/ppermute | solution.py:288
  20.0 0.1 collective-permute-start.3
  20.1 1.5 %collective-permute-done.3.refs_4_ = f32[4,136,128]{2,1,0:T(8,128)S(1)} collective-permute-done((f32[4,136,128]{2,1,0:T(8,128)S(1)}, f32[4,136,128]{2,1,0:T(8,128)S(1)}, u32[]{:S(2)}, u32[]{:S(2)}) %collective-permute-start.3) | collective-permute-done | bytes 278560 | tf_op jit(solution)/shard_map/ppermute | solution.py:289
  21.6 0.4 shard_map.78
  22.0 3.9 %all-to-all-done.refs_5_ = f32[16,136,128]{2,1,0:T(8,128)S(1)} async-done(((f32[16,136,128]{2,1,0:T(8,128)}), f32[16,136,128]{2,1,0:T(8,128)S(1)}, u32[]{:S(2)}, u32[]{:S(2)}) %all-to-all-start) | async-done | bytes 1114144 | tf_op jit(solution)/shard_map/all_to_all | solution.py:290
  25.9 84.5 %shard_map.79 = (f32[8,256]{1,0:T(8,128)S(1)}, f32[8,256]{1,0:T(8,128)S(1)}, f32[16,1,256]{2,1,0:T(1,128)}, f32[8,256]{1,0:T(8,128)S(1)}) custom-call(f32[136,128]{1,0:T(8,128)S(1)} %get-tuple-element.14.refs_0_, f32[136,128]{1,0:T(8,128)S(1)} %collective-permute-done.refs_1_, f32[136,128]{1,0:T(8,128)S(1)} %collective-permute-done.1.refs_2_, ...), custom_call_target="tpu_custom_call" | custom-call | flops 4294967296 | bytes 4194304 | tf_op jit(solution)/shard_map/pallas_call | solution.py:306
  110.5 0.0 collective-permute-start.4
  110.5 6.1 %all-to-all-start.1 = ((f32[16,1,256]{2,1,0:T(1,128)}), f32[16,1,256]{2,1,0:T(1,128)S(1)}, u32[]{:S(2)}, u32[]{:S(2)}) async-start(f32[16,1,256]{2,1,0:T(1,128)} %get-tuple-element.18), calls=%async_computation.1 | async-start | bytes 32768 | tf_op jit(solution)/shard_map/all_to_all | solution.py:314
  116.6 0.0 collective-permute-done.4.other
  116.6 2.0 %collective-permute-start.5 = (f32[8,256]{1,0:T(8,128)S(1)}, f32[8,256]{1,0:T(8,128)S(1)}, u32[]{:S(2)}, u32[]{:S(2)}) collective-permute-start(f32[8,256]{1,0:T(8,128)S(1)} %get-tuple-element.23), channel_id=1, source_target_pairs={{0,64},{64,16},{16,80},{80,0},{1,65},{65,17},{17,81},{81,1},{2,66}... | collective-permute-start | bytes 24584 | tf_op jit(solution)/shard_map/ppermute | solution.py:318
  118.6 3.6 %collective-permute-start.6 = (f32[8,256]{1,0:T(8,128)S(1)}, f32[8,256]{1,0:T(8,128)S(1)}, u32[]{:S(2)}, u32[]{:S(2)}) collective-permute-start(f32[8,256]{1,0:T(8,128)S(1)} %get-tuple-element.24), channel_id=1, source_target_pairs={{0,16},{64,80},{16,0},{80,64},{1,17},{65,81},{17,1},{81,65},{2,18}... | collective-permute-start | bytes 24584 | tf_op jit(solution)/shard_map/ppermute | solution.py:318
  122.2 1.0 collective-permute-start.7
  123.2 0.0 all-to-all-done.1.got
  123.2 0.0 collective-permute-done.5.refs_1_
  123.2 0.7 collective-permute-done.6.refs_2_
  123.9 1.9 %collective-permute-done.7.refs_3_ = f32[8,256]{1,0:T(8,128)S(1)} collective-permute-done((f32[8,256]{1,0:T(8,128)S(1)}, f32[8,256]{1,0:T(8,128)S(1)}, u32[]{:S(2)}, u32[]{:S(2)}) %collective-permute-start.7) | collective-permute-done | bytes 8224 | tf_op jit(solution)/shard_map/ppermute | solution.py:318
  125.8 0.6 shard_map.81
  (2 shorter events, 0.0 us)
Async XLA Ops:
  2.6 23.3 %all-to-all-start = ((f32[16,136,128]{2,1,0:T(8,128)}), f32[16,136,128]{2,1,0:T(8,128)S(1)}, u32[]{:S(2)}, u32[]{:S(2)}) async-start(f32[16,136,128]{2,1,0:T(8,128)} %get-tuple-element.15), calls=%async_computation | async-start | bytes 2228224 | tf_op jit(solution)/shard_map/all_to_all | solution.py:290
  10.1 7.1 %collective-permute-start.2 = (f32[136,128]{1,0:T(8,128)S(1)}, f32[136,128]{1,0:T(8,128)S(1)}, u32[]{:S(2)}, u32[]{:S(2)}) collective-permute-start(f32[136,128]{1,0:T(8,128)S(1)} %get-tuple-element.14.refs_0_), channel_id=1, source_target_pairs={{0,64},{64,16},{16,80},{80,0},{1,65},{65,17},{17,81},{81,1},{2,66}... | collective-permute-start | bytes 208904 | tf_op jit(solution)/shard_map/ppermute | solution.py:288
  12.1 6.6 %collective-permute-start.1 = (f32[136,128]{1,0:T(8,128)S(1)}, f32[136,128]{1,0:T(8,128)S(1)}, u32[]{:S(2)}, u32[]{:S(2)}) collective-permute-start(f32[136,128]{1,0:T(8,128)S(1)} %get-tuple-element.14.refs_0_), channel_id=1, source_target_pairs={{0,16},{64,80},{16,0},{80,64},{1,17},{65,81},{17,1},{81,65},{2,18}... | collective-permute-start | bytes 208904 | tf_op jit(solution)/shard_map/ppermute | solution.py:288
  15.6 4.3 %collective-permute-start = (f32[136,128]{1,0:T(8,128)S(1)}, f32[136,128]{1,0:T(8,128)S(1)}, u32[]{:S(2)}, u32[]{:S(2)}) collective-permute-start(f32[136,128]{1,0:T(8,128)S(1)} %get-tuple-element.14.refs_0_), channel_id=1, source_target_pairs={{0,80},{64,0},{16,64},{80,16},{1,81},{65,1},{17,65},{81,17},{2,82}... | collective-permute-start | bytes 208904 | tf_op jit(solution)/shard_map/ppermute | solution.py:288
  20.0 1.6 %collective-permute-start.3 = (f32[4,136,128]{2,1,0:T(8,128)S(1)}, f32[4,136,128]{2,1,0:T(8,128)S(1)}, u32[]{:S(2)}, u32[]{:S(2)}) collective-permute-start(f32[4,136,128]{2,1,0:T(8,128)S(1)} %pad_maximum_fusion), channel_id=1, source_target_pairs={{0,32},{32,0},{1,33},{33,1},{2,34},{34,2},{3,35},{35,3},{4,36},{36... | collective-permute-start | bytes 835592 | tf_op jit(solution)/shard_map/ppermute | solution.py:289
  110.5 6.1 %collective-permute-start.4 = (f32[8,256]{1,0:T(8,128)S(1)}, f32[8,256]{1,0:T(8,128)S(1)}, u32[]{:S(2)}, u32[]{:S(2)}) collective-permute-start(f32[8,256]{1,0:T(8,128)S(1)} %get-tuple-element.21), channel_id=1, source_target_pairs={{0,32},{32,0},{1,33},{33,1},{2,34},{34,2},{3,35},{35,3},{4,36},{36... | collective-permute-start | bytes 24584 | tf_op jit(solution)/shard_map/ppermute | solution.py:313
  110.5 12.7 %all-to-all-start.1 = ((f32[16,1,256]{2,1,0:T(1,128)}), f32[16,1,256]{2,1,0:T(1,128)S(1)}, u32[]{:S(2)}, u32[]{:S(2)}) async-start(f32[16,1,256]{2,1,0:T(1,128)} %get-tuple-element.18), calls=%async_computation.1 | async-start | bytes 32768 | tf_op jit(solution)/shard_map/all_to_all | solution.py:314
  116.6 6.6 %collective-permute-start.5 = (f32[8,256]{1,0:T(8,128)S(1)}, f32[8,256]{1,0:T(8,128)S(1)}, u32[]{:S(2)}, u32[]{:S(2)}) collective-permute-start(f32[8,256]{1,0:T(8,128)S(1)} %get-tuple-element.23), channel_id=1, source_target_pairs={{0,64},{64,16},{16,80},{80,0},{1,65},{65,17},{17,81},{81,1},{2,66}... | collective-permute-start | bytes 24584 | tf_op jit(solution)/shard_map/ppermute | solution.py:318
  118.6 5.3 %collective-permute-start.6 = (f32[8,256]{1,0:T(8,128)S(1)}, f32[8,256]{1,0:T(8,128)S(1)}, u32[]{:S(2)}, u32[]{:S(2)}) collective-permute-start(f32[8,256]{1,0:T(8,128)S(1)} %get-tuple-element.24), channel_id=1, source_target_pairs={{0,16},{64,80},{16,0},{80,64},{1,17},{65,81},{17,1},{81,65},{2,18}... | collective-permute-start | bytes 24584 | tf_op jit(solution)/shard_map/ppermute | solution.py:318
  122.2 3.7 %collective-permute-start.7 = (f32[8,256]{1,0:T(8,128)S(1)}, f32[8,256]{1,0:T(8,128)S(1)}, u32[]{:S(2)}, u32[]{:S(2)}) collective-permute-start(f32[8,256]{1,0:T(8,128)S(1)} %get-tuple-element.25), channel_id=1, source_target_pairs={{0,80},{64,0},{16,64},{80,16},{1,81},{65,1},{17,65},{81,17},{2,82}... | collective-permute-start | bytes 24584 | tf_op jit(solution)/shard_map/ppermute | solution.py:318

commit v13 on v12

--- a/solution.py
+++ b/solution.py
@@ -314,7 +314,7 @@
     got = lax.all_to_all(out, PLANE, 0, 0, tiled=True)
     small = pl.CostEstimate(flops=10**5, bytes_accessed=10**5, transcendentals=0)
     parts = list(call(merge_kernel, (f32(SENT, BLK),) * SIDE, 2, cost=small)(lines, crossed))
-    for k in (2, 1, 3):
+    for k in (1, 3, 2):
         parts[k] = lax.ppermute(parts[k], LINE, along(k))
     return call(finish_kernel, (f32(BLK), f32(BLK)), 2 + SIDE)(got, own, *parts)
 

time: 127 us -> 127 us (level)
  no operation moved by 1% of the time
where the time goes in v13:
time: 127 us; the launch traced here: 126 us
  Pallas kernels  87.6 us (69%)
  starting transfers between devices  26.8 us (21%)
  waiting for transfers between devices  11.4 us (9%)
    pallas_call x1, Pallas kernels, local(): call(functools.partial(tile_kernel, nrow, ncol), (f32(LINES, BLK), f32(LI...  84.5 us
    all_to_all x1, starting transfers between devices, local(): cols = lax.all_to_all(copies, PLANE, 0, 0, tiled=True)  7.49 us
    ppermute x3, starting transfers between devices, local(): parts[k] = lax.ppermute(parts[k], LINE, along(k))  6.58 us
    ppermute x3, starting transfers between devices, local(): mine.append(lax.ppermute(rows, LINE, along(-k)))  6.51 us
    all_to_all x1, starting transfers between devices, local(): got = lax.all_to_all(out, PLANE, 0, 0, tiled=True)  6.13 us
    all_to_all x1, waiting for transfers between devices, local(): cols = lax.all_to_all(copies, PLANE, 0, 0, tiled=True)  3.9 us
    ppermute x3, waiting for transfers between devices, local(): mine.append(lax.ppermute(rows, LINE, along(-k)))  3.3 us
    ppermute x3, waiting for transfers between devices, local(): parts[k] = lax.ppermute(parts[k], LINE, along(k))  2.63 us
  transfers between devices with their start and end apart: 10, of which 7 were waited for; matrix products, arithmetic and copies ran while one was open for 0% of the time, Pallas kernels for 0%

profile of v13, /device:TPU:2, one launch (start us, length us, event | category | flops | bytes accessed | tf_op | source)
XLA Modules:
  0.0 126.5 jit_solution(4480136132091429339)
XLA Ops:
  0.6 2.0 %shard_map.77 = (f32[136,128]{1,0:T(8,128)S(1)}, f32[16,136,128]{2,1,0:T(8,128)}) custom-call(f32[64,256]{1,0:T(8,128)} %spts.1, f32[64,256]{1,0:T(8,128)} %tpts.1, f32[2,128]{1,0:T(2,128)} %bitcast.12, f32[2,128]{1,0:T(2,128)} %bitcast.13, f32[2,128]{1,0:T(2,128)} %bitcast.14, f32[2,128]{1,0:T(2,128)} %bitcast.15), custom_call_target="tpu_custom_call" | custom-call | tf_op jit(solution)/shard_map/pallas_call | solution.py:274
  2.6 7.5 %all-to-all-start = ((f32[16,136,128]{2,1,0:T(8,128)}), f32[16,136,128]{2,1,0:T(8,128)S(1)}, u32[]{:S(2)}, u32[]{:S(2)}) async-start(f32[16,136,128]{2,1,0:T(8,128)} %get-tuple-element.15), calls=%async_computation | async-start | bytes 2228224 | tf_op jit(solution)/shard_map/all_to_all | solution.py:290
  10.1 1.9 %collective-permute-start.2 = (f32[136,128]{1,0:T(8,128)S(1)}, f32[136,128]{1,0:T(8,128)S(1)}, u32[]{:S(2)}, u32[]{:S(2)}) collective-permute-start(f32[136,128]{1,0:T(8,128)S(1)} %get-tuple-element.14.refs_0_), channel_id=1, source_target_pairs={{0,64},{64,16},{16,80},{80,0},{1,65},{65,17},{17,81},{81,1},{2,66}... | collective-permute-start | bytes 208904 | tf_op jit(solution)/shard_map/ppermute | solution.py:288
  12.1 3.6 %collective-permute-start.1 = (f32[136,128]{1,0:T(8,128)S(1)}, f32[136,128]{1,0:T(8,128)S(1)}, u32[]{:S(2)}, u32[]{:S(2)}) collective-permute-start(f32[136,128]{1,0:T(8,128)S(1)} %get-tuple-element.14.refs_0_), channel_id=1, source_target_pairs={{0,16},{64,80},{16,0},{80,64},{1,17},{65,81},{17,1},{81,65},{2,18}... | collective-permute-start | bytes 208904 | tf_op jit(solution)/shard_map/ppermute | solution.py:288
  15.6 1.0 collective-permute-start
  16.6 0.6 collective-permute-done.2.refs_3_
  17.2 1.5 %collective-permute-done.1.refs_2_ = f32[136,128]{1,0:T(8,128)S(1)} collective-permute-done((f32[136,128]{1,0:T(8,128)S(1)}, f32[136,128]{1,0:T(8,128)S(1)}, u32[]{:S(2)}, u32[]{:S(2)}) %collective-permute-start.1) | collective-permute-done | bytes 69664 | tf_op jit(solution)/shard_map/ppermute | solution.py:288
  18.7 1.3 %collective-permute-done.refs_1_ = f32[136,128]{1,0:T(8,128)S(1)} collective-permute-done((f32[136,128]{1,0:T(8,128)S(1)}, f32[136,128]{1,0:T(8,128)S(1)}, u32[]{:S(2)}, u32[]{:S(2)}) %collective-permute-start) | collective-permute-done | bytes 69664 | tf_op jit(solution)/shard_map/ppermute | solution.py:288
  20.0 0.1 collective-permute-start.3
  20.1 1.5 %collective-permute-done.3.refs_4_ = f32[4,136,128]{2,1,0:T(8,128)S(1)} collective-permute-done((f32[4,136,128]{2,1,0:T(8,128)S(1)}, f32[4,136,128]{2,1,0:T(8,128)S(1)}, u32[]{:S(2)}, u32[]{:S(2)}) %collective-permute-start.3) | collective-permute-done | bytes 278560 | tf_op jit(solution)/shard_map/ppermute | solution.py:289
  21.6 0.4 shard_map.78
  22.0 3.9 %all-to-all-done.refs_5_ = f32[16,136,128]{2,1,0:T(8,128)S(1)} async-done(((f32[16,136,128]{2,1,0:T(8,128)}), f32[16,136,128]{2,1,0:T(8,128)S(1)}, u32[]{:S(2)}, u32[]{:S(2)}) %all-to-all-start) | async-done | bytes 1114144 | tf_op jit(solution)/shard_map/all_to_all | solution.py:290
  25.9 84.5 %shard_map.79 = (f32[8,256]{1,0:T(8,128)S(1)}, f32[8,256]{1,0:T(8,128)S(1)}, f32[16,1,256]{2,1,0:T(1,128)}, f32[8,256]{1,0:T(8,128)S(1)}) custom-call(f32[136,128]{1,0:T(8,128)S(1)} %get-tuple-element.14.refs_0_, f32[136,128]{1,0:T(8,128)S(1)} %collective-permute-done.refs_1_, f32[136,128]{1,0:T(8,128)S(1)} %collective-permute-done.1.refs_2_, ...), custom_call_target="tpu_custom_call" | custom-call | flops 4294967296 | bytes 4194304 | tf_op jit(solution)/shard_map/pallas_call | solution.py:306
  110.5 0.0 collective-permute-start.4
  110.5 6.1 %all-to-all-start.1 = ((f32[16,1,256]{2,1,0:T(1,128)}), f32[16,1,256]{2,1,0:T(1,128)S(1)}, u32[]{:S(2)}, u32[]{:S(2)}) async-start(f32[16,1,256]{2,1,0:T(1,128)} %get-tuple-element.18), calls=%async_computation.1 | async-start | bytes 32768 | tf_op jit(solution)/shard_map/all_to_all | solution.py:314
  116.6 0.0 collective-permute-done.4.other
  116.6 2.0 %collective-permute-start.5 = (f32[8,256]{1,0:T(8,128)S(1)}, f32[8,256]{1,0:T(8,128)S(1)}, u32[]{:S(2)}, u32[]{:S(2)}) collective-permute-start(f32[8,256]{1,0:T(8,128)S(1)} %get-tuple-element.23), channel_id=1, source_target_pairs={{0,64},{64,16},{16,80},{80,0},{1,65},{65,17},{17,81},{81,1},{2,66}... | collective-permute-start | bytes 24584 | tf_op jit(solution)/shard_map/ppermute | solution.py:318
  118.6 3.6 %collective-permute-start.6 = (f32[8,256]{1,0:T(8,128)S(1)}, f32[8,256]{1,0:T(8,128)S(1)}, u32[]{:S(2)}, u32[]{:S(2)}) collective-permute-start(f32[8,256]{1,0:T(8,128)S(1)} %get-tuple-element.24), channel_id=1, source_target_pairs={{0,16},{64,80},{16,0},{80,64},{1,17},{65,81},{17,1},{81,65},{2,18}... | collective-permute-start | bytes 24584 | tf_op jit(solution)/shard_map/ppermute | solution.py:318
  122.2 1.0 collective-permute-start.7
  123.2 0.0 all-to-all-done.1.got
  123.2 0.0 collective-permute-done.5.refs_1_
  123.2 0.7 collective-permute-done.6.refs_2_
  123.9 1.9 %collective-permute-done.7.refs_3_ = f32[8,256]{1,0:T(8,128)S(1)} collective-permute-done((f32[8,256]{1,0:T(8,128)S(1)}, f32[8,256]{1,0:T(8,128)S(1)}, u32[]{:S(2)}, u32[]{:S(2)}) %collective-permute-start.7) | collective-permute-done | bytes 8224 | tf_op jit(solution)/shard_map/ppermute | solution.py:318
  125.8 0.6 shard_map.81
  (2 shorter events, 0.0 us)
Async XLA Ops:
  2.6 23.3 %all-to-all-start = ((f32[16,136,128]{2,1,0:T(8,128)}), f32[16,136,128]{2,1,0:T(8,128)S(1)}, u32[]{:S(2)}, u32[]{:S(2)}) async-start(f32[16,136,128]{2,1,0:T(8,128)} %get-tuple-element.15), calls=%async_computation | async-start | bytes 2228224 | tf_op jit(solution)/shard_map/all_to_all | solution.py:290
  10.1 7.1 %collective-permute-start.2 = (f32[136,128]{1,0:T(8,128)S(1)}, f32[136,128]{1,0:T(8,128)S(1)}, u32[]{:S(2)}, u32[]{:S(2)}) collective-permute-start(f32[136,128]{1,0:T(8,128)S(1)} %get-tuple-element.14.refs_0_), channel_id=1, source_target_pairs={{0,64},{64,16},{16,80},{80,0},{1,65},{65,17},{17,81},{81,1},{2,66}... | collective-permute-start | bytes 208904 | tf_op jit(solution)/shard_map/ppermute | solution.py:288
  12.1 6.6 %collective-permute-start.1 = (f32[136,128]{1,0:T(8,128)S(1)}, f32[136,128]{1,0:T(8,128)S(1)}, u32[]{:S(2)}, u32[]{:S(2)}) collective-permute-start(f32[136,128]{1,0:T(8,128)S(1)} %get-tuple-element.14.refs_0_), channel_id=1, source_target_pairs={{0,16},{64,80},{16,0},{80,64},{1,17},{65,81},{17,1},{81,65},{2,18}... | collective-permute-start | bytes 208904 | tf_op jit(solution)/shard_map/ppermute | solution.py:288
  15.6 4.3 %collective-permute-start = (f32[136,128]{1,0:T(8,128)S(1)}, f32[136,128]{1,0:T(8,128)S(1)}, u32[]{:S(2)}, u32[]{:S(2)}) collective-permute-start(f32[136,128]{1,0:T(8,128)S(1)} %get-tuple-element.14.refs_0_), channel_id=1, source_target_pairs={{0,80},{64,0},{16,64},{80,16},{1,81},{65,1},{17,65},{81,17},{2,82}... | collective-permute-start | bytes 208904 | tf_op jit(solution)/shard_map/ppermute | solution.py:288
  20.0 1.6 %collective-permute-start.3 = (f32[4,136,128]{2,1,0:T(8,128)S(1)}, f32[4,136,128]{2,1,0:T(8,128)S(1)}, u32[]{:S(2)}, u32[]{:S(2)}) collective-permute-start(f32[4,136,128]{2,1,0:T(8,128)S(1)} %pad_maximum_fusion), channel_id=1, source_target_pairs={{0,32},{32,0},{1,33},{33,1},{2,34},{34,2},{3,35},{35,3},{4,36},{36... | collective-permute-start | bytes 835592 | tf_op jit(solution)/shard_map/ppermute | solution.py:289
  110.5 6.1 %collective-permute-start.4 = (f32[8,256]{1,0:T(8,128)S(1)}, f32[8,256]{1,0:T(8,128)S(1)}, u32[]{:S(2)}, u32[]{:S(2)}) collective-permute-start(f32[8,256]{1,0:T(8,128)S(1)} %get-tuple-element.21), channel_id=1, source_target_pairs={{0,32},{32,0},{1,33},{33,1},{2,34},{34,2},{3,35},{35,3},{4,36},{36... | collective-permute-start | bytes 24584 | tf_op jit(solution)/shard_map/ppermute | solution.py:313
  110.5 12.7 %all-to-all-start.1 = ((f32[16,1,256]{2,1,0:T(1,128)}), f32[16,1,256]{2,1,0:T(1,128)S(1)}, u32[]{:S(2)}, u32[]{:S(2)}) async-start(f32[16,1,256]{2,1,0:T(1,128)} %get-tuple-element.18), calls=%async_computation.1 | async-start | bytes 32768 | tf_op jit(solution)/shard_map/all_to_all | solution.py:314
  116.6 6.6 %collective-permute-start.5 = (f32[8,256]{1,0:T(8,128)S(1)}, f32[8,256]{1,0:T(8,128)S(1)}, u32[]{:S(2)}, u32[]{:S(2)}) collective-permute-start(f32[8,256]{1,0:T(8,128)S(1)} %get-tuple-element.23), channel_id=1, source_target_pairs={{0,64},{64,16},{16,80},{80,0},{1,65},{65,17},{17,81},{81,1},{2,66}... | collective-permute-start | bytes 24584 | tf_op jit(solution)/shard_map/ppermute | solution.py:318
  118.6 5.3 %collective-permute-start.6 = (f32[8,256]{1,0:T(8,128)S(1)}, f32[8,256]{1,0:T(8,128)S(1)}, u32[]{:S(2)}, u32[]{:S(2)}) collective-permute-start(f32[8,256]{1,0:T(8,128)S(1)} %get-tuple-element.24), channel_id=1, source_target_pairs={{0,16},{64,80},{16,0},{80,64},{1,17},{65,81},{17,1},{81,65},{2,18}... | collective-permute-start | bytes 24584 | tf_op jit(solution)/shard_map/ppermute | solution.py:318
  122.2 3.7 %collective-permute-start.7 = (f32[8,256]{1,0:T(8,128)S(1)}, f32[8,256]{1,0:T(8,128)S(1)}, u32[]{:S(2)}, u32[]{:S(2)}) collective-permute-start(f32[8,256]{1,0:T(8,128)S(1)} %get-tuple-element.25), channel_id=1, source_target_pairs={{0,80},{64,0},{16,64},{80,16},{1,81},{65,1},{17,65},{81,17},{2,82}... | collective-permute-start | bytes 24584 | tf_op jit(solution)/shard_map/ppermute | solution.py:318
